TPU v7x, 32 devices: a whole 2x2x4 slice. The times are simulated.
32 devices in a mesh: dp: 8 (over y, x, core), tensor: 4 (over z).
Axes of the slice: x: 2, y: 2, z: 4, core: 2. Of those that a mesh axis runs over, the one named last changes fastest.
Arguments:
- inputs: bfloat16 [6144, 2048], P('dp'), may hold values from -6 to 6
- block_ids: int32 [8, 768], P('dp'), may hold values from 0 to 3, never falling along the last dimension, each value on 1 to 256 neighbouring positions
- first_gain: float32 [2048], replicated, may hold values from 0.5 to 1.5
- first_shift: float32 [2048], replicated, may hold values from -3 to 3
- mixing_weight: bfloat16 [2048, 3, 2048], P(None, None, 'tensor'), may hold values from -0.125 to 0.125
- mixing_bias: float32 [2, 2048], P(None, 'tensor'), may hold values from -3 to 3
- output_weight: bfloat16 [2048, 2048], P('tensor'), may hold values from -0.75 to 0.75
- output_bias: float32 [2048], replicated, may hold values from -3 to 3
- second_gain: float32 [2048], replicated, may hold values from 0.5 to 1.5
- second_shift: float32 [2048], replicated, may hold values from -3 to 3
- expand_weight: bfloat16 [2048, 8192], P(None, 'tensor'), may hold values from -0.125 to 0.125
- expand_bias: float32 [8192], P('tensor'), may hold values from -3 to 3
- shrink_weight: bfloat16 [8192, 2048], P('tensor'), may hold values from -0.0625 to 0.0625
- shrink_bias: float32 [2048], replicated, may hold values from -3 to 3
- cotangent: bfloat16 [6144, 2048], P('dp'), may hold values from -6 to 6
Outputs:
- outputs: bfloat16 [6144, 2048], P('dp')
- input_grad: bfloat16 [6144, 2048], P('dp')
- first_gain_grad: float32 [2048], replicated
- first_shift_grad: float32 [2048], replicated
- mixing_weight_grad: float32 [2048, 3, 2048], P(None, None, 'tensor')
- mixing_bias_grad: float32 [2, 2048], P(None, 'tensor')
- output_weight_grad: float32 [2048, 2048], P('tensor')
- output_bias_grad: float32 [2048], replicated
- second_gain_grad: float32 [2048], replicated
- second_shift_grad: float32 [2048], replicated
- expand_weight_grad: float32 [2048, 8192], P(None, 'tensor')
- expand_bias_grad: float32 [8192], P('tensor')
- shrink_weight_grad: float32 [8192, 2048], P('tensor')
- shrink_bias_grad: float32 [2048], replicated
Inputs may be any that keep to these rules, and one draw needn't show every extreme that they name: `block_ids`: each sequence's block numbers start at 0, never fall, rise by one from block to block, give 4 blocks of 1 to 256 tokens, and one block has exactly 256 tokens.
All inputs are finite; a program needn't handle non-finite values.
Results may differ from a plain program's by a relative error of at most 0.014.
Values may be sent and summed in bfloat16 or wider, within the bound.
A program may use at most 256 MiB of HBM per device.

v0:
```python
import math

import jax
import jax.numpy as jnp
from jax import lax
from jax.sharding import PartitionSpec as P

H = 32
HD = 64


EPS = 1e-05


def layer_norm(values, scale_gain, shift_bias):
    row_mean = jnp.mean(values, axis=-1, keepdims=True)
    centred = values - row_mean
    row_var = jnp.mean(centred * centred, axis=-1, keepdims=True)
    return centred * lax.rsqrt(row_var + EPS) * scale_gain + shift_bias


def norm_backward(values, scale_gain, shift_bias, upstream):
    _, pull_back = jax.vjp(layer_norm, values, scale_gain, shift_bias)
    return pull_back(upstream)


def gelu_exact(values):
    return jax.nn.gelu(values, approximate=False)


def biased_scores(query, keys, blocks, first_head):
    length, local_heads, head_width = query.shape
    scores = jnp.einsum("qhd,khd->hqk", query, keys, preferred_element_type=jnp.float32) * (
        1.0 / math.sqrt(head_width)
    )
    heads_index = (first_head + jnp.arange(local_heads)).astype(jnp.float32)
    slopes = 2.0 ** (-8.0 * (heads_index + 1.0) / H)
    places = jnp.arange(length)
    offsets = (places[None, :] - places[:, None]).astype(jnp.float32)
    scores = scores + slopes[:, None, None] * offsets[None]
    allowed = blocks[None, :] <= blocks[:, None]
    return jnp.where(allowed[None], scores, -1e30)


def on_device(
    inputs,
    block_ids,
    first_gain,
    first_shift,
    mixing_weight,
    mixing_bias,
    output_weight,
    output_bias,
    second_gain,
    second_shift,
    expand_weight,
    expand_bias,
    shrink_weight,
    shrink_bias,
    cotangent,
):
    source = inputs.astype(jnp.float32)
    upstream = cotangent.astype(jnp.float32)
    length, width = source.shape
    blocks = block_ids[0]
    local_width = mixing_weight.shape[2]
    local_heads = local_width // HD
    first_head = lax.axis_index("tensor") * local_heads
    normed_low = layer_norm(source, first_gain, first_shift).astype(jnp.bfloat16)
    flat_weight = mixing_weight.reshape(width, 3 * local_width)
    mixed = jnp.dot(normed_low, flat_weight, preferred_element_type=jnp.float32).reshape(
        length, 3, local_width
    )
    query = (mixed[:, 0] + mixing_bias[0]).astype(jnp.bfloat16).reshape(length, local_heads, HD)
    keys = mixed[:, 1].astype(jnp.bfloat16).reshape(length, local_heads, HD)
    vals = (mixed[:, 2] + mixing_bias[1]).astype(jnp.bfloat16).reshape(length, local_heads, HD)
    masked = biased_scores(query, keys, blocks, first_head)
    row_top = jnp.max(masked, axis=-1, keepdims=True)
    logsum = row_top + jnp.log(jnp.sum(jnp.exp(masked - row_top), axis=-1, keepdims=True))
    probs_low = jnp.exp(masked - logsum).astype(jnp.bfloat16)
    attended = (
        jnp.einsum("hqk,khd->qhd", probs_low, vals, preferred_element_type=jnp.float32)
        .reshape(length, local_width)
        .astype(jnp.bfloat16)
    )
    partial_out = jnp.dot(attended, output_weight, preferred_element_type=jnp.float32)
    resid = lax.psum(partial_out, "tensor") + output_bias
    hidden_state = source + resid
    second_low = layer_norm(hidden_state, second_gain, second_shift).astype(jnp.bfloat16)
    pre_act = jnp.dot(second_low, expand_weight, preferred_element_type=jnp.float32) + expand_bias
    activ_low = gelu_exact(pre_act).astype(jnp.bfloat16)
    partial_mlp = jnp.dot(activ_low, shrink_weight, preferred_element_type=jnp.float32)
    outputs = (
        hidden_state
        + lax.psum(partial_mlp.astype(jnp.bfloat16), "tensor").astype(jnp.float32)
        + shrink_bias
    ).astype(jnp.bfloat16)
    act_grad = jnp.einsum("td,fd->tf", cotangent, shrink_weight, preferred_element_type=jnp.float32)
    _, gelu_pull = jax.vjp(gelu_exact, pre_act)
    pre_grad = gelu_pull(act_grad)[0].astype(jnp.bfloat16)
    shrink_weight_grad = jnp.einsum(
        "tf,td->fd", activ_low, cotangent, preferred_element_type=jnp.float32
    )
    shrink_bias_grad = jnp.sum(upstream, axis=0)
    expand_weight_grad = jnp.einsum(
        "td,tf->df", second_low, pre_grad, preferred_element_type=jnp.float32
    )
    expand_bias_grad = jnp.sum(pre_grad.astype(jnp.float32), axis=0)
    second_part = jnp.einsum(
        "tf,df->td", pre_grad, expand_weight, preferred_element_type=jnp.float32
    )
    second_grad = lax.psum(second_part, "tensor")
    hidden_grad, second_gain_grad, second_shift_grad = norm_backward(
        hidden_state, second_gain, second_shift, second_grad
    )
    hidden_grad = hidden_grad + upstream
    resid_low = hidden_grad.astype(jnp.bfloat16)
    output_weight_grad = jnp.einsum(
        "tc,td->cd", attended, resid_low, preferred_element_type=jnp.float32
    )
    output_bias_grad = jnp.sum(resid_low.astype(jnp.float32), axis=0)
    attended_grad = (
        jnp.einsum("td,cd->tc", resid_low, output_weight, preferred_element_type=jnp.float32)
        .astype(jnp.bfloat16)
        .reshape(length, local_heads, HD)
    )
    probs = jnp.exp(biased_scores(query, keys, blocks, first_head) - logsum)
    probs_low = probs.astype(jnp.bfloat16)
    prob_grad = jnp.einsum("qhd,khd->hqk", attended_grad, vals, preferred_element_type=jnp.float32)
    vals_grad = jnp.einsum(
        "hqk,qhd->khd", probs_low, attended_grad, preferred_element_type=jnp.float32
    ).astype(jnp.bfloat16)
    row_delta = jnp.sum(probs * prob_grad, axis=-1, keepdims=True)
    score_grad = (probs * (prob_grad - row_delta)).astype(jnp.bfloat16)
    scale_factor = 1.0 / math.sqrt(HD)
    query_grad = (
        jnp.einsum("hqk,khd->qhd", score_grad, keys, preferred_element_type=jnp.float32)
        * scale_factor
    ).astype(jnp.bfloat16)
    keys_grad = (
        jnp.einsum("hqk,qhd->khd", score_grad, query, preferred_element_type=jnp.float32)
        * scale_factor
    ).astype(jnp.bfloat16)
    mixed_grad = jnp.stack([query_grad, keys_grad, vals_grad], axis=1).reshape(
        length, 3 * local_width
    )
    mixing_weight_grad = jnp.einsum(
        "td,tc->dc", normed_low, mixed_grad, preferred_element_type=jnp.float32
    ).reshape(width, 3, local_width)
    mixing_bias_grad = jnp.stack(
        [
            jnp.sum(query_grad.astype(jnp.float32), axis=0).reshape(local_width),
            jnp.sum(vals_grad.astype(jnp.float32), axis=0).reshape(local_width),
        ]
    )
    normed_part = jnp.einsum(
        "tc,dc->td", mixed_grad, flat_weight, preferred_element_type=jnp.float32
    )
    normed_grad = lax.psum(normed_part, "tensor")
    source_grad, first_gain_grad, first_shift_grad = norm_backward(
        source, first_gain, first_shift, normed_grad
    )
    input_grad = (source_grad + hidden_grad).astype(jnp.bfloat16)
    summed = lax.psum(
        (
            first_gain_grad,
            first_shift_grad,
            mixing_weight_grad,
            mixing_bias_grad,
            output_weight_grad,
            output_bias_grad,
            second_gain_grad,
            second_shift_grad,
            expand_weight_grad,
            expand_bias_grad,
            shrink_weight_grad,
            shrink_bias_grad,
        ),
        "dp",
    )
    return (
        outputs,
        input_grad,
        summed[0],
        summed[1],
        summed[2],
        summed[3],
        summed[4],
        summed[5],
        summed[6],
        summed[7],
        summed[8],
        summed[9],
        summed[10],
        summed[11],
    )


def solution(mesh):
    in_specs = (
        P("dp", None),
        P("dp", None),
        P(),
        P(),
        P(None, None, "tensor"),
        P(None, "tensor"),
        P("tensor", None),
        P(),
        P(),
        P(),
        P(None, "tensor"),
        P("tensor"),
        P("tensor", None),
        P(),
        P("dp", None),
    )
    out_specs = (
        P("dp", None),
        P("dp", None),
        P(),
        P(),
        P(None, None, "tensor"),
        P(None, "tensor"),
        P("tensor", None),
        P(),
        P(),
        P(),
        P(None, "tensor"),
        P("tensor"),
        P("tensor", None),
        P(),
    )
    return jax.shard_map(
        on_device, mesh=mesh, in_specs=in_specs, out_specs=out_specs, check_vma=False
    )
```

profile of v0, /device:TPU:0, one launch (start us, length us, event | category | flops | bytes accessed | tf_op | source)
XLA Modules:
  0.0 1608.9 jit_solution(12495282931637150068)
XLA Ops:
  7.3 1.6 subtract_convert_fusion
  8.9 2.6 convert_reduce_fusion
  11.6 1.0 fusion.10
  13.2 8.8 copy.34
  22.0 8.5 fusion.13
  30.6 1.9 fusion.47
  33.1 11.5 fusion.48
  44.6 8.9 exponential_reduce_fusion
  53.5 9.8 fusion.26
  64.2 4.5 fusion.49
  68.8 225.7 %all-reduce.8.cloned.1.call-done = f32[768,2048]{1,0:T(8,128)} async-done(((f32[768,2048]{1,0:T(8,128)}), f32[768,2048]{1,0:T(8,128)}) %all-reduce.8.cloned.1.call-update) | async-done | bytes 6291472 | tf_op jit(solution)/shard_map/psum | solution.py:87
  294.5 4.6 fusion.46
  299.9 11.6 fusion.41
  311.5 26.1 %convert_reduce_fusion.2 = (f32[2048]{0:T(1024)}, bf16[768,2048]{1,0:T(8,128)(2,1)S(1)}, f32[768,2048]{1,0:T(8,128)}) fusion(f32[768,2048]{1,0:T(8,128)S(1)} %fusion.41, f32[2048]{0:T(1024)S(1)} %copy-done.37, bf16[768,2048]{1,0:T(8,128)(2,1)S(1)} %copy-done.9, bf16[2048,2048]{1,0:T(8,128)(2,1)} %param.27), kind=kOutput, calls=%fused_computation.28 | convolution fusion | flops 6560413696 | bytes 27279360 | tf_op jit(solution)/shard_map/td,fd->tf/dot_general | solution.py:98
  337.7 1.7 copy-done.47
  339.3 10.9 fusion.50
  350.5 6.6 multiply_convert_fusion.1
  357.1 1.7 copy-done.19
  358.8 10.2 convolution_convert_fusion
  369.1 203.1 %all-reduce.12.cloned.1.call-done = f32[768,2048]{1,0:T(8,128)} async-done(((f32[768,2048]{1,0:T(8,128)}), f32[768,2048]{1,0:T(8,128)}) %all-reduce.12.cloned.1.call-update) | async-done | bytes 6291472 | tf_op jit(solution)/shard_map/psum | solution.py:112
  572.2 5.8 multiply_reduce_fusion.1
  578.0 117.2 %all-reduce.10.cloned.1.call-done = bf16[768,2048]{1,0:T(8,128)(2,1)} async-done(((bf16[768,2048]{1,0:T(8,128)(2,1)}), bf16[768,2048]{1,0:T(8,128)(2,1)}) %all-reduce.10.cloned.1.call-update) | async-done | bytes 3145744 | tf_op jit(solution)/shard_map/psum | solution.py:95
  695.2 8.1 fusion.45
  703.3 1.0 convert_reduce_fusion.3
  704.3 1.6 copy-done.6
  705.9 1.8 convolution_convert_fusion.1
  707.8 9.6 convert_reduce_fusion.4
  717.4 11.9 multiply_reduce_fusion
  729.3 13.7 multiply_convert_fusion
  743.0 3.0 fusion.32
  746.0 1.8 convert_reduce_fusion.5
  748.1 1.4 copy-done.22
  749.5 7.1 fusion.51
  756.8 12.9 fusion.53
  769.7 14.0 fusion.40
  783.7 3.8 fusion.52
  787.6 9.8 fusion.33
  797.6 181.1 %all-reduce.14.cloned.1.call-done = f32[768,2048]{1,0:T(8,128)} async-done(((f32[768,2048]{1,0:T(8,128)}), f32[768,2048]{1,0:T(8,128)}) %all-reduce.14.cloned.1.call-update) | async-done | bytes 6291472 | tf_op jit(solution)/shard_map/psum | solution.py:159
  978.7 4.8 fusion.42
  984.2 4.6 fusion.9
  988.9 6.6 convert_reduce_fusion.1
  995.5 27.8 %all-reduce = (f32[2048]{0:T(1024)}, f32[2048]{0:T(1024)}, f32[2,512]{1,0:T(2,128)}, f32[2048]{0:T(1024)}, f32[2048]{0:T(1024)}, /*index=5*/f32[2048]{0:T(1024)}, f32[2048]{0:T(1024)}, f32[2048]{0:T(1024)}) all-reduce(f32[2048]{0:T(1024)S(1)} %get-tuple-element.16, ...), channel_id=1, replica_groups=mesh['dp'=8,'tensor'=4] {'dp'}, use_global_device_ids=true, to_apply=%region_16.17 | all-reduce | flops 15360 | bytes 122880 | tf_op jit(solution)/shard_map/psum | solution.py:164
  1023.4 543.2 %all-reduce.16.cloned.1.call-done = (f32[2048,3,512]{2,0,1:T(8,128)}, f32[512,2048]{1,0:T(8,128)}, f32[2048,2048]{1,0:T(8,128)}, f32[2048,2048]{1,0:T(8,128)}) async-done(((f32[2048,3,512]{2,0,1:T(8,128)}, f32[512,2048]{1,0:T(8,128)}, f32[2048,2048]{1,0:T(8,128)}, f32[2048,2048]{1,0:T(8,128)}), (f32[2048,3,512]{2,0,1:T(8,128)}, f32[512,2048]{1,0:T(8,128)}, f32[2048,2048]{1,0:T(8,128)}, ...) | async-done | bytes 50331664 | tf_op jit(solution)/shard_map/psum | solution.py:164
  1566.6 11.1 copy.54
  1577.7 2.1 copy.55
  1579.8 14.0 copy.56
  1593.8 2.0 slice-done.3
  1595.9 6.3 copy.57
  (138 shorter events, 4.8 us)
Async XLA Ops:
  7.2 57.0 %copy-start = (bf16[512,2048]{1,0:T(8,128)(2,1)S(1)}, bf16[512,2048]{1,0:T(8,128)(2,1)}, u32[]{:S(2)}) copy-start(bf16[512,2048]{1,0:T(8,128)(2,1)} %param.21) | copy-start | bytes 6291460
  7.2 287.3 %all-reduce.8.cloned.1.call-start = ((), (), s32[]{:S(2)}) async-start(), calls=%async_computation | async-start | bytes 12582912 | tf_op jit(solution)/shard_map/psum | solution.py:87
  7.2 4.3 copy-start.2
  11.6 10.4 copy-start.24
  13.1 8.8 copy-start.28
  13.1 8.8 copy-start.26
  13.1 8.8 copy-start.45
  30.6 14.0 copy-start.15
  32.6 20.9 %copy-start.30 = (f32[8,64]{1,0:T(8,128)}, f32[8,64]{1,0:T(8,128)S(1)}, u32[]{:S(2)}) copy-start(f32[8,64]{1,0:T(8,128)S(1)} %add.163) | copy-start | bytes 6148
  32.7 11.9 copy-start.35
  64.2 230.3 %copy-start.38 = (f32[2048]{0:T(1024)S(1)}, f32[2048]{0:T(1024)}, u32[]{:S(2)}) copy-start(f32[2048]{0:T(1024)} %param.22) | copy-start | bytes 24580
  68.8 503.4 %all-reduce.12.cloned.1.call-start = ((), (), s32[]{:S(2)}) async-start(), calls=%async_computation.2 | async-start | bytes 12582912 | tf_op jit(solution)/shard_map/psum | solution.py:112
  299.1 12.4 copy-start.5
  299.9 11.6 copy-start.9
  299.9 11.6 copy-start.37
  311.5 26.1 %copy-start.12 = (f32[768,2048]{1,0:T(8,128)}, f32[768,2048]{1,0:T(8,128)S(1)}, u32[]{:S(2)}) copy-start(f32[768,2048]{1,0:T(8,128)S(1)} %fusion.41) | copy-start | bytes 18874372
  350.3 345.0 %all-reduce.10.cloned.1.call-start = ((), (), s32[]{:S(2)}) async-start(), calls=%async_computation.1 | async-start | bytes 6291456 | tf_op jit(solution)/shard_map/psum | solution.py:95
  369.0 326.2 %copy-start.39 = (f32[2048]{0:T(1024)S(1)}, f32[2048]{0:T(1024)}, u32[]{:S(2)}) copy-start(f32[2048]{0:T(1024)} %param.28) | copy-start | bytes 24580
  369.0 609.6 %all-reduce.14.cloned.1.call-start = ((), (), s32[]{:S(2)}) async-start(), calls=%async_computation.3 | async-start | bytes 12582912 | tf_op jit(solution)/shard_map/psum | solution.py:159
  695.2 8.1 copy-start.10
  705.9 11.4 copy-start.20
  707.8 9.6 copy-start.8
  707.8 9.6 copy-start.31
  729.3 13.7 copy-start.13
  729.3 13.7 copy-start.36
  743.0 6.5 slice-start.4
  756.7 13.0 copy-start.44
  756.7 809.9 %all-reduce.16.cloned.1.call-start = ((), (), s32[]{:S(2)}) async-start(), calls=%async_computation.4 | async-start | bytes 100663296 | tf_op jit(solution)/shard_map/psum | solution.py:164
  756.8 12.9 copy-start.48
  769.7 14.0 copy-start.18
  769.7 14.0 copy-start.21
  783.7 3.9 copy-start.3
  783.7 3.9 copy-start.23
  783.7 3.9 copy-start.25
  783.7 3.9 copy-start.27
  783.7 3.9 copy-start.29
  783.7 3.9 copy-start.46
  797.4 186.2 %copy-start.33 = (f32[768]{0:T(1024)S(1)}, f32[768]{0:T(1024)}, u32[]{:S(2)}) copy-start(f32[768]{0:T(1024)} %copy-done.32) | copy-start | bytes 9220
  978.7 5.5 copy-start.7
  983.5 5.4 copy-start.4
  983.5 5.4 copy-start.11
  988.9 6.6 copy-start.40
  1566.6 11.1 copy-start.14
  1577.7 16.2 %slice-start = ((s8[16777216]{0:T(1024)(128)(4,1)}), s8[4194304]{0:T(1024)(128)(4,1)S(1)}, s32[]{:S(2)}) async-start(s8[16777216]{0:T(1024)(128)(4,1)} %bitcast.61), calls=%async_computation.5 | async-start | bytes 8388608
  1579.8 14.0 slice-start.1
  1579.8 14.0 slice-start.2
  1579.8 16.0 slice-start.3
  1595.8 6.3 copy-start.1
  (12 other events, 21.1 us)
Sparse Core Ops, SparseCore 0:
  68.9 225.5 all-reduce.7
  350.4 221.7 all-reduce.11
  575.2 120.0 all-reduce.9
  756.8 221.8 all-reduce.13
  983.9 582.6 all-reduce.15
where the time goes:
time: 1620 us; the launch traced here: 1610 us
  waiting for transfers between devices  1270 us (78%)
  matrix products  169 us (10%)
  other arithmetic  71.5 us (4%)
  local copies, waits for them, and re-layouts  55.2 us (3%)
  blocking collectives  27.8 us (2%)
    psum x1, waiting for transfers between devices, on_device(): lax.psum((first_gain_grad, first_shift_grad, mixing_weight_grad, mixing_b...  543 us
    psum x1, waiting for transfers between devices, on_device(): resid = lax.psum(partial_out, 'tensor') + output_bias  226 us
    psum x1, waiting for transfers between devices, on_device(): second_grad = lax.psum(second_part, 'tensor')  203 us
    psum x1, waiting for transfers between devices, on_device(): normed_grad = lax.psum(normed_part, 'tensor')  181 us
    psum x1, waiting for transfers between devices, on_device(): lax.psum(partial_mlp.astype(jnp.bfloat16), 'tensor').astype(jnp.float32)  117 us
    unnamed x115, local copies, waits for them, and re-layouts  53 us
  transfers between devices with their start and end apart: 5, of which 5 were waited for; matrix products, arithmetic and copies ran while one was open for 5% of the time, Pallas kernels for 0%

commit v1 on v0

v1 whole, which is shorter than its diff:
```python
import functools
import math

import jax
import jax.numpy as jnp
from jax import lax
from jax.experimental import pallas as pl
from jax.experimental.pallas import tpu as pltpu
from jax.sharding import PartitionSpec as P

H = 32
HD = 64
EPS = 1e-05
F32 = jnp.float32
BF16 = jnp.bfloat16
MESH = pl.DeviceIdType.MESH


def layer_norm(values, scale_gain, shift_bias):
    row_mean = jnp.mean(values, axis=-1, keepdims=True)
    centred = values - row_mean
    row_var = jnp.mean(centred * centred, axis=-1, keepdims=True)
    return centred * lax.rsqrt(row_var + EPS) * scale_gain + shift_bias


def norm_backward(values, scale_gain, shift_bias, upstream):
    _, pull_back = jax.vjp(layer_norm, values, scale_gain, shift_bias)
    return pull_back(upstream)


def gelu_exact(values):
    return jax.nn.gelu(values, approximate=False)


def biased_scores(query, keys, blocks, first_head):
    length, local_heads, head_width = query.shape
    scores = jnp.einsum("qhd,khd->hqk", query, keys, preferred_element_type=F32) * (
        1.0 / math.sqrt(head_width)
    )
    heads_index = (first_head + jnp.arange(local_heads)).astype(F32)
    slopes = 2.0 ** (-8.0 * (heads_index + 1.0) / H)
    places = jnp.arange(length)
    offsets = (places[None, :] - places[:, None]).astype(F32)
    scores = scores + slopes[:, None, None] * offsets[None]
    allowed = blocks[None, :] <= blocks[:, None]
    return jnp.where(allowed[None], scores, -1e30)


def add_rows(dst, src, step):
    rows = dst.shape[0]

    def body(i, carry):
        at = pl.ds(pl.multiple_of(i * step, step), step)
        dst[at, :] = (dst[at, :].astype(F32) + src[at, :].astype(F32)).astype(BF16)
        return carry

    lax.fori_loop(0, rows // step, body, 0)


def sums_kernel(n, n_z, n_dp, chunks, pieces, *refs):
    z_in, refs = refs[:n_z], refs[n_z:]
    g_in, refs = refs[:n_dp], refs[n_dp:]
    z_out, refs = refs[0], refs[1:]
    g_out, refs = (refs[0], refs[1:]) if n_dp else (None, refs)
    part, outer_in, inner_in, load_sem, zs_in, zs_out, zr_outer, zr_inner, store_sem, *refs = refs
    if n_dp:
        fin, c0, r1, r2, gl, c0s, c0r, s1, q1, s2, q2, s3, q3, s4, q4, gstore = refs

    total_z = sum(chunks)
    total_p = sum(pieces)
    i = lax.axis_index("tensor")
    left = i < n // 2
    inner = jnp.where(left, i + 1, i - 1)
    depth = jnp.where(left, i, n - 1 - i)
    has_outer = depth > 0
    outer = jnp.where(has_outer, jnp.where(left, i - 1, i + 1), inner)
    is_mid = depth == n // 2 - 1
    lag = 2 * (n // 2 - 1 - depth) + 1

    if n_dp:
        d = lax.axis_index("dp")
        c, x, y = d % 2, (d // 2) % 2, d // 4
        to_c, to_x, to_y = d + 1 - 2 * c, d + 2 - 4 * x, d + 4 - 8 * y

    at = 0
    for k in range(n_z):
        pltpu.make_async_copy(z_in[k], part.at[pl.ds(at, chunks[k])], load_sem.at[k]).start()
        at += chunks[k]
    at = 0
    for k in range(n_dp):
        pltpu.make_async_copy(g_in[k].at[:, c], fin.at[pl.ds(at, pieces[k]), c], gl.at[k]).start()
        at += pieces[k]

    barrier = pltpu.get_barrier_semaphore()
    pl.semaphore_signal(barrier, inc=1, device_id={"tensor": inner}, device_id_type=MESH)

    @pl.when(has_outer)
    def _():
        pl.semaphore_signal(barrier, inc=1, device_id={"tensor": outer}, device_id_type=MESH)

    count = 1
    if n_dp:
        for to in (to_c, to_x, to_y):
            pl.semaphore_signal(barrier, inc=1, device_id={"dp": to}, device_id_type=MESH)
        count = 4

    @pl.when(has_outer)
    def _():
        pl.semaphore_wait(barrier, count + 1)

    @pl.when(jnp.logical_not(has_outer))
    def _():
        pl.semaphore_wait(barrier, count)

    def copy(src, dst, send, recv, axis, to):
        return pltpu.make_async_remote_copy(
            src_ref=src,
            dst_ref=dst,
            send_sem=send,
            recv_sem=recv,
            device_id={axis: to},
            device_id_type=MESH,
        )

    def inward_mid(k):
        return copy(part.at[k], inner_in.at[k], zs_in.at[k], zr_inner.at[k], "tensor", inner)

    def inward(k):
        return copy(part.at[k], outer_in.at[k], zs_in.at[k], zr_outer.at[k], "tensor", inner)

    def outward(k):
        return copy(inner_in.at[k], inner_in.at[k], zs_out.at[k], zr_inner.at[k], "tensor", outer)

    def store(k):
        return pltpu.make_async_copy(inner_in.at[k], z_out.at[k], store_sem.at[k])

    def z_reduce(k):
        at = 0
        for j in range(n_z):

            @pl.when(k == at)
            def _(j=j, at=at):
                pltpu.make_async_copy(z_in[j], part.at[pl.ds(at, chunks[j])], load_sem.at[j]).wait()

            at += chunks[j]

        @pl.when(has_outer)
        def _():
            inward(k).wait_recv()
            add_rows(part.at[k], outer_in.at[k], 16)

        @pl.when(is_mid)
        def _():
            inward_mid(k).start()

        @pl.when(jnp.logical_not(is_mid))
        def _():
            inward(k).start()

    def z_spread(k):
        inward_mid(k).wait_recv()

        @pl.when(is_mid)
        def _():
            add_rows(inner_in.at[k], part.at[k], 16)

        @pl.when(has_outer)
        def _():
            outward(k).start()

        store(k).start()

    if n_dp:

        def core_half(k, j, at):
            return copy(g_in[j].at[k - at, 1 - c], c0.at[k], c0s.at[k], c0r.at[k], "dp", to_c)

        def hop1(k):
            return (
                copy(fin.at[k, c, 0, 1 - x], r1.at[k, 0], s1.at[k, 0], q1.at[k, 0], "dp", to_x),
                copy(fin.at[k, c, 1, 1 - y], r1.at[k, 1], s1.at[k, 1], q1.at[k, 1], "dp", to_y),
            )

        def hop2(k):
            return (
                copy(fin.at[k, c, 0, x], r2.at[k, 0], s2.at[k, 0], q2.at[k, 0], "dp", to_y),
                copy(fin.at[k, c, 1, y], r2.at[k, 1], s2.at[k, 1], q2.at[k, 1], "dp", to_x),
            )

        def hop3(k):
            return (
                copy(fin.at[k, c, 0, x], fin.at[k, c, 0, x], s3.at[k, 0], q3.at[k, 0], "dp", to_x),
                copy(fin.at[k, c, 1, y], fin.at[k, c, 1, y], s3.at[k, 1], q3.at[k, 1], "dp", to_y),
            )

        def hop4(k):
            return copy(fin.at[k, c], fin.at[k, c], s4.at[k], q4.at[k], "dp", to_c)

        def g_store(k):
            return pltpu.make_async_copy(fin.at[k], g_out.at[k], gstore.at[k])

        at = 0
        for j in range(n_dp):

            def send_half(k, carry, j=j, at=at):
                core_half(k + at, j, at).start()
                return carry

            lax.fori_loop(0, pieces[j], send_half, 0)
            at += pieces[j]

        step = 32 if r1.shape[2] % 32 == 0 else 16

        def stage1(k):
            at = 0
            for j in range(n_dp):

                @pl.when(k == at)
                def _(j=j, at=at):
                    pltpu.make_async_copy(
                        g_in[j].at[:, c], fin.at[pl.ds(at, pieces[j]), c], gl.at[j]
                    ).wait()

                at += pieces[j]
            core_half(k, 0, k).wait_recv()
            for a in range(2):
                for b in range(2):
                    add_rows(fin.at[k, c, a, b], c0.at[k, a, b], step)
            for one in hop1(k):
                one.start()

        def stage2(k):
            for one in hop1(k):
                one.wait()
            add_rows(fin.at[k, c, 0, x], r1.at[k, 0], step)
            add_rows(fin.at[k, c, 1, y], r1.at[k, 1], step)
            for one in hop2(k):
                one.start()

        def stage3(k):
            for one in hop2(k):
                one.wait()
            add_rows(fin.at[k, c, 0, x], r2.at[k, 0], step)
            add_rows(fin.at[k, c, 1, y], r2.at[k, 1], step)
            for one in hop3(k):
                one.start()

        def stage4(k):
            for one in hop3(k):
                one.wait_recv()
            hop4(k).start()

        def stage5(k):
            hop4(k).wait_recv()
            g_store(k).start()

    def tick(t, carry):
        @pl.when(t < total_z)
        def _():
            z_reduce(t)

        back = t - lag

        @pl.when(jnp.logical_and(back >= 0, back < total_z))
        def _():
            z_spread(back)

        if n_dp:
            for late, stage in enumerate((stage1, stage2, stage3, stage4, stage5)):
                k = t - late

                @pl.when(jnp.logical_and(k >= 0, k < total_p))
                def _(stage=stage, k=k):
                    stage(k)

        return carry

    ticks = max(total_z + n - 1, total_p + 4 if n_dp else 0)
    lax.fori_loop(0, ticks, tick, 0)

    def drain_z(k, carry):
        @pl.when(is_mid)
        def _():
            inward_mid(k).wait_send()

        @pl.when(jnp.logical_not(is_mid))
        def _():
            inward(k).wait_send()

        @pl.when(has_outer)
        def _():
            outward(k).wait_send()

        store(k).wait()
        return carry

    lax.fori_loop(0, total_z, drain_z, 0)
    if n_dp:

        def drain_g(k, carry):
            core_half(k, 0, k).wait_send()
            for one in hop3(k) + (hop4(k),):
                one.wait_send()
            g_store(k).wait()
            return carry

        lax.fori_loop(0, total_p, drain_g, 0)


def device_sums(n, z_parts, g_parts, collective_id):
    chunks = tuple(one.shape[0] for one in z_parts)
    pieces = tuple(one.shape[0] for one in g_parts)
    nz, npc = sum(chunks), sum(pieces)
    z_block = z_parts[0].shape[1:]
    dma = pltpu.SemaphoreType.DMA
    scratch = [pltpu.VMEM((nz, *z_block), BF16)] * 3 + [dma((len(chunks),))] + [dma((nz,))] * 5
    out_shape = [jax.ShapeDtypeStruct((nz, *z_block), BF16)]
    vmem = 3 * nz * math.prod(z_block) * 2
    if g_parts:
        g_block = g_parts[0].shape[4:]
        scratch += [
            pltpu.VMEM((npc, 2, 2, 2, *g_block), BF16),
            pltpu.VMEM((npc, 2, 2, *g_block), BF16),
            pltpu.VMEM((npc, 2, *g_block), BF16),
            pltpu.VMEM((npc, 2, *g_block), BF16),
            dma((len(pieces),)),
            dma((npc,)),
            dma((npc,)),
        ]
        scratch += [dma((npc, 2))] * 6 + [dma((npc,))] * 3
        out_shape.append(jax.ShapeDtypeStruct((npc, 2, 2, 2, *g_block), BF16))
        vmem += 16 * npc * math.prod(g_block) * 2
    out = pl.pallas_call(
        functools.partial(sums_kernel, n, len(z_parts), len(g_parts), chunks, pieces),
        out_shape=out_shape,
        in_specs=[pl.BlockSpec(memory_space=pl.ANY)] * (len(z_parts) + len(g_parts)),
        out_specs=[pl.BlockSpec(memory_space=pl.ANY)] * len(out_shape),
        scratch_shapes=scratch,
        compiler_params=pltpu.CompilerParams(
            collective_id=collective_id, has_side_effects=True, vmem_limit_bytes=vmem + (2 << 20)
        ),
    )(*z_parts, *g_parts)
    return out


def on_device(
    fast,
    n_tensor,
    inputs,
    block_ids,
    first_gain,
    first_shift,
    mixing_weight,
    mixing_bias,
    output_weight,
    output_bias,
    second_gain,
    second_shift,
    expand_weight,
    expand_bias,
    shrink_weight,
    shrink_bias,
    cotangent,
):
    source = inputs.astype(F32)
    upstream = cotangent.astype(F32)
    length, width = source.shape
    blocks = block_ids[0]
    local_width = mixing_weight.shape[2]
    local_heads = local_width // HD
    units = expand_weight.shape[1]
    first_head = lax.axis_index("tensor") * local_heads
    rows = 96

    def sums(z_parts, g_parts, collective_id):
        if not fast:
            return (
                [lax.psum(one.astype(BF16), "tensor").astype(F32) for one in z_parts],
                [lax.psum(one, "dp") for one in g_parts],
            )
        z_low = [one.astype(BF16).reshape(length // rows, rows, width) for one in z_parts]
        out = device_sums(n_tensor, z_low, [one.astype(BF16) for one in g_parts], collective_id)
        z_all = out[0].reshape(len(z_parts), length, width)
        z_out = [z_all[k].astype(F32) for k in range(len(z_parts))]
        g_out, at = [], 0
        for one in g_parts:
            g_out.append(out[1][at : at + one.shape[0]].astype(F32))
            at += one.shape[0]
        return z_out, g_out

    weights = mixing_weight.transpose(1, 0, 2)
    normed_low = layer_norm(source, first_gain, first_shift).astype(BF16)

    def project(k):
        return jnp.dot(normed_low, weights[k], preferred_element_type=F32)

    query = (project(0) + mixing_bias[0]).astype(BF16).reshape(length, local_heads, HD)
    keys = project(1).astype(BF16).reshape(length, local_heads, HD)
    vals = (project(2) + mixing_bias[1]).astype(BF16).reshape(length, local_heads, HD)
    masked = biased_scores(query, keys, blocks, first_head)
    row_top = jnp.max(masked, axis=-1, keepdims=True)
    logsum = row_top + jnp.log(jnp.sum(jnp.exp(masked - row_top), axis=-1, keepdims=True))
    probs_low = jnp.exp(masked - logsum).astype(BF16)
    attended = (
        jnp.einsum("hqk,khd->qhd", probs_low, vals, preferred_element_type=F32)
        .reshape(length, local_width)
        .astype(BF16)
    )
    partial_out = jnp.dot(attended, output_weight, preferred_element_type=F32)
    (resid,), _ = sums([partial_out], [], 0)
    hidden_state = source + (resid + output_bias)
    second_low = layer_norm(hidden_state, second_gain, second_shift).astype(BF16)
    pre_act = jnp.dot(second_low, expand_weight, preferred_element_type=F32) + expand_bias
    activ_low = gelu_exact(pre_act).astype(BF16)
    partial_mlp = jnp.dot(activ_low, shrink_weight, preferred_element_type=F32)
    act_grad = jnp.einsum("td,fd->tf", cotangent, shrink_weight, preferred_element_type=F32)
    _, gelu_pull = jax.vjp(gelu_exact, pre_act)
    pre_grad = gelu_pull(act_grad)[0].astype(BF16)
    shrink_part = jnp.einsum("tf,td->fd", activ_low, cotangent, preferred_element_type=F32)
    shrink_bias_part = jnp.sum(upstream, axis=0)
    expand_part = jnp.einsum("td,tf->df", second_low, pre_grad, preferred_element_type=F32)
    expand_bias_part = jnp.sum(pre_grad.astype(F32), axis=0)
    second_part = jnp.einsum("tf,df->td", pre_grad, expand_weight, preferred_element_type=F32)

    (second_grad, mlp_sum), (shrink_sum, expand_sum) = sums(
        [second_part, partial_mlp],
        [
            shrink_part.reshape(-1, 2, 2, 2, 32, width),
            expand_part.reshape(-1, 2, 2, 2, 32, units),
        ],
        1,
    )
    shrink_weight_grad = shrink_sum.reshape(units, width)
    expand_weight_grad = expand_sum.reshape(width, units)
    outputs = (hidden_state + mlp_sum + shrink_bias).astype(BF16)
    hidden_grad, second_gain_part, second_shift_part = norm_backward(
        hidden_state, second_gain, second_shift, second_grad
    )
    hidden_grad = hidden_grad + upstream
    resid_low = hidden_grad.astype(BF16)
    output_part = jnp.einsum("tc,td->cd", attended, resid_low, preferred_element_type=F32)
    output_bias_part = jnp.sum(resid_low.astype(F32), axis=0)
    attended_grad = (
        jnp.einsum("td,cd->tc", resid_low, output_weight, preferred_element_type=F32)
        .astype(BF16)
        .reshape(length, local_heads, HD)
    )
    probs = jnp.exp(biased_scores(query, keys, blocks, first_head) - logsum)
    probs_low = probs.astype(BF16)
    prob_grad = jnp.einsum("qhd,khd->hqk", attended_grad, vals, preferred_element_type=F32)
    vals_grad = jnp.einsum(
        "hqk,qhd->khd", probs_low, attended_grad, preferred_element_type=F32
    ).astype(BF16)
    row_delta = jnp.sum(probs * prob_grad, axis=-1, keepdims=True)
    score_grad = (probs * (prob_grad - row_delta)).astype(BF16)
    scale_factor = 1.0 / math.sqrt(HD)
    query_grad = (
        jnp.einsum("hqk,khd->qhd", score_grad, keys, preferred_element_type=F32) * scale_factor
    ).astype(BF16)
    keys_grad = (
        jnp.einsum("hqk,qhd->khd", score_grad, query, preferred_element_type=F32) * scale_factor
    ).astype(BF16)
    grads = [one.reshape(length, local_width) for one in (query_grad, keys_grad, vals_grad)]
    mixing_part = jnp.stack(
        [jnp.einsum("td,tc->dc", normed_low, one, preferred_element_type=F32) for one in grads]
    )
    mixing_bias_part = jnp.stack(
        [jnp.sum(grads[0].astype(F32), axis=0), jnp.sum(grads[2].astype(F32), axis=0)]
    )
    normed_part = sum(
        jnp.einsum("tc,dc->td", one, weights[k], preferred_element_type=F32)
        for k, one in enumerate(grads)
    )
    quarters = width // local_width
    (normed_grad,), (mixing_sum, output_sum) = sums(
        [normed_part],
        [
            mixing_part.reshape(-1, 2, 2, 2, 128, local_width),
            output_part.reshape(local_width, quarters, local_width)
            .transpose(1, 0, 2)
            .reshape(-1, 2, 2, 2, 128, local_width),
        ],
        2,
    )
    mixing_weight_grad = mixing_sum.reshape(3, width, local_width).transpose(1, 0, 2)
    output_weight_grad = (
        output_sum.reshape(quarters, local_width, local_width)
        .transpose(1, 0, 2)
        .reshape(local_width, width)
    )
    source_grad, first_gain_part, first_shift_part = norm_backward(
        source, first_gain, first_shift, normed_grad
    )
    input_grad = (source_grad + hidden_grad).astype(BF16)
    small = lax.psum(
        (
            first_gain_part,
            first_shift_part,
            mixing_bias_part,
            output_bias_part,
            second_gain_part,
            second_shift_part,
            expand_bias_part,
            shrink_bias_part,
        ),
        "dp",
    )
    return (
        outputs,
        input_grad,
        small[0],
        small[1],
        mixing_weight_grad,
        small[2],
        output_weight_grad,
        small[3],
        small[4],
        small[5],
        expand_weight_grad,
        small[6],
        shrink_weight_grad,
        small[7],
    )


def solution(mesh):
    in_specs = (
        P("dp", None),
        P("dp", None),
        P(),
        P(),
        P(None, None, "tensor"),
        P(None, "tensor"),
        P("tensor", None),
        P(),
        P(),
        P(),
        P(None, "tensor"),
        P("tensor"),
        P("tensor", None),
        P(),
        P("dp", None),
    )
    out_specs = (
        P("dp", None),
        P("dp", None),
        P(),
        P(),
        P(None, None, "tensor"),
        P(None, "tensor"),
        P("tensor", None),
        P(),
        P(),
        P(),
        P(None, "tensor"),
        P("tensor"),
        P("tensor", None),
        P(),
    )
    n_tensor = mesh.shape["tensor"]
    fast = mesh.shape["dp"] == 8 and n_tensor % 2 == 0
    return jax.shard_map(
        functools.partial(on_device, fast, n_tensor),
        mesh=mesh,
        in_specs=in_specs,
        out_specs=out_specs,
        check_vma=False,
    )
```

time: 1620 us -> 662 us (0.41)
  waiting for transfers between devices: 1270 us -> 0 us
  Pallas kernels: 0 us -> 350 us
  local copies, waits for them, and re-layouts: 55.2 us -> 29.5 us
  other arithmetic: 71.5 us -> 88.2 us
    psum x5 -> x0, waiting for transfers between devices: 1270 us -> none  [the longest x1 543 us: on_device(): lax.psum((first_gain_grad, first_shift_grad, mixing_weight_grad, mixing_b...]
    pallas_call x0 -> x3, Pallas kernels: none -> 350 us  [device_sums(): pl.pallas_call(functools.partial(sums_kernel, n, len(z_parts), len(g_part...]
    unnamed x115 -> x114, local copies, waits for them, and re-layouts: 53 us -> 9.73 us
    dot_general x15 -> x21, matrix products: 131 us -> 128 us  [the longest x3 16.7 us: on_device(): jnp.einsum('tc,dc->td', one, weights[k], preferred_element_type=F32)]
  transfers between devices with their start and end apart: 5 -> 0, of which waited for: 5 -> 0; matrix products, arithmetic and copies ran while one was open for 5% -> 0% of each run, Pallas kernels for 0% -> 0%
where the time goes in v1:
time: 662 us; the launch traced here: 656 us
  Pallas kernels  350 us (53%)
  matrix products  162 us (24%)
  other arithmetic  88.2 us (13%)
  local copies, waits for them, and re-layouts  29.5 us (4%)
  blocking collectives  25 us (4%)
    pallas_call x3, Pallas kernels, device_sums(): pl.pallas_call(functools.partial(sums_kernel, n, len(z_parts), len(g_part...  350 us
    psum x1, blocking collectives, on_device(): lax.psum((first_gain_part, first_shift_part, mixing_bias_part, output_bia...  25 us
    dot_general x1, matrix products, on_device(): jnp.einsum('td,fd->tf', cotangent, shrink_weight, preferred_element_type=...  22.7 us
    dot_general x3, matrix products, on_device(): jnp.einsum('tc,dc->td', one, weights[k], preferred_element_type=F32)  16.7 us
    dot_general x3, matrix products, project(): return jnp.dot(normed_low, weights[k], preferred_element_type=F32)  14.5 us
    reduce_sum x5, other arithmetic, layer_norm(): return centred * lax.rsqrt(row_var + EPS) * scale_gain + shift_bias  14 us
    convert_element_type x1, other arithmetic, on_device(): score_grad = (probs * (prob_grad - row_delta)).astype(BF16)  13.3 us

profile of v1, /device:TPU:0, one launch (start us, length us, event | category | flops | bytes accessed | tf_op | source)
XLA Modules:
  0.0 656.4 jit_solution(12743143254410044952)
XLA Ops:
  0.7 2.5 convert_reduce_fusion
  3.2 2.8 fusion.10
  8.0 4.7 fusion.41
  14.4 5.3 add_convert_fusion.4
  20.1 10.9 %fusion.56 = (f32[8,768]{1,0:T(8,128)S(1)}, f32[8,768,768]{1,2,0:T(8,128)}) fusion(f32[768,768]{0,1:T(8,128)} %subtract_convert_fusion, f32[8]{0:T(128)S(1)} %multiply_power_fusion, bf16[768,8,64]{0,2,1:T(8,128)(2,1)} %bitcast.202, bf16[768,8,64]{0,2,1:T(8,128)(2,1)S(1)} %bitcast.198, pred[768,768]{0,1:T(8,128)(4,1)S(1)} %broadcast_compare_fusion), kind=kOutput, calls=%fused_computation.121 | convolution fusion | flops 627566592 | bytes 23420960 | tf_op jit(solution)/shard_map/qhd,khd->hqk/dot_general | solution.py:37
  31.0 8.9 %exponential_reduce_fusion = f32[8,768]{1,0:T(8,128)S(1)} fusion(f32[8,768,768]{1,2,0:T(8,128)} %get-tuple-element.49, f32[8,768]{1,0:T(8,128)S(1)} %get-tuple-element.48), kind=kLoop, calls=%fused_computation.3 | loop fusion | flops 9431040 | bytes 18923520 | tf_op jit(solution)/shard_map/reduce_sum | solution.py:402
  39.9 4.5 add_convert_fusion.5
  44.4 3.7 copy-done.7
  48.1 3.2 fusion.42
  51.3 1.8 convolution_convert_fusion.4
  53.2 91.8 %shard_map.257 = bf16[8,96,2048]{2,1,0:T(8,128)(2,1)S(1)} custom-call(bf16[8,96,2048]{2,1,0:T(8,128)(2,1)S(1)} %bitcast.169), custom_call_target="tpu_custom_call" | custom-call | tf_op jit(solution)/shard_map/pallas_call | solution.py:333
  147.9 2.7 copy-done.17
  150.6 9.4 %fusion.50 = f32[768,2048]{1,0:T(8,128)S(1)} fusion(bf16[2048,2048]{1,0:T(8,128)(2,1)} %param.25, f32[768,2048]{1,0:T(8,128)S(1)} %get-tuple-element.42, f32[2048]{0:T(1024)S(1)} %copy-done.51, f32[2048]{0:T(1024)S(1)} %copy-done.38, f32[768]{0:T(1024)S(1)} %fusion.49), kind=kOutput, calls=%fused_computation.117 | convolution fusion | flops 6448742400 | bytes 20990976 | tf_op jit(solution)/shard_map/dot_general | solution.py:413
  160.1 22.7 %convert_reduce_fusion.4 = (f32[2048]{0:T(1024)}, bf16[768,2048]{1,0:T(8,128)(2,1)}, f32[768,2048]{1,0:T(8,128)S(1)}) fusion(f32[768,2048]{1,0:T(8,128)S(1)} %fusion.50, f32[2048]{0:T(1024)S(1)} %copy-done.45, bf16[768,2048]{1,0:T(8,128)(2,1)S(1)} %copy-done.14, bf16[2048,2048]{1,0:T(8,128)(2,1)S(1)} %bitcast.207), kind=kOutput, calls=%fused_computation.46 | convolution fusion | flops 6560413696 | bytes 27279360 | tf_op jit(solution)/shard_map/td,fd->tf/dot_general | solution.py:416
  182.8 12.1 %convolution_convert_fusion.3 = bf16[768,2048]{1,0:T(8,128)(2,1)} fusion(bf16[768,2048]{1,0:T(8,128)(2,1)} %get-tuple-element.35, bf16[2048,2048]{1,0:T(8,128)(2,1)} %param.25), kind=kOutput, calls=%fused_computation.73 | convolution fusion | flops 6444023808 | bytes 14680064 | tf_op jit(solution)/shard_map/tf,df->td/dot_general | solution.py:423
  194.9 3.3 multiply_convert_fusion.1
  198.2 12.0 %convolution_convert_fusion.2 = bf16[768,2048]{1,0:T(8,128)(2,1)} fusion(bf16[768,2048]{1,0:T(8,128)(2,1)} %multiply_convert_fusion.1, bf16[2048,2048]{1,0:T(8,128)(2,1)} %param.27), kind=kOutput, calls=%fused_computation.72 | convolution fusion | flops 6444023808 | bytes 14680064 | tf_op jit(solution)/shard_map/dot_general | solution.py:415
  210.2 9.1 %convolution_convert_fusion.1 = bf16[2048,2048]{1,0:T(8,128)(2,1)} fusion(bf16[768,2048]{1,0:T(8,128)(2,1)S(1)} %copy-done.18, bf16[768,2048]{1,0:T(8,128)(2,1)S(1)} %copy-done.14), kind=kOutput, calls=%fused_computation.22 | convolution fusion | flops 6446645248 | bytes 14680064 | tf_op jit(solution)/shard_map/tf,td->fd/dot_general | solution.py:419
  219.3 12.1 %convolution_convert_fusion = bf16[2048,2048]{1,0:T(8,128)(2,1)} fusion(bf16[768,2048]{1,0:T(8,128)(2,1)S(1)} %copy-done.52, f32[768,2048]{1,0:T(8,128)} %copy-done.17, f32[2048]{0:T(1024)S(1)} %copy-done.51, f32[2048]{0:T(1024)S(1)} %copy-done.38, f32[768]{0:T(1024)S(1)} %fusion.49), kind=kOutput, calls=%fused_computation.21 | convolution fusion | flops 6452936704 | bytes 17845248 | tf_op jit(solution)/shard_map/td,tf->df/dot_general | solution.py:421
  231.4 159.7 %shard_map.258 = (bf16[16,96,2048]{2,1,0:T(8,128)(2,1)}, bf16[16,2,2,2,32,2048]{5,4,3,2,1,0:T(8,128)(2,1)}) custom-call(bf16[8,96,2048]{2,1,0:T(8,128)(2,1)} %bitcast.190, bf16[8,96,2048]{2,1,0:T(8,128)(2,1)} %bitcast.191, bf16[8,2,2,2,32,2048]{5,4,3,2,1,0:T(8,128)(2,1)} %bitcast.176, bf16[8,2,2,2,32,2048]{5,4,3,2,1,0:T(8,128)(2,1)} %bitcast.177), custom_call_target="tpu_custom_call" | custom-call | tf_op jit(solution)/shard_map/pallas_call | solution.py:333
  391.2 3.9 fusion.18
  395.1 4.1 fusion.19
  399.2 3.9 convert_reduce_fusion.5
  403.1 1.8 convolution_convert_fusion.9
  405.0 11.9 %multiply_reduce_fusion = (f32[8,768]{1,0:T(8,128)S(1)}, f32[8,768,768]{1,2,0:T(8,128)}) fusion(f32[8,768,768]{1,2,0:T(8,128)} %get-tuple-element.49, f32[8,768]{1,0:T(8,128)S(1)} %copy-done.29, bf16[768,8,64]{0,2,1:T(8,128)(2,1)S(1)} %bitcast.196, bf16[768,8,64]{0,2,1:T(8,128)(2,1)S(1)} %bitcast.195), kind=kOutput, calls=%fused_computation.1 | convolution fusion | flops 618129408 | bytes 39370752 | tf_op jit(solution)/shard_map/qhd,khd->hqk/dot_general | solution.py:450
  416.9 13.3 %multiply_convert_fusion = bf16[8,768,768]{1,2,0:T(8,128)(2,1)S(1)} fusion(f32[8,768,768]{1,2,0:T(8,128)} %get-tuple-element.51, f32[8,768,768]{1,2,0:T(8,128)} %get-tuple-element.49, f32[8,768]{1,0:T(8,128)S(1)} %get-tuple-element.50, f32[8,768]{1,0:T(8,128)S(1)} %copy-done.29), kind=kLoop, calls=%fused_computation | loop fusion | flops 18874368 | bytes 47235072 | tf_op jit(solution)/shard_map/convert_element_type | solution.py:455
  430.3 1.9 convert_reduce_fusion.7
  432.1 3.5 fusion.37
  435.7 2.9 multiply_convert_fusion.2
  438.6 6.1 fusion.39
  444.8 9.4 %convert_reduce_fusion.6 = (f32[8,64]{1,0:T(8,128)S(1)}, bf16[8,64,768]{2,1,0:T(8,128)(2,1)S(1)}) fusion(bf16[768,8,64]{0,2,1:T(8,128)(2,1)S(1)} %bitcast.197, f32[8,768,768]{1,2,0:T(8,128)} %get-tuple-element.49, f32[8,768]{1,0:T(8,128)S(1)} %copy-done.29), kind=kOutput, calls=%fused_computation.93 | convolution fusion | flops 614596096 | bytes 20473856 | tf_op jit(solution)/shard_map/hqk,qhd->khd/dot_general | solution.py:451
  454.2 7.1 %add_convert_fusion.1 = bf16[768,2048]{1,0:T(8,128)(2,1)} fusion(f32[768,2048]{1,0:T(8,128)S(1)} %fusion.37, f32[768,2048]{1,0:T(8,128)} %fusion.39, bf16[768,512]{0,1:T(8,128)(2,1)S(1)} %bitcast.187, bf16[3,2048,512]{2,1,0:T(8,128)(2,1)} %bitcast.183), kind=kOutput, calls=%fused_computation.49 | convolution fusion | flops 1615331328 | bytes 18612224 | tf_op jit(solution)/shard_map/tc,dc->td/dot_general | solution.py:471
  461.3 2.0 fusion.31
  463.4 1.9 fusion.30
  465.2 1.9 fusion.29
  467.1 3.1 pad_maximum_fusion
  470.2 4.7 copy.39
  474.9 3.9 convolution_convert_fusion.8
  479.6 98.3 %shard_map.259 = (bf16[8,96,2048]{2,1,0:T(8,128)(2,1)S(1)}, bf16[8,2,2,2,128,512]{5,4,3,2,1,0:T(8,128)(2,1)S(1)}) custom-call(bf16[8,96,2048]{2,1,0:T(8,128)(2,1)S(1)} %bitcast.168, bf16[6,2,2,2,128,512]{5,4,3,2,1,0:T(8,128)(2,1)S(1)} %bitcast.167, bf16[2,2,2,2,128,512]{5,4,3,2,1,0:T(8,128)(2,1)S(1)} %bitcast.170), custom_call_target="tpu_custom_call" | custom-call | tf_op jit(solution)/shard_map/pallas_call | solution.py:333
  579.3 3.3 fusion.9
  585.0 10.4 %add_convert_fusion = (bf16[768,2048]{1,0:T(8,128)(2,1)}, bf16[768,2048]{1,0:T(8,128)(2,1)}, f32[2048]{0:T(1024)S(1)}) fusion(bf16[768,2048]{1,0:T(8,128)(2,1)S(1)} %copy-done.11, bf16[8,96,2048]{2,1,0:T(8,128)(2,1)S(1)} %get-tuple-element.19, bf16[768,2048]{1,0:T(8,128)(2,1)S(1)} %copy-done.16, f32[768]{0:T(1024)S(1)} %negate_multiply_fusion.1, ...), kind=kLoop, calls=%fused_computation.48 | loop fusion | flops 45611008 | bytes 25231360 | tf_op jit(solution)/shard_map/convert_element_type | solution.py:494
  596.9 25.0 %all-reduce = (f32[2048]{0:T(1024)}, f32[2048]{0:T(1024)}, f32[2,512]{1,0:T(2,128)}, f32[2048]{0:T(1024)}, f32[2048]{0:T(1024)}, /*index=5*/f32[2048]{0:T(1024)}, f32[2048]{0:T(1024)}, f32[2048]{0:T(1024)}) all-reduce(f32[2048]{0:T(1024)S(1)} %get-tuple-element.24, ...), channel_id=1, replica_groups=mesh['dp'=8,'tensor'=4] {'dp'}, use_global_device_ids=true, to_apply=%region_12.13 | all-reduce | flops 15360 | bytes 122880 | tf_op jit(solution)/shard_map/psum | solution.py:495
  621.9 3.5 slice.45
  625.4 6.6 %convert_bitcast_fusion = f32[2048,3,512]{2,0,1:T(8,128)} fusion(bf16[3,2048,512]{2,1,0:T(8,128)(2,1)S(1)} %bitcast.173), kind=kLoop, calls=%fused_computation.6 | loop fusion | flops 3145728 | bytes 18874368 | tf_op jit(solution)/shard_map/transpose | solution.py:485
  632.0 1.8 slice.46
  634.3 2.7 copy.40
  637.0 6.6 fusion.54
  643.6 12.6 %bitcast_convert_fusion = (f32[2048,2048]{1,0:T(8,128)}, f32[2048,2048]{1,0:T(8,128)}) fusion(bf16[8,2,2,2,32,2048]{5,4,3,2,1,0:T(8,128)(2,1)S(1)} %get-tuple-element.39, bf16[8,2,2,2,32,2048]{5,4,3,2,1,0:T(8,128)(2,1)S(1)} %get-tuple-element.40), kind=kLoop, calls=%fused_computation.17 | loop fusion | flops 8388608 | bytes 50331648 | tf_op jit(solution)/shard_map/reshape | solution.py:433
  (138 shorter events, 13.3 us)
Async XLA Ops:
  0.6 50.7 %copy-start = (bf16[512,2048]{1,0:T(8,128)(2,1)S(1)}, bf16[512,2048]{1,0:T(8,128)(2,1)}, u32[]{:S(2)}) copy-start(bf16[512,2048]{1,0:T(8,128)(2,1)} %param.21) | copy-start | bytes 6291460
  0.7 6.0 copy-start.8
  0.7 6.0 copy-start.46
  0.7 6.0 copy-start.36
  3.2 9.4 %copy-start.32 = (f32[768]{0:T(1024)}, f32[768]{0:T(1024)S(1)}, u32[]{:S(2)}) copy-start(f32[768]{0:T(1024)S(1)} %broadcast_multiply_fusion.1) | copy-start | bytes 9220
  6.7 5.9 copy-start.39
  7.9 4.7 copy-start.19
  7.9 6.4 copy-start.49
  12.7 7.4 %copy-start.23 = (bf16[768,512]{0,1:T(8,128)(2,1)}, bf16[768,512]{0,1:T(8,128)(2,1)S(1)}, u32[]{:S(2)}) copy-start(bf16[768,512]{0,1:T(8,128)(2,1)S(1)} %fusion.41) | copy-start | bytes 2359300
  14.4 5.3 copy-start.50
  39.9 4.6 copy-start.28
  39.9 8.2 %copy-start.7 = (f32[8,768,768]{1,2,0:T(8,128)S(1)}, f32[8,768,768]{1,2,0:T(8,128)}, u32[]{:S(2)}) copy-start(f32[8,768,768]{1,2,0:T(8,128)} %get-tuple-element.49) | copy-start | bytes 56623108
  44.4 6.9 %copy-start.21 = (bf16[768,512]{0,1:T(8,128)(2,1)}, bf16[768,512]{0,1:T(8,128)(2,1)S(1)}, u32[]{:S(2)}) copy-start(bf16[768,512]{0,1:T(8,128)(2,1)S(1)} %add_convert_fusion.5) | copy-start | bytes 2359300
  51.3 93.7 %copy-start.25 = (bf16[8,64,768]{2,1,0:T(8,128)(2,1)}, bf16[8,64,768]{2,1,0:T(8,128)(2,1)S(1)}, u32[]{:S(2)}) copy-start(bf16[8,64,768]{2,1,0:T(8,128)(2,1)S(1)} %fusion.42) | copy-start | bytes 2359300
  51.3 93.7 %copy-start.9 = (bf16[768,2048]{1,0:T(8,128)(2,1)S(1)}, bf16[768,2048]{1,0:T(8,128)(2,1)}, u32[]{:S(2)}) copy-start(bf16[768,2048]{1,0:T(8,128)(2,1)} %param.15) | copy-start | bytes 9437188
  51.3 93.7 %copy-start.30 = (f32[2048]{0:T(1024)S(1)}, f32[2048]{0:T(1024)}, u32[]{:S(2)}) copy-start(f32[2048]{0:T(1024)} %param.22) | copy-start | bytes 24580
  146.2 4.3 copy-start.38
  146.2 4.3 copy-start.51
  146.2 13.8 %slice-start.2 = ((s8[8388608]{0:T(1024)(128)(4,1)}), s8[4194304]{0:T(1024)(128)(4,1)S(1)}, s32[]{:S(2)}) async-start(s8[8388608]{0:T(1024)(128)(4,1)} %bitcast.206), calls=%async_computation.2 | async-start | bytes 8388608
  147.9 12.1 %copy-start.43 = (f32[768]{0:T(1024)}, f32[768]{0:T(1024)S(1)}, u32[]{:S(2)}) copy-start(f32[768]{0:T(1024)S(1)} %get-tuple-element.41) | copy-start | bytes 9220
  150.6 9.5 %copy-start.14 = (bf16[768,2048]{1,0:T(8,128)(2,1)S(1)}, bf16[768,2048]{1,0:T(8,128)(2,1)}, u32[]{:S(2)}) copy-start(bf16[768,2048]{1,0:T(8,128)(2,1)} %param.29) | copy-start | bytes 9437188
  150.6 9.5 %copy-start.45 = (f32[2048]{0:T(1024)S(1)}, f32[2048]{0:T(1024)}, u32[]{:S(2)}) copy-start(f32[2048]{0:T(1024)} %param.26) | copy-start | bytes 24580
  150.6 9.5 %slice-start.3 = ((s8[8388608]{0:T(1024)(128)(4,1)}), s8[4194304]{0:T(1024)(128)(4,1)S(1)}, s32[]{:S(2)}) async-start(s8[8388608]{0:T(1024)(128)(4,1)} %bitcast.206), calls=%async_computation.3 | async-start | bytes 8388608
  198.2 12.0 %copy-start.18 = (bf16[768,2048]{1,0:T(8,128)(2,1)S(1)}, bf16[768,2048]{1,0:T(8,128)(2,1)}, u32[]{:S(2)}) copy-start(bf16[768,2048]{1,0:T(8,128)(2,1)} %multiply_convert_fusion.1) | copy-start | bytes 9437188
  210.2 9.1 %copy-start.52 = (bf16[768,2048]{1,0:T(8,128)(2,1)S(1)}, bf16[768,2048]{1,0:T(8,128)(2,1)}, u32[]{:S(2)}) copy-start(bf16[768,2048]{1,0:T(8,128)(2,1)} %get-tuple-element.35) | copy-start | bytes 9437188
  231.4 159.7 %copy-start.2 = (bf16[8,96,2048]{2,1,0:T(8,128)(2,1)S(1)}, bf16[8,96,2048]{2,1,0:T(8,128)(2,1)}, u32[]{:S(2)}) copy-start(bf16[8,96,2048]{2,1,0:T(8,128)(2,1)} %copy-done.1) | copy-start | bytes 9437188
  231.4 159.8 %copy-start.10 = (bf16[768,2048]{1,0:T(8,128)(2,1)S(1)}, bf16[768,2048]{1,0:T(8,128)(2,1)}, u32[]{:S(2)}) copy-start(bf16[768,2048]{1,0:T(8,128)(2,1)} %param.15) | copy-start | bytes 9437188
  231.4 159.8 %copy-start.31 = (f32[2048]{0:T(1024)S(1)}, f32[2048]{0:T(1024)}, u32[]{:S(2)}) copy-start(f32[2048]{0:T(1024)} %param.22) | copy-start | bytes 24580
  231.4 159.8 %copy-start.35 = (f32[768]{0:T(1024)S(1)}, f32[768]{0:T(1024)}, u32[]{:S(2)}) copy-start(f32[768]{0:T(1024)} %copy-done.34) | copy-start | bytes 9220
  391.1 3.9 copy-start.44
  391.1 3.9 copy-start.12
  395.0 4.1 copy-start.15
  403.1 13.8 %copy-start.13 = (bf16[768,2048]{1,0:T(8,128)(2,1)}, bf16[768,2048]{1,0:T(8,128)(2,1)S(1)}, u32[]{:S(2)}) copy-start(bf16[768,2048]{1,0:T(8,128)(2,1)S(1)} %get-tuple-element.38) | copy-start | bytes 9437188
  416.9 13.3 %copy-start.24 = (bf16[768,512]{0,1:T(8,128)(2,1)S(1)}, bf16[768,512]{0,1:T(8,128)(2,1)}, u32[]{:S(2)}) copy-start(bf16[768,512]{0,1:T(8,128)(2,1)} %copy-done.23) | copy-start | bytes 2359300
  454.2 7.1 %copy-start.20 = (bf16[768,2048]{1,0:T(8,128)(2,1)S(1)}, bf16[768,2048]{1,0:T(8,128)(2,1)}, u32[]{:S(2)}) copy-start(bf16[768,2048]{1,0:T(8,128)(2,1)} %copy-done.19) | copy-start | bytes 9437188
  470.2 4.7 copy-start.26
  474.9 4.7 copy-start.5
  478.8 99.1 %copy-start.11 = (bf16[768,2048]{1,0:T(8,128)(2,1)S(1)}, bf16[768,2048]{1,0:T(8,128)(2,1)}, u32[]{:S(2)}) copy-start(bf16[768,2048]{1,0:T(8,128)(2,1)} %param.15) | copy-start | bytes 9437188
  478.8 99.1 %copy-start.33 = (f32[768]{0:T(1024)S(1)}, f32[768]{0:T(1024)}, u32[]{:S(2)}) copy-start(f32[768]{0:T(1024)} %copy-done.32) | copy-start | bytes 9220
  478.8 99.1 %copy-start.37 = (f32[2048]{0:T(1024)S(1)}, f32[2048]{0:T(1024)}, u32[]{:S(2)}) copy-start(f32[2048]{0:T(1024)} %param.17) | copy-start | bytes 24580
  479.6 99.7 %copy-start.42 = (f32[768]{0:T(1024)S(1)}, f32[768]{0:T(1024)}, u32[]{:S(2)}) copy-start(f32[768]{0:T(1024)} %copy-done.41) | copy-start | bytes 9220
  479.6 99.7 %copy-start.40 = (f32[768]{0:T(1024)S(1)}, f32[768]{0:T(1024)}, u32[]{:S(2)}) copy-start(f32[768]{0:T(1024)} %copy-done.39) | copy-start | bytes 9220
  479.6 103.1 %slice-start = ((s8[6291456]{0:T(1024)(128)(4,1)}), s8[2097152]{0:T(1024)(128)(4,1)S(1)}, s32[]{:S(2)}) async-start(s8[6291456]{0:T(1024)(128)(4,1)} %bitcast.171), calls=%async_computation | async-start | bytes 4194304
  577.9 4.8 copy-start.6
  577.9 5.2 slice-start.1
  579.3 4.7 copy-start.3
  579.3 5.6 copy-start.16
  579.3 5.6 copy-start.47
  (9 other events, 20.4 us)

commit v2 on v0

v2 whole, which is shorter than its diff:
```python
import functools
import math

import jax
import jax.numpy as jnp
from jax import lax
from jax.experimental import pallas as pl
from jax.experimental.pallas import tpu as pltpu
from jax.sharding import PartitionSpec as P

H = 32
HD = 64
EPS = 1e-05
F32 = jnp.float32
BF16 = jnp.bfloat16
MESH = pl.DeviceIdType.MESH


def layer_norm(values, scale_gain, shift_bias):
    row_mean = jnp.mean(values, axis=-1, keepdims=True)
    centred = values - row_mean
    row_var = jnp.mean(centred * centred, axis=-1, keepdims=True)
    return centred * lax.rsqrt(row_var + EPS) * scale_gain + shift_bias


def norm_backward(values, scale_gain, shift_bias, upstream):
    _, pull_back = jax.vjp(layer_norm, values, scale_gain, shift_bias)
    return pull_back(upstream)


def gelu_exact(values):
    return jax.nn.gelu(values, approximate=False)


def biased_scores(query, keys, blocks, first_head):
    length, local_heads, head_width = query.shape
    scores = jnp.einsum("qhd,khd->hqk", query, keys, preferred_element_type=F32) * (
        1.0 / math.sqrt(head_width)
    )
    heads_index = (first_head + jnp.arange(local_heads)).astype(F32)
    slopes = 2.0 ** (-8.0 * (heads_index + 1.0) / H)
    places = jnp.arange(length)
    offsets = (places[None, :] - places[:, None]).astype(F32)
    scores = scores + slopes[:, None, None] * offsets[None]
    allowed = blocks[None, :] <= blocks[:, None]
    return jnp.where(allowed[None], scores, -1e30)


def add_rows(dst, src, step):
    rows = dst.shape[0]

    def body(i, carry):
        at = pl.ds(pl.multiple_of(i * step, step), step)
        dst[at, :] = (dst[at, :].astype(F32) + src[at, :].astype(F32)).astype(BF16)
        return carry

    lax.fori_loop(0, rows // step, body, 0)


def remote(src, dst, send, recv, axis, to):
    return pltpu.make_async_remote_copy(
        src_ref=src,
        dst_ref=dst,
        send_sem=send,
        recv_sem=recv,
        device_id={axis: to},
        device_id_type=MESH,
    )


class Chain:
    def __init__(self, n, refs, slack=1):
        self.part, self.outer_in, self.inner_in, self.s_in, self.s_out, self.r_outer, self.r_inner = refs
        i = lax.axis_index("tensor")
        left = i < n // 2
        depth = jnp.where(left, i, n - 1 - i)
        self.inner = jnp.where(left, i + 1, i - 1)
        self.has_outer = depth > 0
        self.outer = jnp.where(self.has_outer, jnp.where(left, i - 1, i + 1), self.inner)
        self.is_mid = depth == n // 2 - 1
        self.lag = slack * (2 * (n // 2 - 1 - depth) + 1)
        self.most_lag = slack * (n - 1)

    @staticmethod
    def scratch(count, block):
        dma = pltpu.SemaphoreType.DMA
        return [pltpu.VMEM((count, *block), BF16)] * 3 + [dma((count,))] * 4

    def to_mid(self, k):
        return remote(
            self.part.at[k], self.inner_in.at[k], self.s_in.at[k], self.r_inner.at[k], "tensor", self.inner
        )

    def to_inner(self, k):
        return remote(
            self.part.at[k], self.outer_in.at[k], self.s_in.at[k], self.r_outer.at[k], "tensor", self.inner
        )

    def to_outer(self, k):
        return remote(
            self.inner_in.at[k], self.inner_in.at[k], self.s_out.at[k], self.r_inner.at[k], "tensor", self.outer
        )

    def greet(self, barrier):
        pl.semaphore_signal(barrier, inc=1, device_id={"tensor": self.inner}, device_id_type=MESH)

        @pl.when(self.has_outer)
        def _():
            pl.semaphore_signal(barrier, inc=1, device_id={"tensor": self.outer}, device_id_type=MESH)

    def wait_greetings(self, barrier, others):
        @pl.when(self.has_outer)
        def _():
            pl.semaphore_wait(barrier, others + 2)

        @pl.when(jnp.logical_not(self.has_outer))
        def _():
            pl.semaphore_wait(barrier, others + 1)

    def reduce(self, k):
        @pl.when(self.has_outer)
        def _():
            self.to_inner(k).wait_recv()
            add_rows(self.part.at[k], self.outer_in.at[k], 16)

        @pl.when(self.is_mid)
        def _():
            self.to_mid(k).start()

        @pl.when(jnp.logical_not(self.is_mid))
        def _():
            self.to_inner(k).start()

    def spread(self, k):
        self.to_mid(k).wait_recv()

        @pl.when(self.is_mid)
        def _():
            add_rows(self.inner_in.at[k], self.part.at[k], 16)

        @pl.when(self.has_outer)
        def _():
            self.to_outer(k).start()

    def drain(self, k):
        self.to_mid(k).wait_send()

        @pl.when(self.has_outer)
        def _():
            self.to_outer(k).wait_send()


def between(k, count):
    return jnp.logical_and(k >= 0, k < count)


ROWS = 32
SLACK = 2
BLOCK_ROWS = 256
TILE = 512


def mlp_kernel(n, length, *refs):
    (att_h, wo_h, src_h, dy_h, wu_h, wd_h, vec_h), refs = refs[:7], refs[7:]
    (tot_h, second_h, activ_h, pre_h, mlp_h, grad_h, bias_h), refs = refs[:7], refs[7:]
    (att, wo, src, dy, wu, wd, vec, second, activ, pre, mlp, grad, bias), refs = refs[:13], refs[13:]
    load, store, tot_store, *refs = refs
    chain = Chain(n, refs, SLACK)
    width = wo.shape[1]
    units = wu.shape[1]
    chunks = length // ROWS
    blocks = length // BLOCK_ROWS
    per_block = BLOCK_ROWS // ROWS
    group = 4

    loads = [
        pltpu.make_async_copy(a, b, load.at[k])
        for k, (a, b) in enumerate(
            ((att_h, att), (wo_h, wo), (vec_h, vec), (src_h, src), (wu_h, wu), (dy_h, dy), (wd_h, wd))
        )
    ]
    for one in loads:
        one.start()
    barrier = pltpu.get_barrier_semaphore()
    chain.greet(barrier)
    bias[...] = jnp.zeros_like(bias)
    chain.wait_greetings(barrier, 0)
    for one in loads[:3]:
        one.wait()

    def tot_copy(k):
        return pltpu.make_async_copy(chain.inner_in.at[k], tot_h.at[k], tot_store.at[k])

    def block_copies(b):
        at = pl.ds(pl.multiple_of(b * BLOCK_ROWS, BLOCK_ROWS), BLOCK_ROWS)
        pairs = ((second, second_h), (activ, activ_h), (pre, pre_h), (mlp, mlp_h), (grad, grad_h))
        return [
            pltpu.make_async_copy(a.at[at], h.at[at], store.at[b, j]) for j, (a, h) in enumerate(pairs)
        ]

    def produce(g):
        rows = group * ROWS
        left = att[pl.ds(pl.multiple_of(g * rows, rows), rows), :]
        for j in range(width // 512):
            cols = pl.ds(j * 512, 512)
            got = jnp.dot(left, wo[:, cols], preferred_element_type=F32).astype(BF16)
            for q in range(group):
                chain.part[g * group + q, :, cols] = got[q * ROWS : (q + 1) * ROWS]

    def normalize(b):
        step = 16

        def body(i, carry):
            at = pl.ds(pl.multiple_of(b * BLOCK_ROWS + i * step, step), step)
            k = b * per_block + i // (ROWS // step)
            inside = pl.ds(pl.multiple_of((i % (ROWS // step)) * step, step), step)
            value = src[at, :].astype(F32) + (chain.inner_in[k, inside, :].astype(F32) + vec[0:1, :width])
            centred = value - jnp.mean(value, axis=-1, keepdims=True)
            var = jnp.mean(centred * centred, axis=-1, keepdims=True)
            second[at, :] = (
                centred * lax.rsqrt(var + EPS) * vec[1:2, :width] + vec[2:3, :width]
            ).astype(BF16)
            return carry

        lax.fori_loop(0, BLOCK_ROWS // step, body, 0)

    def hidden_tile(b, j):
        at = pl.ds(pl.multiple_of(b * BLOCK_ROWS, BLOCK_ROWS), BLOCK_ROWS)
        cols = pl.ds(pl.multiple_of(j * TILE, TILE), TILE)
        value = jnp.dot(second[at, :], wu[:, cols], preferred_element_type=F32) + vec[3:4, cols]
        back = lax.dot_general(
            dy[at, :], wd[cols, :], (((1,), (1,)), ((), ())), preferred_element_type=F32
        )
        below = 0.5 + 0.5 * lax.erf(value * math.sqrt(0.5))
        density = jnp.exp(-0.5 * value * value) * (1.0 / math.sqrt(2.0 * math.pi))
        activ[at, cols] = (value * below).astype(BF16)
        low = (back * (below + value * density)).astype(BF16)
        pre[at, cols] = low
        bias[:, cols] += jnp.sum(low.astype(F32).reshape(BLOCK_ROWS // 8, 8, TILE), axis=0)

    def out_tile(b, j):
        at = pl.ds(pl.multiple_of(b * BLOCK_ROWS, BLOCK_ROWS), BLOCK_ROWS)
        cols = pl.ds(pl.multiple_of(j * TILE, TILE), TILE)
        mlp[at, cols] = jnp.dot(activ[at, :], wd[:, cols], preferred_element_type=F32).astype(BF16)
        grad[at, cols] = lax.dot_general(
            pre[at, :], wu[cols, :], (((1,), (1,)), ((), ())), preferred_element_type=F32
        ).astype(BF16)

    ahead = units // TILE
    steps = ahead + width // TILE
    per_tick = -(-steps // per_block)
    first_tick = per_block + chain.most_lag

    def tick(t, carry):
        @pl.when(jnp.logical_and(t % group == 0, t < chunks))
        def _():
            produce(t // group)

        @pl.when(t < chunks)
        def _():
            chain.reduce(t)

        back = t - chain.lag

        @pl.when(between(back, chunks))
        def _():
            chain.spread(back)
            tot_copy(back).start()

        late = t - first_tick

        @pl.when(late == 0)
        def _():
            for one in loads[3:]:
                one.wait()

        @pl.when(between(late, blocks * per_block))
        def _():
            b = late // per_block
            for q in range(per_tick):
                s = (late % per_block) * per_tick + q

                @pl.when(s == 0)
                def _():
                    normalize(b)

                @pl.when(s < ahead)
                def _():
                    hidden_tile(b, s)

                @pl.when(between(s - ahead, width // TILE))
                def _():
                    out_tile(b, s - ahead)

                @pl.when(s == steps - 1)
                def _():
                    for one in block_copies(b):
                        one.start()

        return carry

    lax.fori_loop(0, chunks + first_tick, tick, 0)
    bias_copy = pltpu.make_async_copy(bias, bias_h, load.at[0])
    bias_copy.start()

    def drain(k, carry):
        chain.drain(k)
        tot_copy(k).wait()
        return carry

    lax.fori_loop(0, chunks, drain, 0)
    for b in range(blocks):
        for one in block_copies(b):
            one.wait()
    bias_copy.wait()


def mlp_call(n, att, wo, src, dy, wu, wd, vec):
    length, width = src.shape
    units = wu.shape[1]
    chunks = length // ROWS
    dma = pltpu.SemaphoreType.DMA
    inputs = (att, wo, src, dy, wu, wd, vec)
    outs = [(chunks, ROWS, width), (length, width), (length, units), (length, units)]
    outs += [(length, width), (length, width)]
    out_shape = [jax.ShapeDtypeStruct(one, BF16) for one in outs] + [jax.ShapeDtypeStruct((8, units), F32)]
    scratch = [pltpu.VMEM(one.shape, one.dtype) for one in inputs]
    scratch += [pltpu.VMEM(one.shape, one.dtype) for one in out_shape[1:]]
    scratch += [dma((7,)), dma((length // BLOCK_ROWS, 5)), dma((chunks,))]
    scratch += Chain.scratch(chunks, (ROWS, width))
    return pl.pallas_call(
        functools.partial(mlp_kernel, n, length),
        out_shape=out_shape,
        in_specs=[pl.BlockSpec(memory_space=pl.ANY)] * len(inputs),
        out_specs=[pl.BlockSpec(memory_space=pl.ANY)] * len(out_shape),
        scratch_shapes=scratch,
        compiler_params=pltpu.CompilerParams(
            collective_id=0, has_side_effects=True, vmem_limit_bytes=60 << 20
        ),
    )(*inputs)


class Ring:
    GONE = 5

    def __init__(self, n, refs, slots):
        self.chain = Chain(n, refs)
        self.slots = slots

    def at(self, k):
        return lax.rem(k, self.slots)

    def reduce(self, k):
        self.chain.reduce(self.at(k))

    def spread(self, k):
        self.chain.spread(self.at(k))

    def retire(self, k):
        self.chain.drain(self.at(k))


class Cube:
    SLOTS = 7
    GONE = 6

    def __init__(self, refs, out, step):
        (self.fin, self.give, self.c0, self.r1, self.r2), refs = refs[:5], refs[5:]
        self.s0, self.q0, self.s1, self.q1, self.s2, self.q2, self.s3, self.q3, self.s4, self.q4, self.kept = refs
        self.out, self.step = out, step
        d = lax.axis_index("dp")
        self.c, self.x, self.y = d % 2, (d // 2) % 2, d // 4
        self.to_c, self.to_x, self.to_y = d + 1 - 2 * self.c, d + 2 - 4 * self.x, d + 4 - 8 * self.y
        self.stages = (self.stage1, self.stage2, self.stage3, self.stage4, self.stage5, self.retire)

    @classmethod
    def scratch(cls, block):
        dma, n = pltpu.SemaphoreType.DMA, cls.SLOTS
        return [
            pltpu.VMEM((n, 2, 2, 2, *block), BF16),
            pltpu.VMEM((n, 2, 2, *block), BF16),
            pltpu.VMEM((n, 2, 2, *block), BF16),
            pltpu.VMEM((n, 2, *block), BF16),
            pltpu.VMEM((n, 2, *block), BF16),
            *[dma((n,))] * 2,
            *[dma((n, 2))] * 6,
            *[dma((n,))] * 3,
        ]

    def greet(self, barrier):
        for to in (self.to_c, self.to_x, self.to_y):
            pl.semaphore_signal(barrier, inc=1, device_id={"dp": to}, device_id_type=MESH)

    def slot(self, k):
        return lax.rem(k, self.SLOTS)

    def half(self, k):
        p = self.slot(k)
        return remote(self.give.at[p], self.c0.at[p], self.s0.at[p], self.q0.at[p], "dp", self.to_c)

    def quarters(self, p):
        return self.fin.at[p, self.c, 0, self.x], self.fin.at[p, self.c, 1, self.y]

    def hop1(self, k):
        p, fin, c = self.slot(k), self.fin, self.c
        return (
            remote(fin.at[p, c, 0, 1 - self.x], self.r1.at[p, 0], self.s1.at[p, 0], self.q1.at[p, 0], "dp", self.to_x),
            remote(fin.at[p, c, 1, 1 - self.y], self.r1.at[p, 1], self.s1.at[p, 1], self.q1.at[p, 1], "dp", self.to_y),
        )

    def hop2(self, k):
        p = self.slot(k)
        a, b = self.quarters(p)
        return (
            remote(a, self.r2.at[p, 0], self.s2.at[p, 0], self.q2.at[p, 0], "dp", self.to_y),
            remote(b, self.r2.at[p, 1], self.s2.at[p, 1], self.q2.at[p, 1], "dp", self.to_x),
        )

    def hop3(self, k):
        p = self.slot(k)
        a, b = self.quarters(p)
        return (
            remote(a, a, self.s3.at[p, 0], self.q3.at[p, 0], "dp", self.to_x),
            remote(b, b, self.s3.at[p, 1], self.q3.at[p, 1], "dp", self.to_y),
        )

    def hop4(self, k):
        p = self.slot(k)
        mine = self.fin.at[p, self.c]
        return remote(mine, mine, self.s4.at[p], self.q4.at[p], "dp", self.to_c)

    def keep(self, k):
        p = self.slot(k)
        return pltpu.make_async_copy(self.fin.at[p], self.out.at[k], self.kept.at[p])

    def add_quarters(self, k, got):
        p = self.slot(k)
        for j, quarter in enumerate(self.quarters(p)):
            add_rows(quarter, got.at[p, j], self.step)

    def stage1(self, k):
        self.half(k).wait()
        p = self.slot(k)
        for a in range(2):
            for b in range(2):
                add_rows(self.fin.at[p, self.c, a, b], self.c0.at[p, a, b], self.step)
        for one in self.hop1(k):
            one.start()

    def stage2(self, k):
        for one in self.hop1(k):
            one.wait()
        self.add_quarters(k, self.r1)
        for one in self.hop2(k):
            one.start()

    def stage3(self, k):
        for one in self.hop2(k):
            one.wait()
        self.add_quarters(k, self.r2)
        for one in self.hop3(k):
            one.start()

    def stage4(self, k):
        for one in self.hop3(k):
            one.wait_recv()
        self.hop4(k).start()

    def stage5(self, k):
        self.hop4(k).wait_recv()
        self.keep(k).start()

    def retire(self, k):
        for one in self.hop3(k) + (self.hop4(k),):
            one.wait_send()
        self.keep(k).wait()

    def tick(self, t, count):
        for late, stage in reversed(tuple(enumerate(self.stages, 1))):
            k = t - late

            @pl.when(between(k, count))
            def _(stage=stage, k=k):
                stage(k)


def weighted(left, right):
    return lax.dot_general(left, right, (((0,), (0,)), ((), ())), preferred_element_type=F32).astype(BF16)


def lane_half(odd):
    return (lax.broadcasted_iota(jnp.int32, (1, 2 * HD), 1) // HD == odd).astype(F32)


def head_backward(head, q, k, v, up, lse, slope, off, tile, grads, acc):
    q_grad, k_grad, v_grad = grads
    k_acc, v_acc = acc
    length = q.shape[0]
    odd = lax.rem(head, 2)
    mask = lane_half(odd).astype(BF16)
    lanes = pl.ds(pl.multiple_of((head // 2) * 2 * HD, 2 * HD), 2 * HD)
    scale = 1.0 / math.sqrt(HD)
    gain = slope[pl.ds(head, 1), 0:1]
    nt = (((1,), (1,)), ((), ()))
    for j in range(length // tile):
        rows = slice(j * tile, (j + 1) * tile)
        most = min(length, (j + 2) * tile)
        q_here = q[rows, lanes]
        up_here = up[rows, lanes] * mask
        k_here = k[0:most, lanes] * mask
        scores = lax.dot_general(k_here, q_here, nt, preferred_element_type=F32)
        probs = jnp.exp(scores * scale + gain * off[0:most, rows] - lse[pl.ds(head, 1), rows])
        back = lax.dot_general(v[0:most, lanes], up_here, nt, preferred_element_type=F32)
        delta = jnp.sum(probs * back, axis=0, keepdims=True)
        score_grad = (probs * (back - delta)).astype(BF16)
        v_part = jnp.dot(probs.astype(BF16), up_here, preferred_element_type=F32)
        k_part = jnp.dot(score_grad, q_here * mask, preferred_element_type=F32)
        if j == 0:
            v_acc[0:most, :] = v_part
            k_acc[0:most, :] = k_part
            if most < length:
                v_acc[most:length, :] = jnp.zeros((length - most, 2 * HD), F32)
                k_acc[most:length, :] = jnp.zeros((length - most, 2 * HD), F32)
        else:
            v_acc[0:most, :] += v_part
            k_acc[0:most, :] += k_part
        q_part = lax.dot_general(k_here, score_grad, (((0,), (0,)), ((), ())), preferred_element_type=F32)
        mine = (q_part.T * scale).astype(BF16)

        @pl.when(odd == 0)
        def _(rows=rows, mine=mine):
            q_grad[rows, lanes] = mine

        @pl.when(odd == 1)
        def _(rows=rows, mine=mine):
            q_grad[rows, lanes] += mine

    for to, got, factor in ((k_grad, k_acc, scale), (v_grad, v_acc, 1.0)):

        @pl.when(odd == 0)
        def _(to=to, got=got, factor=factor):
            to[:, lanes] = (got[...] * factor).astype(BF16)

        @pl.when(odd == 1)
        def _(to=to, got=got, factor=factor):
            to[:, lanes] += (got[...] * factor).astype(BF16)


BACK_ROWS = 96
HEAD_TILE = 256


def back_kernel(n, heads, *refs):
    (grad_h, mlp_h, activ_h, dy_h, second_h, pre_h, src_h, tot_h), refs = refs[:8], refs[8:]
    smalls_h, refs = refs[:8], refs[8:]
    (sum_h, g_out, resid_h, qg_h, kg_h, vg_h, cols_h), refs = refs[:7], refs[7:]
    (left, dy, pre, src, tot, resid), refs = refs[:6], refs[6:]
    smalls, refs = refs[:8], refs[8:]
    vec, wo, q, k, v, lse, slope, off = smalls
    (up, qg, kg, vg, k_acc, v_acc, cols), refs = refs[:7], refs[7:]
    (load, left_sem, part_sem, row_sem, resid_sem, sum_sem), refs = refs[:6], refs[6:]
    slots = 8
    ring, refs = Ring(n, refs[:7], slots), refs[7:]
    chain = ring.chain
    cube = Cube(refs, g_out, 32)
    width, units = dy.shape[1], pre.shape[1]
    rows, per_sum = BACK_ROWS, grad_h.shape[0]
    total_z = 2 * per_sum
    piece = 256
    first = activ_h.shape[1] // piece
    total_p = first + second_h.shape[1] // piece

    loads = [pltpu.make_async_copy(a, b, load.at[j]) for j, (a, b) in enumerate(zip(smalls_h, smalls))]
    loads += [pltpu.make_async_copy(dy_h, dy, load.at[8]), pltpu.make_async_copy(pre_h, pre, load.at[9])]

    def part_load(j, which):
        return pltpu.make_async_copy(
            (grad_h, mlp_h)[which].at[lax.rem(j, per_sum)], chain.part.at[ring.at(j)], part_sem.at[ring.at(j)]
        )

    def part_start(j):
        @pl.when(j < per_sum)
        def _():
            part_load(j, 0).start()

        @pl.when(between(j - per_sum, per_sum))
        def _():
            part_load(j, 1).start()

    def left_load(p, which):
        at = (p - which * first) * piece
        return pltpu.make_async_copy(
            (activ_h, second_h)[which].at[:, pl.ds(pl.multiple_of(at, piece), piece)],
            left.at[lax.rem(p, 2)],
            left_sem.at[lax.rem(p, 2)],
        )

    def left_start(p):
        @pl.when(p < first)
        def _():
            left_load(p, 0).start()

        @pl.when(between(p - first, total_p - first))
        def _():
            left_load(p, 1).start()

    def row_loads(j):
        at = lax.rem(j, 2)
        return (
            pltpu.make_async_copy(src_h.at[j], src.at[at], row_sem.at[at, 0]),
            pltpu.make_async_copy(tot_h.at[j], tot.at[at], row_sem.at[at, 1]),
        )

    def resid_store(j):
        at = lax.rem(j, 2)
        return pltpu.make_async_copy(resid.at[at], resid_h.at[j], resid_sem.at[at])

    def sum_store(j):
        at = ring.at(j)
        return pltpu.make_async_copy(chain.inner_in.at[at], sum_h.at[j - per_sum], sum_sem.at[at])

    part_start(0)
    part_start(1)
    left_start(0)
    loads[8].start()
    for one in loads[:8] + loads[9:]:
        one.start()
    barrier = pltpu.get_barrier_semaphore()
    chain.greet(barrier)
    cube.greet(barrier)
    cols[...] = jnp.zeros_like(cols)
    chain.wait_greetings(barrier, 3)
    for one in loads:
        one.wait()

    def produce(p):
        at = lax.rem(p, 2)
        to = cube.slot(p)
        pltpu.make_async_copy(activ_h.at[:, pl.ds(0, piece)], left.at[at], left_sem.at[at]).wait()
        mine, theirs = cube.c, 1 - cube.c
        count = piece // 8

        def product(right):
            for side, store in ((theirs, cube.give.at[to]), (mine, cube.fin.at[to, cube.c])):
                rows_of = left[at, :, pl.ds(pl.multiple_of(side * (piece // 2), piece // 2), piece // 2)]
                for j in range(right.shape[1] // 512):
                    here = pl.ds(j * 512, 512)
                    got = weighted(rows_of, right[:, here])
                    for a in range(2):
                        for b in range(2):
                            lo = (2 * a + b) * count
                            store[a, b, :, here] = got[lo : lo + count]

        @pl.when(p < first)
        def _():
            product(dy)

        @pl.when(p >= first)
        def _():
            product(pre)

        cube.half(p).start()

    def row_sum(x):
        return jnp.sum(x, axis=-1, keepdims=True)

    def rows_back(j):
        for one in row_loads(j):
            one.wait()
        at, got = lax.rem(j, 2), ring.at(j)
        step = 16

        def body(i, carry):
            here = pl.ds(pl.multiple_of(i * step, step), step)
            value = src[at, here, :].astype(F32) + (tot[at, here, :].astype(F32) + vec[0:1, :])
            centred = value - row_sum(value) / width
            spread = lax.rsqrt(row_sum(centred * centred) / width + EPS)
            normal = centred * spread
            down = chain.inner_in[got, here, :].astype(F32)
            scaled = down * vec[1:2, :]
            flat, slope_of = row_sum(scaled) / width, row_sum(scaled * normal) / width
            back = spread * (scaled - flat - normal * slope_of)
            all_rows = pl.ds(pl.multiple_of(j * rows + i * step, step), step)
            low = (back + dy[all_rows, :].astype(F32)).astype(BF16)
            resid[at, here, :] = low
            for c, item in enumerate((down * normal, down, low.astype(F32))):
                cols[c] += item[0:8] + item[8:16]
            return carry

        lax.fori_loop(0, rows // step, body, 0)
        all_rows = pl.ds(pl.multiple_of(j * rows, rows), rows)
        up[all_rows, :] = lax.dot_general(
            resid[at], wo[...], (((1,), (1,)), ((), ())), preferred_element_type=F32
        ).astype(BF16)
        resid_store(j).start()

    def tick(t, carry):
        gone = t - Ring.GONE

        @pl.when(between(gone, total_z))
        def _():
            ring.retire(gone)

            @pl.when(gone >= per_sum)
            def _():
                sum_store(gone).wait()

        part_start(t + 2)

        @pl.when(t < total_z)
        def _():
            part_load(t, 0).wait()
            ring.reduce(t)

        back = t - chain.lag

        @pl.when(between(back, total_z))
        def _():
            ring.spread(back)

            @pl.when(back >= per_sum)
            def _():
                sum_store(back).start()

        cube.tick(t, total_p)

        @pl.when(t < total_p)
        def _():
            left_start(t + 1)
            produce(t)

        chunk = t - 4

        @pl.when(between(chunk + 1, per_sum))
        def _():
            for one in row_loads(chunk + 1):
                one.start()

        @pl.when(between(chunk - 2, per_sum))
        def _():
            resid_store(chunk - 2).wait()

        @pl.when(between(chunk, per_sum))
        def _():
            rows_back(chunk)

        head = t - 4 - per_sum

        @pl.when(between(head, heads))
        def _():
            head_backward(head, q, k, v, up, lse, slope, off, HEAD_TILE, (qg, kg, vg), (k_acc, v_acc))

        return carry

    ticks = max(total_z + Ring.GONE, total_p + Cube.GONE, 4 + per_sum + max(heads, 2))
    lax.fori_loop(0, ticks, tick, 0)
    stores = [
        pltpu.make_async_copy(a, b, load.at[j])
        for j, (a, b) in enumerate(((qg, qg_h), (kg, kg_h), (vg, vg_h), (cols, cols_h)))
    ]
    for one in stores:
        one.start()
    for one in stores:
        one.wait()


def back_call(n, grad, mlp, activ, dy, second, pre, src, tot, vec, wo, q, k, v, lse, slope, off):
    length, width = dy.shape
    chunks = length // BACK_ROWS
    dma = pltpu.SemaphoreType.DMA

    def cut(one):
        return one.reshape(chunks, BACK_ROWS, one.shape[-1])

    smalls = (vec, wo, q, k, v, lse, slope, off)
    inputs = (cut(grad), cut(mlp), activ, dy, second, pre, cut(src), cut(tot), *smalls)
    pieces = (activ.shape[1] + second.shape[1]) // 256
    shapes = [
        ((chunks, BACK_ROWS, width), BF16),
        ((pieces, 2, 2, 2, 32, width), BF16),
        ((chunks, BACK_ROWS, width), BF16),
        *[(q.shape, BF16)] * 3,
        ((3, 8, width), F32),
    ]
    slots = 8
    scratch = [
        pltpu.VMEM((2, length, 256), BF16),
        pltpu.VMEM(dy.shape, BF16),
        pltpu.VMEM(pre.shape, BF16),
        *[pltpu.VMEM((2, BACK_ROWS, width), BF16)] * 3,
        *[pltpu.VMEM(one.shape, one.dtype) for one in smalls],
        *[pltpu.VMEM(q.shape, BF16)] * 4,
        *[pltpu.VMEM((length, 2 * HD), F32)] * 2,
        pltpu.VMEM((3, 8, width), F32),
        dma((10,)),
        dma((2,)),
        dma((slots,)),
        dma((2, 2)),
        dma((2,)),
        dma((slots,)),
        *Chain.scratch(slots, (BACK_ROWS, width)),
        *Cube.scratch((32, width)),
    ]
    return pl.pallas_call(
        functools.partial(back_kernel, n, q.shape[1] // HD),
        out_shape=[jax.ShapeDtypeStruct(*one) for one in shapes],
        in_specs=[pl.BlockSpec(memory_space=pl.ANY)] * len(inputs),
        out_specs=[pl.BlockSpec(memory_space=pl.ANY)] * len(shapes),
        scratch_shapes=scratch,
        compiler_params=pltpu.CompilerParams(
            collective_id=1, has_side_effects=True, vmem_limit_bytes=60 << 20
        ),
    )(*inputs)


def sums_kernel(n, n_z, n_dp, chunks, pieces, *refs):
    z_in, refs = refs[:n_z], refs[n_z:]
    g_in, refs = refs[:n_dp], refs[n_dp:]
    z_out, g_out, load_sem, store_sem, *refs = refs
    chain, refs = Chain(n, refs[:7]), refs[7:]
    fin, c0, r1, r2, gl, c0s, c0r, s1, q1, s2, q2, s3, q3, s4, q4, gstore = refs

    total_z = sum(chunks)
    total_p = sum(pieces)
    d = lax.axis_index("dp")
    c, x, y = d % 2, (d // 2) % 2, d // 4
    to_c, to_x, to_y = d + 1 - 2 * c, d + 2 - 4 * x, d + 4 - 8 * y

    def z_load(j, at):
        return pltpu.make_async_copy(z_in[j], chain.part.at[pl.ds(at, chunks[j])], load_sem.at[j])

    def g_load(j, at):
        return pltpu.make_async_copy(g_in[j].at[:, c], fin.at[pl.ds(at, pieces[j]), c], gl.at[j])

    z_at = [sum(chunks[:k]) for k in range(n_z)]
    p_at = [sum(pieces[:k]) for k in range(n_dp)]
    for j in range(n_z):
        z_load(j, z_at[j]).start()
    for j in range(n_dp):
        g_load(j, p_at[j]).start()

    barrier = pltpu.get_barrier_semaphore()
    chain.greet(barrier)
    for to in (to_c, to_x, to_y):
        pl.semaphore_signal(barrier, inc=1, device_id={"dp": to}, device_id_type=MESH)
    chain.wait_greetings(barrier, 3)

    def store(k):
        return pltpu.make_async_copy(chain.inner_in.at[k], z_out.at[k], store_sem.at[k])

    def core_half(k, j, at):
        return remote(g_in[j].at[k - at, 1 - c], c0.at[k], c0s.at[k], c0r.at[k], "dp", to_c)

    def hop1(k):
        return (
            remote(fin.at[k, c, 0, 1 - x], r1.at[k, 0], s1.at[k, 0], q1.at[k, 0], "dp", to_x),
            remote(fin.at[k, c, 1, 1 - y], r1.at[k, 1], s1.at[k, 1], q1.at[k, 1], "dp", to_y),
        )

    def hop2(k):
        return (
            remote(fin.at[k, c, 0, x], r2.at[k, 0], s2.at[k, 0], q2.at[k, 0], "dp", to_y),
            remote(fin.at[k, c, 1, y], r2.at[k, 1], s2.at[k, 1], q2.at[k, 1], "dp", to_x),
        )

    def hop3(k):
        return (
            remote(fin.at[k, c, 0, x], fin.at[k, c, 0, x], s3.at[k, 0], q3.at[k, 0], "dp", to_x),
            remote(fin.at[k, c, 1, y], fin.at[k, c, 1, y], s3.at[k, 1], q3.at[k, 1], "dp", to_y),
        )

    def hop4(k):
        return remote(fin.at[k, c], fin.at[k, c], s4.at[k], q4.at[k], "dp", to_c)

    def g_store(k):
        return pltpu.make_async_copy(fin.at[k], g_out.at[k], gstore.at[k])

    for j in range(n_dp):

        def send_half(k, carry, j=j):
            core_half(k + p_at[j], j, p_at[j]).start()
            return carry

        lax.fori_loop(0, pieces[j], send_half, 0)

    step = 32 if r1.shape[2] % 32 == 0 else 16

    def stage1(k):
        for j in range(n_dp):

            @pl.when(k == p_at[j])
            def _(j=j):
                g_load(j, p_at[j]).wait()

        core_half(k, 0, k).wait_recv()
        for a in range(2):
            for b in range(2):
                add_rows(fin.at[k, c, a, b], c0.at[k, a, b], step)
        for one in hop1(k):
            one.start()

    def stage2(k):
        for one in hop1(k):
            one.wait()
        add_rows(fin.at[k, c, 0, x], r1.at[k, 0], step)
        add_rows(fin.at[k, c, 1, y], r1.at[k, 1], step)
        for one in hop2(k):
            one.start()

    def stage3(k):
        for one in hop2(k):
            one.wait()
        add_rows(fin.at[k, c, 0, x], r2.at[k, 0], step)
        add_rows(fin.at[k, c, 1, y], r2.at[k, 1], step)
        for one in hop3(k):
            one.start()

    def stage4(k):
        for one in hop3(k):
            one.wait_recv()
        hop4(k).start()

    def stage5(k):
        hop4(k).wait_recv()
        g_store(k).start()

    def tick(t, carry):
        @pl.when(t < total_z)
        def _():
            for j in range(n_z):

                @pl.when(t == z_at[j])
                def _(j=j):
                    z_load(j, z_at[j]).wait()

            chain.reduce(t)

        back = t - chain.lag

        @pl.when(between(back, total_z))
        def _():
            chain.spread(back)
            store(back).start()

        for late, stage in enumerate((stage1, stage2, stage3, stage4, stage5)):
            k = t - late

            @pl.when(between(k, total_p))
            def _(stage=stage, k=k):
                stage(k)

        return carry

    lax.fori_loop(0, max(total_z + chain.most_lag, total_p + 4), tick, 0)

    def drain_z(k, carry):
        chain.drain(k)
        store(k).wait()
        return carry

    lax.fori_loop(0, total_z, drain_z, 0)

    def drain_g(k, carry):
        core_half(k, 0, k).wait_send()
        for one in hop3(k) + (hop4(k),):
            one.wait_send()
        g_store(k).wait()
        return carry

    lax.fori_loop(0, total_p, drain_g, 0)


def device_sums(n, z_parts, g_parts, collective_id):
    chunks = tuple(one.shape[0] for one in z_parts)
    pieces = tuple(one.shape[0] for one in g_parts)
    nz, npc = sum(chunks), sum(pieces)
    z_block = z_parts[0].shape[1:]
    g_block = g_parts[0].shape[4:]
    dma = pltpu.SemaphoreType.DMA
    scratch = [dma((len(chunks),)), dma((nz,))] + Chain.scratch(nz, z_block)
    scratch += [
        pltpu.VMEM((npc, 2, 2, 2, *g_block), BF16),
        pltpu.VMEM((npc, 2, 2, *g_block), BF16),
        pltpu.VMEM((npc, 2, *g_block), BF16),
        pltpu.VMEM((npc, 2, *g_block), BF16),
        dma((len(pieces),)),
        dma((npc,)),
        dma((npc,)),
    ]
    scratch += [dma((npc, 2))] * 6 + [dma((npc,))] * 3
    out_shape = [
        jax.ShapeDtypeStruct((nz, *z_block), BF16),
        jax.ShapeDtypeStruct((npc, 2, 2, 2, *g_block), BF16),
    ]
    vmem = 2 * (3 * nz * math.prod(z_block) + 16 * npc * math.prod(g_block))
    return pl.pallas_call(
        functools.partial(sums_kernel, n, len(z_parts), len(g_parts), chunks, pieces),
        out_shape=out_shape,
        in_specs=[pl.BlockSpec(memory_space=pl.ANY)] * (len(z_parts) + len(g_parts)),
        out_specs=[pl.BlockSpec(memory_space=pl.ANY)] * len(out_shape),
        scratch_shapes=scratch,
        compiler_params=pltpu.CompilerParams(
            collective_id=collective_id, has_side_effects=True, vmem_limit_bytes=vmem + (2 << 20)
        ),
    )(*z_parts, *g_parts)


def on_device(
    fast,
    n_tensor,
    inputs,
    block_ids,
    first_gain,
    first_shift,
    mixing_weight,
    mixing_bias,
    output_weight,
    output_bias,
    second_gain,
    second_shift,
    expand_weight,
    expand_bias,
    shrink_weight,
    shrink_bias,
    cotangent,
):
    source = inputs.astype(F32)
    upstream = cotangent.astype(F32)
    length, width = source.shape
    blocks = block_ids[0]
    local_width = mixing_weight.shape[2]
    local_heads = local_width // HD
    units = expand_weight.shape[1]
    first_head = lax.axis_index("tensor") * local_heads
    rows = 96

    def sums(z_parts, g_parts, collective_id):
        if not fast:
            return (
                [lax.psum(one.astype(BF16), "tensor").astype(F32) for one in z_parts],
                [lax.psum(one, "dp") for one in g_parts],
            )
        z_low = [one.astype(BF16).reshape(length // rows, rows, width) for one in z_parts]
        out = device_sums(n_tensor, z_low, [one.astype(BF16) for one in g_parts], collective_id)
        z_all = out[0].reshape(len(z_parts), length, width)
        z_out = [z_all[k].astype(F32) for k in range(len(z_parts))]
        g_out, at = [], 0
        for one in g_parts:
            g_out.append(out[1][at : at + one.shape[0]].astype(F32))
            at += one.shape[0]
        return z_out, g_out

    weights = mixing_weight.transpose(1, 0, 2)
    normed_low = layer_norm(source, first_gain, first_shift).astype(BF16)

    def project(k):
        return jnp.dot(normed_low, weights[k], preferred_element_type=F32)

    query = (project(0) + mixing_bias[0]).astype(BF16).reshape(length, local_heads, HD)
    keys = project(1).astype(BF16).reshape(length, local_heads, HD)
    vals = (project(2) + mixing_bias[1]).astype(BF16).reshape(length, local_heads, HD)
    masked = biased_scores(query, keys, blocks, first_head)
    row_top = jnp.max(masked, axis=-1, keepdims=True)
    logsum = row_top + jnp.log(jnp.sum(jnp.exp(masked - row_top), axis=-1, keepdims=True))
    probs_low = jnp.exp(masked - logsum).astype(BF16)
    attended = (
        jnp.einsum("hqk,khd->qhd", probs_low, vals, preferred_element_type=F32)
        .reshape(length, local_width)
        .astype(BF16)
    )
    if fast:
        most = max(width, units)
        vectors = jnp.stack(
            [
                jnp.pad(one, (0, most - one.shape[0]))
                for one in (output_bias, second_gain, second_shift, expand_bias)
            ]
        )
        total, second_low, activ_low, pre_grad, partial_mlp, second_part, expand_bias_part = mlp_call(
            n_tensor, attended, output_weight, inputs, cotangent, expand_weight, shrink_weight, vectors
        )
        expand_bias_part = jnp.sum(expand_bias_part, axis=0)
        hidden_state = source + (total.reshape(length, width).astype(F32) + output_bias)
    else:
        partial_out = jnp.dot(attended, output_weight, preferred_element_type=F32)
        resid = lax.psum(partial_out.astype(BF16), "tensor").astype(F32)
        hidden_state = source + (resid + output_bias)
        second_low = layer_norm(hidden_state, second_gain, second_shift).astype(BF16)
        pre_act = jnp.dot(second_low, expand_weight, preferred_element_type=F32) + expand_bias
        activ_low = gelu_exact(pre_act).astype(BF16)
        partial_mlp = jnp.dot(activ_low, shrink_weight, preferred_element_type=F32)
        act_grad = jnp.einsum("td,fd->tf", cotangent, shrink_weight, preferred_element_type=F32)
        _, gelu_pull = jax.vjp(gelu_exact, pre_act)
        pre_grad = gelu_pull(act_grad)[0].astype(BF16)
        expand_bias_part = jnp.sum(pre_grad.astype(F32), axis=0)
        second_part = jnp.einsum("tf,df->td", pre_grad, expand_weight, preferred_element_type=F32)
    shrink_bias_part = jnp.sum(upstream, axis=0)
    if fast:
        places = jnp.arange(length)
        off = jnp.where(
            blocks[:, None] <= blocks[None, :], (places[:, None] - places[None, :]).astype(F32), -1e30
        )
        numbers = (first_head + jnp.arange(local_heads)).astype(F32)
        slope = jnp.broadcast_to((2.0 ** (-8.0 * (numbers + 1.0) / H))[:, None], (local_heads, 128))
        flat = [one.reshape(length, local_width) for one in (query, keys, vals)]
        mlp_sum, weight_sums, resid_low, query_grad, keys_grad, vals_grad, sums_back = back_call(
            n_tensor, second_part, partial_mlp, activ_low, cotangent, second_low, pre_grad, inputs, total,
            vectors[:, :width], output_weight, *flat, logsum.reshape(local_heads, length), slope, off,
        )
        mlp_sum = mlp_sum.reshape(length, width).astype(F32)
        resid_low = resid_low.reshape(length, width)
        hidden_grad = resid_low.astype(F32)
        second_gain_part, second_shift_part, output_bias_part = (
            jnp.sum(sums_back[k], axis=0) for k in range(3)
        )
        pieces = units // 256
        shrink_weight_grad = weight_sums[:pieces].astype(F32).reshape(units, width)
        expand_weight_grad = weight_sums[pieces:].astype(F32).reshape(width, units)
        outputs = (hidden_state + mlp_sum + shrink_bias).astype(BF16)
        output_part = jnp.einsum("tc,td->cd", attended, resid_low, preferred_element_type=F32)
    else:
        shrink_part = jnp.einsum("tf,td->fd", activ_low, cotangent, preferred_element_type=F32)
        expand_part = jnp.einsum("td,tf->df", second_low, pre_grad, preferred_element_type=F32)

        (second_grad, mlp_sum), (shrink_sum, expand_sum) = sums(
            [second_part, partial_mlp],
            [
                shrink_part.reshape(-1, 2, 2, 2, 32, width),
                expand_part.reshape(-1, 2, 2, 2, 32, units),
            ],
            1,
        )
        shrink_weight_grad = shrink_sum.reshape(units, width)
        expand_weight_grad = expand_sum.reshape(width, units)
        outputs = (hidden_state + mlp_sum + shrink_bias).astype(BF16)
        hidden_grad, second_gain_part, second_shift_part = norm_backward(
            hidden_state, second_gain, second_shift, second_grad
        )
        hidden_grad = hidden_grad + upstream
        resid_low = hidden_grad.astype(BF16)
        output_part = jnp.einsum("tc,td->cd", attended, resid_low, preferred_element_type=F32)
        output_bias_part = jnp.sum(resid_low.astype(F32), axis=0)
        attended_grad = (
            jnp.einsum("td,cd->tc", resid_low, output_weight, preferred_element_type=F32)
            .astype(BF16)
            .reshape(length, local_heads, HD)
        )
        probs = jnp.exp(biased_scores(query, keys, blocks, first_head) - logsum)
        probs_low = probs.astype(BF16)
        prob_grad = jnp.einsum("qhd,khd->hqk", attended_grad, vals, preferred_element_type=F32)
        vals_grad = jnp.einsum(
            "hqk,qhd->khd", probs_low, attended_grad, preferred_element_type=F32
        ).astype(BF16)
        row_delta = jnp.sum(probs * prob_grad, axis=-1, keepdims=True)
        score_grad = (probs * (prob_grad - row_delta)).astype(BF16)
        scale_factor = 1.0 / math.sqrt(HD)
        query_grad = (
            jnp.einsum("hqk,khd->qhd", score_grad, keys, preferred_element_type=F32) * scale_factor
        ).astype(BF16)
        keys_grad = (
            jnp.einsum("hqk,qhd->khd", score_grad, query, preferred_element_type=F32) * scale_factor
        ).astype(BF16)
    grads = [one.reshape(length, local_width) for one in (query_grad, keys_grad, vals_grad)]
    mixing_part = jnp.stack(
        [jnp.einsum("td,tc->dc", normed_low, one, preferred_element_type=F32) for one in grads]
    )
    mixing_bias_part = jnp.stack(
        [jnp.sum(grads[0].astype(F32), axis=0), jnp.sum(grads[2].astype(F32), axis=0)]
    )
    normed_part = sum(
        jnp.einsum("tc,dc->td", one, weights[k], preferred_element_type=F32)
        for k, one in enumerate(grads)
    )
    quarters = width // local_width
    (normed_grad,), (mixing_sum, output_sum) = sums(
        [normed_part],
        [
            mixing_part.reshape(-1, 2, 2, 2, 128, local_width),
            output_part.reshape(local_width, quarters, local_width)
            .transpose(1, 0, 2)
            .reshape(-1, 2, 2, 2, 128, local_width),
        ],
        2,
    )
    mixing_weight_grad = mixing_sum.reshape(3, width, local_width).transpose(1, 0, 2)
    output_weight_grad = (
        output_sum.reshape(quarters, local_width, local_width)
        .transpose(1, 0, 2)
        .reshape(local_width, width)
    )
    source_grad, first_gain_part, first_shift_part = norm_backward(
        source, first_gain, first_shift, normed_grad
    )
    input_grad = (source_grad + hidden_grad).astype(BF16)
    small = lax.psum(
        (
            first_gain_part,
            first_shift_part,
            mixing_bias_part,
            output_bias_part,
            second_gain_part,
            second_shift_part,
            expand_bias_part,
            shrink_bias_part,
        ),
        "dp",
    )
    return (
        outputs,
        input_grad,
        small[0],
        small[1],
        mixing_weight_grad,
        small[2],
        output_weight_grad,
        small[3],
        small[4],
        small[5],
        expand_weight_grad,
        small[6],
        shrink_weight_grad,
        small[7],
    )


def solution(mesh):
    in_specs = (
        P("dp", None),
        P("dp", None),
        P(),
        P(),
        P(None, None, "tensor"),
        P(None, "tensor"),
        P("tensor", None),
        P(),
        P(),
        P(),
        P(None, "tensor"),
        P("tensor"),
        P("tensor", None),
        P(),
        P("dp", None),
    )
    out_specs = (
        P("dp", None),
        P("dp", None),
        P(),
        P(),
        P(None, None, "tensor"),
        P(None, "tensor"),
        P("tensor", None),
        P(),
        P(),
        P(),
        P(None, "tensor"),
        P("tensor"),
        P("tensor", None),
        P(),
    )
    n_tensor = mesh.shape["tensor"]
    fast = mesh.shape["dp"] == 8 and n_tensor % 2 == 0
    return jax.shard_map(
        functools.partial(on_device, fast, n_tensor),
        mesh=mesh,
        in_specs=in_specs,
        out_specs=out_specs,
        check_vma=False,
    )
```

time: 1620 us -> 537 us (0.33)
  waiting for transfers between devices: 1270 us -> 0 us
  Pallas kernels: 0 us -> 377 us
  matrix products: 169 us -> 45.3 us
  local copies, waits for them, and re-layouts: 55.2 us -> 23.7 us
    psum x5 -> x0, waiting for transfers between devices: 1270 us -> none  [the longest x1 543 us: on_device(): lax.psum((first_gain_grad, first_shift_grad, mixing_weight_grad, mixing_b...]
    pallas_call x0 -> x3, Pallas kernels: none -> 377 us  [the longest x1 174 us: back_call(): pl.pallas_call(functools.partial(back_kernel, n, q.shape[1] // HD), out_s...]
    dot_general x18 -> x12, matrix products: 169 us -> 45.3 us  [the longest x3 10.8 us: on_device(): jnp.einsum('tc,dc->td', one, weights[k], preferred_element_type=F32)]
    unnamed x115 -> x62, local copies, waits for them, and re-layouts: 53 us -> 0.54 us
  transfers between devices with their start and end apart: 5 -> 0, of which waited for: 5 -> 0; matrix products, arithmetic and copies ran while one was open for 5% -> 0% of each run, Pallas kernels for 0% -> 0%
where the time goes in v2:
time: 537 us; the launch traced here: 533 us
  Pallas kernels  377 us (70%)
  other arithmetic  59.7 us (11%)
  matrix products  45.3 us (8%)
  blocking collectives  25.2 us (5%)
  local copies, waits for them, and re-layouts  23.7 us (4%)
    pallas_call x1, Pallas kernels, back_call(): pl.pallas_call(functools.partial(back_kernel, n, q.shape[1] // HD), out_s...  174 us
    pallas_call x1, Pallas kernels, mlp_call(): pl.pallas_call(functools.partial(mlp_kernel, n, length), out_shape=out_sh...  106 us
    pallas_call x1, Pallas kernels, device_sums(): pl.pallas_call(functools.partial(sums_kernel, n, len(z_parts), len(g_part...  97.1 us
    psum x1, blocking collectives, on_device(): lax.psum((first_gain_part, first_shift_part, mixing_bias_part, output_bia...  25.2 us
    reshape x1, other arithmetic, on_device(): shrink_weight_grad = weight_sums[:pieces].astype(F32).reshape(units, width)  12.6 us
    dot_general x3, matrix products, on_device(): jnp.einsum('tc,dc->td', one, weights[k], preferred_element_type=F32)  10.8 us

profile of v2, /device:TPU:0, one launch (start us, length us, event | category | flops | bytes accessed | tf_op | source)
XLA Modules:
  0.0 532.9 jit_solution(9415930111946711214)
XLA Ops:
  0.7 0.7 reduce.4
  1.4 0.7 broadcast_in_dim.24.refs_14_
  2.1 2.6 convert_reduce_fusion
  4.8 3.0 fusion.11
  7.8 0.5 convert_reduce_fusion.2
  8.4 0.6 pad_maximum_fusion.1.refs_6_.refs_8_
  9.0 1.2 broadcast_compare_fusion
  10.2 2.6 copy.42
  12.8 1.8 convert_select_fusion.refs_15_
  14.6 1.6 subtract_convert_fusion
  16.3 1.2 fusion.9
  17.5 4.6 add_convert_fusion.2.refs_10_
  22.1 2.7 add_convert_fusion.3.refs_12_
  24.8 2.7 fusion.26.refs_11_
  27.5 2.3 copy.46
  29.8 2.3 copy.41
  32.1 1.2 copy.44
  33.2 7.5 %fusion = (f32[8,768]{1,0:T(8,128)S(1)}, f32[8,768,768]{1,2,0:T(8,128)S(1)}) fusion(f32[768,768]{0,1:T(8,128)S(1)} %copy-done.6, f32[8]{0:T(128)S(1)} %multiply_power_fusion, pred[768,768]{0,1:T(8,128)(4,1)} %copy.42, bf16[768,8,64]{0,2,1:T(8,128)(2,1)} %bitcast.133, bf16[768,8,64]{0,2,1:T(8,128)(2,1)} %bitcast.132), kind=kOutput, calls=%fused_computation.4 | convolution fusion | flops 627566592 | bytes 23420960 | tf_op jit(solution)/shard_map/qhd,khd->hqk/dot_general | solution.py:37
  40.7 5.4 %exponential_reduce_fusion = f32[8,768]{1,0:T(8,128)S(1)} fusion(f32[8,768,768]{1,2,0:T(8,128)S(1)} %get-tuple-element.66, f32[8,768]{1,0:T(8,128)S(1)} %get-tuple-element.65, f32[768,768]{0,1:T(8,128)S(1)} %copy-done.6, f32[8]{0:T(128)S(1)} %multiply_power_fusion, pred[768,768]{0,1:T(8,128)(4,1)S(1)} %copy-done.14), kind=kLoop, calls=%fused_computation.1 | loop fusion | flops 28305408 | bytes 21872672 | tf_op jit(solution)/shard_map/reduce_sum | solution.py:1064
  46.2 6.5 %fusion.27 = bf16[8,64,768]{2,1,0:T(8,128)(2,1)S(1)} fusion(bf16[768,8,64]{0,2,1:T(8,128)(2,1)S(1)} %bitcast.131, f32[8,768,768]{1,2,0:T(8,128)S(1)} %get-tuple-element.66, f32[8,768]{1,0:T(8,128)S(1)} %log_add_fusion.refs_13_, f32[768,768]{0,1:T(8,128)S(1)} %copy-done.6, f32[8]{0:T(128)S(1)} %multiply_power_fusion, pred[768,768]{0,1:T(8,128)(4,1)S(1)} %copy-done.14), kind=kOutput, calls=%fused_computation.58 | convolution fusion | flops 632684544 | bytes 23420960 | tf_op jit(solution)/shard_map/hqk,khd->qhd/dot_general | solution.py:1067
  52.7 1.2 copy.48.refs_0_
  53.9 106.2 %shard_map.257 = (bf16[24,32,2048]{2,1,0:T(8,128)(2,1)}, bf16[768,2048]{1,0:T(8,128)(2,1)}, bf16[768,2048]{1,0:T(8,128)(2,1)}, bf16[768,2048]{1,0:T(8,128)(2,1)}...) custom-call(bf16[768,512]{1,0:T(8,128)(2,1)} %copy.48.refs_0_, ...), custom_call_target="tpu_custom_call" | custom-call | tf_op jit(solution)/shard_map/pallas_call | solution.py:331
  160.1 0.9 reduce_sum.162
  160.9 174.1 %shard_map.258 = (bf16[8,96,2048]{2,1,0:T(8,128)(2,1)}, bf16[16,2,2,2,32,2048]{5,4,3,2,1,0:T(8,128)(2,1)}, bf16[8,96,2048]{2,1,0:T(8,128)(2,1)}, bf16[768,512]{1...) custom-call(bf16[8,96,2048]{2,1,0:T(8,128)(2,1)} %bitcast.127, ...), custom_call_target="tpu_custom_call" | custom-call | tf_op jit(solution)/shard_map/pallas_call | solution.py:804
  335.1 1.6 convert_reduce_fusion.3
  336.7 1.0 slice_reduce_fusion
  337.8 3.0 fusion.19
  340.8 1.8 fusion.18
  342.6 1.8 fusion.20
  344.5 3.1 pad_maximum_fusion
  347.6 0.4 copy-done.5
  348.0 2.9 copy.55
  350.9 4.0 convolution_convert_fusion.3
  355.0 3.5 fusion.22
  358.5 3.6 fusion.24
  362.1 3.7 add_convert_fusion.1
  365.9 97.1 %shard_map.259 = (bf16[8,96,2048]{2,1,0:T(8,128)(2,1)S(1)}, bf16[8,2,2,2,128,512]{5,4,3,2,1,0:T(8,128)(2,1)S(1)}) custom-call(bf16[8,96,2048]{2,1,0:T(8,128)(2,1)S(1)} %bitcast.110, bf16[6,2,2,2,128,512]{5,4,3,2,1,0:T(8,128)(2,1)S(1)} %bitcast.109, bf16[2,2,2,2,128,512]{5,4,3,2,1,0:T(8,128)(2,1)S(1)} %bitcast.111), custom_call_target="tpu_custom_call" | custom-call | tf_op jit(solution)/shard_map/pallas_call | solution.py:996
  463.0 1.4 fusion.12
  464.5 0.5 convert_reduce_fusion.1
  465.0 3.4 fusion.10
  468.3 25.2 %all-reduce = (f32[2048]{0:T(1024)}, f32[2048]{0:T(1024)}, f32[2,512]{1,0:T(2,128)}, f32[2048]{0:T(1024)}, f32[2048]{0:T(1024)}, /*index=5*/f32[2048]{0:T(1024)}, f32[2048]{0:T(1024)}, f32[2048]{0:T(1024)}) all-reduce(f32[2048]{0:T(1024)S(1)} %get-tuple-element.46, ...), channel_id=1, replica_groups=mesh['dp'=8,'tensor'=4] {'dp'}, use_global_device_ids=true, to_apply=%region_7.8 | all-reduce | flops 15360 | bytes 122880 | tf_op jit(solution)/shard_map/psum | solution.py:1195
  493.5 9.3 %add_convert_fusion = (bf16[768,2048]{1,0:T(8,128)(2,1)}, bf16[768,2048]{1,0:T(8,128)(2,1)}) fusion(bf16[768,2048]{1,0:T(8,128)(2,1)} %refs_2_.1, bf16[8,96,2048]{2,1,0:T(8,128)(2,1)S(1)} %get-tuple-element.41, bf16[8,96,2048]{2,1,0:T(8,128)(2,1)} %get-tuple-element.40, f32[768]{0:T(1024)S(1)} %negate_multiply_fusion, f32[768]{0:T(1024)S(1)} %multiply_multiply_fusion, ...), kind=kLoop, calls=%fused_computation.32 | loop fusion | flops 29884416 | bytes 22056960 | tf_op jit(solution)/shard_map/convert_element_type | solution.py:1194
  503.0 0.7 slice.44
  503.7 0.6 convert_bitcast_fusion.1
  504.3 2.7 copy.56
  506.9 6.6 %convert_bitcast_fusion = f32[2048,3,512]{2,0,1:T(8,128)} fusion(bf16[3,2048,512]{2,1,0:T(8,128)(2,1)S(1)} %bitcast.113), kind=kLoop, calls=%fused_computation.3 | loop fusion | flops 3145728 | bytes 18874368 | tf_op jit(solution)/shard_map/transpose | solution.py:1185
  513.5 6.6 %fusion.31 = (bf16[8,2,2,2,32,2048]{5,4,3,2,1,0:T(8,128)(2,1)S(1)}, bf16[8,2,2,2,32,2048]{5,4,3,2,1,0:T(8,128)(2,1)S(1)}) fusion(bf16[16,2,2,2,32,2048]{5,4,3,2,1,0:T(8,128)(2,1)} %get-tuple-element.44), kind=kLoop, calls=%fused_computation.74 | loop fusion | bytes 33554432 | tf_op jit(solution)/shard_map/slice | solution.py:1117
  520.1 12.6 %bitcast_convert_fusion = (f32[2048,2048]{1,0:T(8,128)}, f32[2048,2048]{1,0:T(8,128)}) fusion(bf16[8,2,2,2,32,2048]{5,4,3,2,1,0:T(8,128)(2,1)S(1)} %get-tuple-element.59, bf16[8,2,2,2,32,2048]{5,4,3,2,1,0:T(8,128)(2,1)S(1)} %get-tuple-element.60), kind=kLoop, calls=%fused_computation.14 | loop fusion | flops 8388608 | bytes 50331648 | tf_op jit(solution)/shard_map/reshape | solution.py:1117
  (72 shorter events, 0.4 us)
Async XLA Ops:
  0.6 7.7 %copy-start.20 = (f32[2048]{0:T(1024)S(1)}, f32[2048]{0:T(1024)}, u32[]{:S(2)}) copy-start(f32[2048]{0:T(1024)} %param.22) | copy-start | bytes 24580
  0.7 7.7 %copy-start.23 = (f32[2048]{0:T(1024)S(1)}, f32[2048]{0:T(1024)}, u32[]{:S(2)}) copy-start(f32[2048]{0:T(1024)} %param.26) | copy-start | bytes 24580
  0.7 7.7 %copy-start.24 = (f32[2048]{0:T(1024)S(1)}, f32[2048]{0:T(1024)}, u32[]{:S(2)}) copy-start(f32[2048]{0:T(1024)} %param.24) | copy-start | bytes 24580
  0.7 7.7 %copy-start.25 = (f32[2048]{0:T(1024)S(1)}, f32[2048]{0:T(1024)}, u32[]{:S(2)}) copy-start(f32[2048]{0:T(1024)} %param.23) | copy-start | bytes 24580
  0.7 7.1 %copy-start.26 = (f32[2,512]{1,0:T(2,128)S(1)}, f32[2,512]{1,0:T(2,128)}, u32[]{:S(2)}) copy-start(f32[2,512]{1,0:T(2,128)} %param.20) | copy-start | bytes 12292
  1.4 6.4 %copy-start.4 = (bf16[768,2048]{1,0:T(8,128)(2,1)S(1)}, bf16[768,2048]{1,0:T(8,128)(2,1)}, u32[]{:S(2)}) copy-start(bf16[768,2048]{1,0:T(8,128)(2,1)} %refs_3_.3) | copy-start | bytes 9437188
  4.8 11.5 %copy-start.2 = (bf16[768,2048]{1,0:T(8,128)(2,1)S(1)}, bf16[768,2048]{1,0:T(8,128)(2,1)}, u32[]{:S(2)}) copy-start(bf16[768,2048]{1,0:T(8,128)(2,1)} %refs_2_.1) | copy-start | bytes 9437188
  4.8 11.5 %copy-start.18 = (f32[2048]{0:T(1024)S(1)}, f32[2048]{0:T(1024)}, u32[]{:S(2)}) copy-start(f32[2048]{0:T(1024)} %param.17) | copy-start | bytes 24580
  4.8 11.5 %copy-start.22 = (f32[2048]{0:T(1024)S(1)}, f32[2048]{0:T(1024)}, u32[]{:S(2)}) copy-start(f32[2048]{0:T(1024)} %param.18) | copy-start | bytes 24580
  16.3 5.8 %slice-start.2 = ((s8[6291456]{0:T(1024)(128)(4,1)}), s8[2097152]{0:T(1024)(128)(4,1)S(1)}, s32[]{:S(2)}) async-start(s8[6291456]{0:T(1024)(128)(4,1)} %bitcast.121), calls=%async_computation.2 | async-start | bytes 4194304
  17.5 7.3 %copy-start.11 = (bf16[768,2048]{1,0:T(8,128)(2,1)}, bf16[768,2048]{1,0:T(8,128)(2,1)S(1)}, u32[]{:S(2)}) copy-start(bf16[768,2048]{1,0:T(8,128)(2,1)S(1)} %fusion.9) | copy-start | bytes 9437188
  17.5 4.6 slice-start.3
  22.1 9.9 %copy-start.13 = (bf16[768,512]{1,0:T(8,128)(2,1)}, bf16[768,512]{1,0:T(8,128)(2,1)S(1)}, u32[]{:S(2)}) copy-start(bf16[768,512]{1,0:T(8,128)(2,1)S(1)} %add_convert_fusion.2.refs_10_) | copy-start | bytes 2359300
  24.8 8.4 %copy-start.6 = (f32[768,768]{0,1:T(8,128)S(1)}, f32[768,768]{0,1:T(8,128)}, u32[]{:S(2)}) copy-start(f32[768,768]{0,1:T(8,128)} %subtract_convert_fusion) | copy-start | bytes 7077892
  33.2 7.5 %copy-start.14 = (pred[768,768]{0,1:T(8,128)(4,1)S(1)}, pred[768,768]{0,1:T(8,128)(4,1)}, u32[]{:S(2)}) copy-start(pred[768,768]{0,1:T(8,128)(4,1)} %copy.42) | copy-start | bytes 1769476
  40.7 5.4 %copy-start.17 = (bf16[768,512]{0,1:T(8,128)(2,1)S(1)}, bf16[768,512]{0,1:T(8,128)(2,1)}, u32[]{:S(2)}) copy-start(bf16[768,512]{0,1:T(8,128)(2,1)} %copy.41) | copy-start | bytes 2359300
  46.2 6.5 %copy-start.19 = (f32[8,768]{1,0:T(8,128)}, f32[8,768]{1,0:T(8,128)S(1)}, u32[]{:S(2)}) copy-start(f32[8,768]{1,0:T(8,128)S(1)} %log_add_fusion.refs_13_) | copy-start | bytes 73732
  52.7 107.4 %copy-start.16 = (bf16[8,64,768]{2,1,0:T(8,128)(2,1)}, bf16[8,64,768]{2,1,0:T(8,128)(2,1)S(1)}, u32[]{:S(2)}) copy-start(bf16[8,64,768]{2,1,0:T(8,128)(2,1)S(1)} %fusion.27) | copy-start | bytes 2359300
  160.9 176.9 %copy-start.12 = (bf16[768,2048]{1,0:T(8,128)(2,1)S(1)}, bf16[768,2048]{1,0:T(8,128)(2,1)}, u32[]{:S(2)}) copy-start(bf16[768,2048]{1,0:T(8,128)(2,1)} %copy-done.11) | copy-start | bytes 9437188
  336.7 4.0 copy-start.9
  340.8 1.8 copy-start.7
  344.5 3.5 copy-start.5
  350.9 4.1 copy-start.10
  355.0 3.5 copy-start.15
  358.5 3.6 copy-start.8
  358.5 7.3 %slice-start = ((s8[6291456]{0:T(1024)(128)(4,1)}), s8[4194304]{0:T(1024)(128)(4,1)S(1)}, s32[]{:S(2)}) async-start(s8[6291456]{0:T(1024)(128)(4,1)} %bitcast.107), calls=%async_computation | async-start | bytes 8388608
  362.1 3.8 slice-start.1
  365.8 97.2 %copy-start.3 = (bf16[768,2048]{1,0:T(8,128)(2,1)S(1)}, bf16[768,2048]{1,0:T(8,128)(2,1)}, u32[]{:S(2)}) copy-start(bf16[768,2048]{1,0:T(8,128)(2,1)} %refs_2_.1) | copy-start | bytes 9437188
  463.0 5.3 copy-start
  464.4 29.1 %copy-start.21 = (f32[2048]{0:T(1024)S(1)}, f32[2048]{0:T(1024)}, u32[]{:S(2)}) copy-start(f32[2048]{0:T(1024)} %param.28) | copy-start | bytes 24580
  493.5 9.3 %copy-start.1 = (bf16[8,2,2,2,128,512]{5,4,3,2,1,0:T(8,128)(2,1)S(1)}, bf16[8,2,2,2,128,512]{5,4,3,2,1,0:T(8,128)(2,1)}, u32[]{:S(2)}) copy-start(bf16[8,2,2,2,128,512]{5,4,3,2,1,0:T(8,128)(2,1)} %copy-done) | copy-start | bytes 25165828

commit v3 on v2

--- a/solution.py
+++ b/solution.py
@@ -78,7 +78,8 @@
         self.has_outer = depth > 0
         self.outer = jnp.where(self.has_outer, jnp.where(left, i - 1, i + 1), self.inner)
         self.is_mid = depth == n // 2 - 1
-        self.lag = slack * (2 * (n // 2 - 1 - depth) + 1)
+        self.first = slack * depth
+        self.lag = slack * (n - 1 - depth)
         self.most_lag = slack * (n - 1)
 
     @staticmethod
@@ -152,6 +153,139 @@
 
 def between(k, count):
     return jnp.logical_and(k >= 0, k < count)
+
+
+def head_forward(head, q, k, v, slope, off, tile, attended, lse):
+    length = q.shape[0]
+    odd = lax.rem(head, 2)
+    mask = lane_half(odd).astype(BF16)
+    lanes = pl.ds(pl.multiple_of((head // 2) * 2 * HD, 2 * HD), 2 * HD)
+    gain = slope[pl.ds(head, 1), 0:1]
+    for j in range(length // tile):
+        rows = slice(j * tile, (j + 1) * tile)
+        most = min(length, (j + 2) * tile)
+        scores = lax.dot_general(
+            k[0:most, lanes] * mask, q[rows, lanes], (((1,), (1,)), ((), ())), preferred_element_type=F32
+        )
+        scores = scores * (1.0 / math.sqrt(HD)) + gain * off[0:most, rows]
+        top = jnp.max(scores, axis=0, keepdims=True)
+        raised = jnp.exp(scores - top)
+        total = jnp.sum(raised, axis=0, keepdims=True)
+        lse[pl.ds(head, 1), rows] = top + jnp.log(total)
+        probs = (raised * (1.0 / total)).astype(BF16)
+        got = lax.dot_general(
+            v[0:most, lanes] * mask, probs, (((0,), (0,)), ((), ())), preferred_element_type=F32
+        )
+        mine = got.T.astype(BF16)
+
+        @pl.when(odd == 0)
+        def _(rows=rows, mine=mine):
+            attended[rows, lanes] = mine
+
+        @pl.when(odd == 1)
+        def _(rows=rows, mine=mine):
+            attended[rows, lanes] += mine
+
+
+def head_kernel(heads, *refs):
+    (src_h, w_h, vec_h, bias_h, slope_h, blocks_h), refs = refs[:6], refs[6:]
+    (normed_h, q_h, k_h, v_h, att_h, lse_h, off_h), refs = refs[:7], refs[7:]
+    (src, w, vec, bias, slope, blocks), refs = refs[:6], refs[6:]
+    (normed, q, k, v, att, lse, off), refs = refs[:7], refs[7:]
+    load, w_load, store = refs
+    length, width = src.shape
+    loads = [
+        pltpu.make_async_copy(a, b, load.at[j])
+        for j, (a, b) in enumerate(
+            ((src_h, src), (vec_h, vec), (blocks_h, blocks), (bias_h, bias), (slope_h, slope))
+        )
+    ]
+    w_loads = [pltpu.make_async_copy(w_h.at[m], w.at[m], w_load.at[m]) for m in range(3)]
+    for one in loads + w_loads:
+        one.start()
+    for one in loads:
+        one.wait()
+    step = 16
+
+    def normalize(i, carry):
+        at = pl.ds(pl.multiple_of(i * step, step), step)
+        value = src[at, :].astype(F32)
+        centred = value - jnp.sum(value, axis=-1, keepdims=True) / width
+        var = jnp.sum(centred * centred, axis=-1, keepdims=True) / width
+        normed[at, :] = (centred * lax.rsqrt(var + EPS) * vec[0:1, :] + vec[1:2, :]).astype(BF16)
+        return carry
+
+    lax.fori_loop(0, length // step, normalize, 0)
+
+    here = blocks[...].astype(F32)
+    there = jnp.broadcast_to(here, (8, length)).T[:, 0:1]
+    for j in range(length // 256):
+        cols = slice(j * 256, (j + 1) * 256)
+        distance = (
+            lax.broadcasted_iota(jnp.int32, (length, 256), 0)
+            - lax.broadcasted_iota(jnp.int32, (length, 256), 1)
+            - j * 256
+        ).astype(F32)
+        off[:, cols] = jnp.where(there <= here[:, cols], distance, -1e30)
+
+    for m, to in enumerate((q, k, v)):
+        w_loads[m].wait()
+
+        def project(i, carry, m=m, to=to):
+            at = pl.ds(pl.multiple_of(i * 256, 256), 256)
+            to[at, :] = (
+                jnp.dot(normed[at, :], w[m], preferred_element_type=F32) + bias[m : m + 1, :]
+            ).astype(BF16)
+            return carry
+
+        lax.fori_loop(0, length // 256, project, 0)
+
+    stores = [
+        pltpu.make_async_copy(a, b, store.at[j])
+        for j, (a, b) in enumerate(
+            ((normed, normed_h), (off, off_h), (q, q_h), (k, k_h), (v, v_h), (att, att_h), (lse, lse_h))
+        )
+    ]
+    for one in stores[:5]:
+        one.start()
+
+    def attend(head, carry):
+        head_forward(head, q, k, v, slope, off, HEAD_TILE, att, lse)
+        return carry
+
+    lax.fori_loop(0, heads, attend, 0)
+    for one in stores[5:]:
+        one.start()
+    for one in stores:
+        one.wait()
+
+
+def head_call(src, w, vec, bias, slope, blocks):
+    length, width = src.shape
+    local = w.shape[2]
+    heads = local // HD
+    inputs = (src, w, vec, bias, slope, blocks)
+    shapes = [
+        ((length, width), BF16),
+        *[((length, local), BF16)] * 4,
+        ((heads, length), F32),
+        ((length, length), F32),
+    ]
+    dma = pltpu.SemaphoreType.DMA
+    return pl.pallas_call(
+        functools.partial(head_kernel, heads),
+        out_shape=[jax.ShapeDtypeStruct(*one) for one in shapes],
+        in_specs=[pl.BlockSpec(memory_space=pl.ANY)] * len(inputs),
+        out_specs=[pl.BlockSpec(memory_space=pl.ANY)] * len(shapes),
+        scratch_shapes=[
+            *[pltpu.VMEM(one.shape, one.dtype) for one in inputs],
+            *[pltpu.VMEM(*one) for one in shapes],
+            dma((5,)),
+            dma((3,)),
+            dma((7,)),
+        ],
+        compiler_params=pltpu.CompilerParams(vmem_limit_bytes=60 << 20),
+    )(*inputs)
 
 
 ROWS = 32
@@ -256,9 +390,11 @@
         def _():
             produce(t // group)
 
-        @pl.when(t < chunks)
-        def _():
-            chain.reduce(t)
+        ready = t - chain.first
+
+        @pl.when(between(ready, chunks))
+        def _():
+            chain.reduce(ready)
 
         back = t - chain.lag
 
@@ -341,11 +477,10 @@
 
 
 class Ring:
-    GONE = 5
-
-    def __init__(self, n, refs, slots):
-        self.chain = Chain(n, refs)
+    def __init__(self, n, refs, slots, slack):
+        self.chain = Chain(n, refs, slack)
         self.slots = slots
+        self.gone = self.chain.most_lag + 2
 
     def at(self, k):
         return lax.rem(k, self.slots)
@@ -361,21 +496,20 @@
 
 
 class Cube:
-    SLOTS = 7
-    GONE = 6
-
-    def __init__(self, refs, out, step):
+    def __init__(self, refs, keep, step, apart=1):
         (self.fin, self.give, self.c0, self.r1, self.r2), refs = refs[:5], refs[5:]
         self.s0, self.q0, self.s1, self.q1, self.s2, self.q2, self.s3, self.q3, self.s4, self.q4, self.kept = refs
-        self.out, self.step = out, step
+        self.keep_of, self.step, self.apart = keep, step, apart
+        self.gone = 6 * apart
+        self.slots = self.gone + 1
         d = lax.axis_index("dp")
         self.c, self.x, self.y = d % 2, (d // 2) % 2, d // 4
         self.to_c, self.to_x, self.to_y = d + 1 - 2 * self.c, d + 2 - 4 * self.x, d + 4 - 8 * self.y
         self.stages = (self.stage1, self.stage2, self.stage3, self.stage4, self.stage5, self.retire)
 
     @classmethod
-    def scratch(cls, block):
-        dma, n = pltpu.SemaphoreType.DMA, cls.SLOTS
+    def scratch(cls, block, apart=1):
+        dma, n = pltpu.SemaphoreType.DMA, 6 * apart + 1
         return [
             pltpu.VMEM((n, 2, 2, 2, *block), BF16),
             pltpu.VMEM((n, 2, 2, *block), BF16),
@@ -392,7 +526,7 @@
             pl.semaphore_signal(barrier, inc=1, device_id={"dp": to}, device_id_type=MESH)
 
     def slot(self, k):
-        return lax.rem(k, self.SLOTS)
+        return lax.rem(k, self.slots)
 
     def half(self, k):
         p = self.slot(k)
@@ -429,9 +563,9 @@
         mine = self.fin.at[p, self.c]
         return remote(mine, mine, self.s4.at[p], self.q4.at[p], "dp", self.to_c)
 
-    def keep(self, k):
+    def kept_wait(self, k):
         p = self.slot(k)
-        return pltpu.make_async_copy(self.fin.at[p], self.out.at[k], self.kept.at[p])
+        pltpu.make_async_copy(self.fin.at[p], self.fin.at[p], self.kept.at[p]).wait()
 
     def add_quarters(self, k, got):
         p = self.slot(k)
@@ -468,16 +602,17 @@
 
     def stage5(self, k):
         self.hop4(k).wait_recv()
-        self.keep(k).start()
+        p = self.slot(k)
+        self.keep_of(k, self.fin.at[p], self.kept.at[p])
 
     def retire(self, k):
         for one in self.hop3(k) + (self.hop4(k),):
             one.wait_send()
-        self.keep(k).wait()
+        self.kept_wait(k)
 
     def tick(self, t, count):
         for late, stage in reversed(tuple(enumerate(self.stages, 1))):
-            k = t - late
+            k = t - late * self.apart
 
             @pl.when(between(k, count))
             def _(stage=stage, k=k):
@@ -546,29 +681,40 @@
             to[:, lanes] += (got[...] * factor).astype(BF16)
 
 
-BACK_ROWS = 96
+BACK_ROWS = 48
+BACK_SLOTS = 12
+BACK_SLACK = 2
+BACK_APART = 2
+BACK_COLUMNS = 1024
 HEAD_TILE = 256
 
 
 def back_kernel(n, heads, *refs):
     (grad_h, mlp_h, activ_h, dy_h, second_h, pre_h, src_h, tot_h), refs = refs[:8], refs[8:]
     smalls_h, refs = refs[:8], refs[8:]
-    (sum_h, g_out, resid_h, qg_h, kg_h, vg_h, cols_h), refs = refs[:7], refs[7:]
+    (sum_h, g_out, resid_h, grads_h, cols_h), refs = refs[:5], refs[5:]
     (left, dy, pre, src, tot, resid), refs = refs[:6], refs[6:]
     smalls, refs = refs[:8], refs[8:]
     vec, wo, q, k, v, lse, slope, off = smalls
     (up, qg, kg, vg, k_acc, v_acc, cols), refs = refs[:7], refs[7:]
     (load, left_sem, part_sem, row_sem, resid_sem, sum_sem), refs = refs[:6], refs[6:]
-    slots = 8
-    ring, refs = Ring(n, refs[:7], slots), refs[7:]
+    ring, refs = Ring(n, refs[:7], BACK_SLOTS, BACK_SLACK), refs[7:]
     chain = ring.chain
-    cube = Cube(refs, g_out, 32)
+
+    per_row = dy_h.shape[1] // BACK_COLUMNS
+
+    def keep(k, piece_ref, sem):
+        here = pl.ds(pl.multiple_of(lax.rem(k, per_row) * BACK_COLUMNS, BACK_COLUMNS), BACK_COLUMNS)
+        pltpu.make_async_copy(piece_ref, g_out.at[k // per_row, :, :, :, :, here], sem).start()
+
+    cube = Cube(refs, keep, 32, BACK_APART)
     width, units = dy.shape[1], pre.shape[1]
     rows, per_sum = BACK_ROWS, grad_h.shape[0]
     total_z = 2 * per_sum
     piece = 256
     first = activ_h.shape[1] // piece
-    total_p = first + second_h.shape[1] // piece
+    total_left = first + second_h.shape[1] // piece
+    total_p = total_left * per_row
 
     loads = [pltpu.make_async_copy(a, b, load.at[j]) for j, (a, b) in enumerate(zip(smalls_h, smalls))]
     loads += [pltpu.make_async_copy(dy_h, dy, load.at[8]), pltpu.make_async_copy(pre_h, pre, load.at[9])]
@@ -600,7 +746,7 @@
         def _():
             left_load(p, 0).start()
 
-        @pl.when(between(p - first, total_p - first))
+        @pl.when(between(p - first, total_left - first))
         def _():
             left_load(p, 1).start()
 
@@ -620,9 +766,9 @@
         return pltpu.make_async_copy(chain.inner_in.at[at], sum_h.at[j - per_sum], sum_sem.at[at])
 
     part_start(0)
-    part_start(1)
     left_start(0)
     loads[8].start()
+    part_start(1)
     for one in loads[:8] + loads[9:]:
         one.start()
     barrier = pltpu.get_barrier_semaphore()
@@ -630,32 +776,37 @@
     cube.greet(barrier)
     cols[...] = jnp.zeros_like(cols)
     chain.wait_greetings(barrier, 3)
-    for one in loads:
-        one.wait()
+    loads[8].wait()
 
     def produce(p):
-        at = lax.rem(p, 2)
+        r, part = p // per_row, lax.rem(p, per_row)
+        at = lax.rem(r, 2)
         to = cube.slot(p)
-        pltpu.make_async_copy(activ_h.at[:, pl.ds(0, piece)], left.at[at], left_sem.at[at]).wait()
+
+        @pl.when(part == 0)
+        def _():
+            left_start(r + 1)
+            pltpu.make_async_copy(activ_h.at[:, pl.ds(0, piece)], left.at[at], left_sem.at[at]).wait()
+
         mine, theirs = cube.c, 1 - cube.c
         count = piece // 8
 
         def product(right):
             for side, store in ((theirs, cube.give.at[to]), (mine, cube.fin.at[to, cube.c])):
                 rows_of = left[at, :, pl.ds(pl.multiple_of(side * (piece // 2), piece // 2), piece // 2)]
-                for j in range(right.shape[1] // 512):
-                    here = pl.ds(j * 512, 512)
-                    got = weighted(rows_of, right[:, here])
+                for j in range(BACK_COLUMNS // 512):
+                    from_here = pl.ds(pl.multiple_of(part * BACK_COLUMNS + j * 512, 512), 512)
+                    got = weighted(rows_of, right[:, from_here])
                     for a in range(2):
                         for b in range(2):
                             lo = (2 * a + b) * count
-                            store[a, b, :, here] = got[lo : lo + count]
-
-        @pl.when(p < first)
+                            store[a, b, :, j * 512 : (j + 1) * 512] = got[lo : lo + count]
+
+        @pl.when(r < first)
         def _():
             product(dy)
 
-        @pl.when(p >= first)
+        @pl.when(r >= first)
         def _():
             product(pre)
 
@@ -695,7 +846,7 @@
         resid_store(j).start()
 
     def tick(t, carry):
-        gone = t - Ring.GONE
+        gone = t - ring.gone
 
         @pl.when(between(gone, total_z))
         def _():
@@ -706,11 +857,12 @@
                 sum_store(gone).wait()
 
         part_start(t + 2)
-
-        @pl.when(t < total_z)
-        def _():
-            part_load(t, 0).wait()
-            ring.reduce(t)
+        ready = t - chain.first
+
+        @pl.when(between(ready, total_z))
+        def _():
+            part_load(ready, 0).wait()
+            ring.reduce(ready)
 
         back = t - chain.lag
 
@@ -724,12 +876,16 @@
 
         cube.tick(t, total_p)
 
+        @pl.when(t == 2)
+        def _():
+            for one in loads[:8] + loads[9:]:
+                one.wait()
+
         @pl.when(t < total_p)
         def _():
-            left_start(t + 1)
             produce(t)
 
-        chunk = t - 4
+        chunk = t - chain.most_lag - 1
 
         @pl.when(between(chunk + 1, per_sum))
         def _():
@@ -744,7 +900,7 @@
         def _():
             rows_back(chunk)
 
-        head = t - 4 - per_sum
+        head = t - chain.most_lag - 1 - per_sum
 
         @pl.when(between(head, heads))
         def _():
@@ -752,11 +908,11 @@
 
         return carry
 
-    ticks = max(total_z + Ring.GONE, total_p + Cube.GONE, 4 + per_sum + max(heads, 2))
+    ticks = max(total_z + ring.gone, total_p + cube.gone, chain.most_lag + 1 + per_sum + max(heads, 2))
     lax.fori_loop(0, ticks, tick, 0)
     stores = [
         pltpu.make_async_copy(a, b, load.at[j])
-        for j, (a, b) in enumerate(((qg, qg_h), (kg, kg_h), (vg, vg_h), (cols, cols_h)))
+        for j, (a, b) in enumerate(((qg, grads_h.at[0]), (kg, grads_h.at[1]), (vg, grads_h.at[2]), (cols, cols_h)))
     ]
     for one in stores:
         one.start()
@@ -774,15 +930,15 @@
 
     smalls = (vec, wo, q, k, v, lse, slope, off)
     inputs = (cut(grad), cut(mlp), activ, dy, second, pre, cut(src), cut(tot), *smalls)
-    pieces = (activ.shape[1] + second.shape[1]) // 256
+    tiles = (activ.shape[1] + second.shape[1]) // 256
     shapes = [
         ((chunks, BACK_ROWS, width), BF16),
-        ((pieces, 2, 2, 2, 32, width), BF16),
+        ((tiles, 2, 2, 2, 32, width), BF16),
         ((chunks, BACK_ROWS, width), BF16),
-        *[(q.shape, BF16)] * 3,
+        ((3, *q.shape), BF16),
         ((3, 8, width), F32),
     ]
-    slots = 8
+    slots = BACK_SLOTS
     scratch = [
         pltpu.VMEM((2, length, 256), BF16),
         pltpu.VMEM(dy.shape, BF16),
@@ -799,7 +955,7 @@
         dma((2,)),
         dma((slots,)),
         *Chain.scratch(slots, (BACK_ROWS, width)),
-        *Cube.scratch((32, width)),
+        *Cube.scratch((32, BACK_COLUMNS), BACK_APART),
     ]
     return pl.pallas_call(
         functools.partial(back_kernel, n, q.shape[1] // HD),
@@ -813,196 +969,234 @@
     )(*inputs)
 
 
-def sums_kernel(n, n_z, n_dp, chunks, pieces, *refs):
-    z_in, refs = refs[:n_z], refs[n_z:]
-    g_in, refs = refs[:n_dp], refs[n_dp:]
-    z_out, g_out, load_sem, store_sem, *refs = refs
-    chain, refs = Chain(n, refs[:7]), refs[7:]
-    fin, c0, r1, r2, gl, c0s, c0r, s1, q1, s2, q2, s3, q3, s4, q4, gstore = refs
-
-    total_z = sum(chunks)
-    total_p = sum(pieces)
-    d = lax.axis_index("dp")
-    c, x, y = d % 2, (d // 2) % 2, d // 4
-    to_c, to_x, to_y = d + 1 - 2 * c, d + 2 - 4 * x, d + 4 - 8 * y
-
-    def z_load(j, at):
-        return pltpu.make_async_copy(z_in[j], chain.part.at[pl.ds(at, chunks[j])], load_sem.at[j])
-
-    def g_load(j, at):
-        return pltpu.make_async_copy(g_in[j].at[:, c], fin.at[pl.ds(at, pieces[j]), c], gl.at[j])
-
-    z_at = [sum(chunks[:k]) for k in range(n_z)]
-    p_at = [sum(pieces[:k]) for k in range(n_dp)]
-    for j in range(n_z):
-        z_load(j, z_at[j]).start()
-    for j in range(n_dp):
-        g_load(j, p_at[j]).start()
-
+FRONT_ROWS = 48
+
+
+def front_kernel(n, *refs):
+    (grads_h, w_h, normed_h, att_h, resid_h, src_h, gain_h, small_h), refs = refs[:8], refs[8:]
+    (mix_out, wo_out, input_h, small_out), refs = refs[:4], refs[4:]
+    (grads, w, normed, att, resid, src, gain, cols, buf, got), refs = refs[:10], refs[10:]
+    (load, row_sem, ss, sq), refs = refs[:4], refs[4:]
+    chain, refs = Chain(n, refs[:7], FRONT_SLACK), refs[7:]
+    length, width = src.shape
+    local = att.shape[1]
+    blocks = width // local
+    rows = FRONT_ROWS
+    chunks = length // rows
+    group = 4
+    total_p = 4 * blocks
+
+    def keep(k, piece_ref, sem):
+        @pl.when(k < blocks)
+        def _():
+            at = pl.ds(pl.multiple_of(k * local, local), local)
+            pltpu.make_async_copy(piece_ref, wo_out.at[:, :, :, :, at], sem).start()
+
+        @pl.when(k >= blocks)
+        def _():
+            pltpu.make_async_copy(piece_ref, mix_out.at[k - blocks], sem).start()
+
+    cube = Cube(refs, keep, 32, FRONT_APART)
+
+    pairs = (
+        (grads_h, grads), (w_h, w), (att_h, att), (resid_h, resid), (normed_h, normed), (src_h, src),
+        (gain_h, gain), (small_h, buf.at[0]),
+    )
+    loads = [pltpu.make_async_copy(a, b, load.at[j]) for j, (a, b) in enumerate(pairs)]
+    for one in loads:
+        one.start()
     barrier = pltpu.get_barrier_semaphore()
     chain.greet(barrier)
-    for to in (to_c, to_x, to_y):
-        pl.semaphore_signal(barrier, inc=1, device_id={"dp": to}, device_id_type=MESH)
+    cube.greet(barrier)
+    cols[...] = jnp.zeros_like(cols)
     chain.wait_greetings(barrier, 3)
-
-    def store(k):
-        return pltpu.make_async_copy(chain.inner_in.at[k], z_out.at[k], store_sem.at[k])
-
-    def core_half(k, j, at):
-        return remote(g_in[j].at[k - at, 1 - c], c0.at[k], c0s.at[k], c0r.at[k], "dp", to_c)
-
-    def hop1(k):
-        return (
-            remote(fin.at[k, c, 0, 1 - x], r1.at[k, 0], s1.at[k, 0], q1.at[k, 0], "dp", to_x),
-            remote(fin.at[k, c, 1, 1 - y], r1.at[k, 1], s1.at[k, 1], q1.at[k, 1], "dp", to_y),
-        )
-
-    def hop2(k):
-        return (
-            remote(fin.at[k, c, 0, x], r2.at[k, 0], s2.at[k, 0], q2.at[k, 0], "dp", to_y),
-            remote(fin.at[k, c, 1, y], r2.at[k, 1], s2.at[k, 1], q2.at[k, 1], "dp", to_x),
-        )
-
-    def hop3(k):
-        return (
-            remote(fin.at[k, c, 0, x], fin.at[k, c, 0, x], s3.at[k, 0], q3.at[k, 0], "dp", to_x),
-            remote(fin.at[k, c, 1, y], fin.at[k, c, 1, y], s3.at[k, 1], q3.at[k, 1], "dp", to_y),
-        )
-
-    def hop4(k):
-        return remote(fin.at[k, c], fin.at[k, c], s4.at[k], q4.at[k], "dp", to_c)
-
-    def g_store(k):
-        return pltpu.make_async_copy(fin.at[k], g_out.at[k], gstore.at[k])
-
-    for j in range(n_dp):
-
-        def send_half(k, carry, j=j):
-            core_half(k + p_at[j], j, p_at[j]).start()
-            return carry
-
-        lax.fori_loop(0, pieces[j], send_half, 0)
-
-    step = 32 if r1.shape[2] % 32 == 0 else 16
-
-    def stage1(k):
-        for j in range(n_dp):
-
-            @pl.when(k == p_at[j])
-            def _(j=j):
-                g_load(j, p_at[j]).wait()
-
-        core_half(k, 0, k).wait_recv()
+    for one in loads[:2]:
+        one.wait()
+
+    def produce_rows(g):
+        at = pl.ds(pl.multiple_of(g * group * rows, group * rows), group * rows)
+        for j in range(width // 512):
+            here = pl.ds(j * 512, 512)
+            total = sum(
+                lax.dot_general(
+                    grads[m, at, :], w[m, here, :], (((1,), (1,)), ((), ())), preferred_element_type=F32
+                )
+                for m in range(3)
+            ).astype(BF16)
+            for q in range(group):
+                chain.part[g * group + q, :, here] = total[q * rows : (q + 1) * rows]
+
+    half = local // 2
+    count = half // 4
+
+    def put(to, side, value):
         for a in range(2):
             for b in range(2):
-                add_rows(fin.at[k, c, a, b], c0.at[k, a, b], step)
-        for one in hop1(k):
-            one.start()
-
-    def stage2(k):
-        for one in hop1(k):
-            one.wait()
-        add_rows(fin.at[k, c, 0, x], r1.at[k, 0], step)
-        add_rows(fin.at[k, c, 1, y], r1.at[k, 1], step)
-        for one in hop2(k):
-            one.start()
-
-    def stage3(k):
-        for one in hop2(k):
-            one.wait()
-        add_rows(fin.at[k, c, 0, x], r2.at[k, 0], step)
-        add_rows(fin.at[k, c, 1, y], r2.at[k, 1], step)
-        for one in hop3(k):
-            one.start()
-
-    def stage4(k):
-        for one in hop3(k):
-            one.wait_recv()
-        hop4(k).start()
-
-    def stage5(k):
-        hop4(k).wait_recv()
-        g_store(k).start()
+                lo = (2 * a + b) * count
+                to[a, b] = value[lo : lo + count]
+
+    def produce(p):
+        slot = cube.slot(p)
+        for side, to in ((1 - cube.c, cube.give.at[slot]), (cube.c, cube.fin.at[slot, cube.c])):
+
+            @pl.when(p < blocks)
+            def _(side=side, to=to):
+                left = att[:, pl.ds(pl.multiple_of(side * half, half), half)]
+                right = resid[:, pl.ds(pl.multiple_of(p * local, local), local)]
+                put(to, side, weighted(left, right))
+
+            @pl.when(p >= blocks)
+            def _(side=side, to=to):
+                m, r = p // blocks - 1, lax.rem(p, blocks)
+                left = normed[:, pl.ds(pl.multiple_of(r * local + side * half, half), half)]
+                put(to, side, weighted(left, grads[m]))
+
+        cube.half(p).start()
+
+    def row_sum(x):
+        return jnp.sum(x, axis=-1, keepdims=True)
+
+    def row_store(j):
+        at = pl.ds(pl.multiple_of(j * rows, rows), rows)
+        return pltpu.make_async_copy(src.at[at], input_h.at[at], row_sem.at[j])
+
+    def rows_back(j):
+        step = 16
+
+        def body(i, carry):
+            here = pl.ds(pl.multiple_of(i * step, step), step)
+            at = pl.ds(pl.multiple_of(j * rows + i * step, step), step)
+            value = src[at, :].astype(F32)
+            centred = value - row_sum(value) / width
+            spread = lax.rsqrt(row_sum(centred * centred) / width + EPS)
+            normal = centred * spread
+            down = chain.inner_in[j, here, :].astype(F32)
+            scaled = down * gain[0:1, :]
+            flat, slope_of = row_sum(scaled) / width, row_sum(scaled * normal) / width
+            back = spread * (scaled - flat - normal * slope_of)
+            src[at, :] = (back + resid[at, :].astype(F32)).astype(BF16)
+            for c, item in enumerate((down * normal, down)):
+                cols[c] += item[0:8] + item[8:16]
+            return carry
+
+        lax.fori_loop(0, rows // step, body, 0)
+        row_store(j).start()
+
+    def swap(j):
+        to = (cube.to_c, cube.to_x, cube.to_y)[j]
+        return remote(buf.at[j], got.at[j], ss.at[j], sq.at[j], "dp", to)
+
+    def small_step(j):
+        if j == 0:
+            for c in range(2):
+                buf[0, c : c + 1, :] = jnp.sum(cols[c], axis=0, keepdims=True)
+        else:
+            swap(j - 1).wait()
+            buf[j] = buf[j - 1] + got[j - 1]
+        if j < 3:
+            swap(j).start()
+
+    late = chain.most_lag + 1
 
     def tick(t, carry):
-        @pl.when(t < total_z)
-        def _():
-            for j in range(n_z):
-
-                @pl.when(t == z_at[j])
-                def _(j=j):
-                    z_load(j, z_at[j]).wait()
-
-            chain.reduce(t)
+        @pl.when(jnp.logical_and(lax.rem(t, group) == 0, t < chunks))
+        def _():
+            produce_rows(t // group)
+
+        ready = t - chain.first
+
+        @pl.when(between(ready, chunks))
+        def _():
+            chain.reduce(ready)
 
         back = t - chain.lag
 
-        @pl.when(between(back, total_z))
+        @pl.when(between(back, chunks))
         def _():
             chain.spread(back)
-            store(back).start()
-
-        for late, stage in enumerate((stage1, stage2, stage3, stage4, stage5)):
-            k = t - late
-
-            @pl.when(between(k, total_p))
-            def _(stage=stage, k=k):
-                stage(k)
+
+        cube.tick(t, total_p)
+
+        @pl.when(t == 0)
+        def _():
+            for one in loads[2:4]:
+                one.wait()
+
+        @pl.when(t == 2)
+        def _():
+            for one in loads[4:]:
+                one.wait()
+
+        @pl.when(t < total_p)
+        def _():
+            produce(t)
+
+        @pl.when(between(t - late, chunks))
+        def _():
+            rows_back(t - late)
+
+        for j in range(4):
+
+            @pl.when(t == late + chunks + j)
+            def _(j=j):
+                small_step(j)
 
         return carry
 
-    lax.fori_loop(0, max(total_z + chain.most_lag, total_p + 4), tick, 0)
-
-    def drain_z(k, carry):
+    lax.fori_loop(0, max(chunks + late + 4, total_p + cube.gone), tick, 0)
+    small_store = pltpu.make_async_copy(buf.at[3], small_out, load.at[0])
+    small_store.start()
+
+    def drain(k, carry):
         chain.drain(k)
-        store(k).wait()
+        row_store(k).wait()
         return carry
 
-    lax.fori_loop(0, total_z, drain_z, 0)
-
-    def drain_g(k, carry):
-        core_half(k, 0, k).wait_send()
-        for one in hop3(k) + (hop4(k),):
-            one.wait_send()
-        g_store(k).wait()
-        return carry
-
-    lax.fori_loop(0, total_p, drain_g, 0)
-
-
-def device_sums(n, z_parts, g_parts, collective_id):
-    chunks = tuple(one.shape[0] for one in z_parts)
-    pieces = tuple(one.shape[0] for one in g_parts)
-    nz, npc = sum(chunks), sum(pieces)
-    z_block = z_parts[0].shape[1:]
-    g_block = g_parts[0].shape[4:]
+    lax.fori_loop(0, chunks, drain, 0)
+    small_store.wait()
+
+
+FRONT_SLACK = 2
+FRONT_APART = 2
+
+
+def front_call(n, grads, w, normed, att, resid, src, gain, small):
+    length, width = src.shape
+    local = att.shape[1]
+    blocks = width // local
+    chunks = length // FRONT_ROWS
+    block = (local // 8, local)
     dma = pltpu.SemaphoreType.DMA
-    scratch = [dma((len(chunks),)), dma((nz,))] + Chain.scratch(nz, z_block)
-    scratch += [
-        pltpu.VMEM((npc, 2, 2, 2, *g_block), BF16),
-        pltpu.VMEM((npc, 2, 2, *g_block), BF16),
-        pltpu.VMEM((npc, 2, *g_block), BF16),
-        pltpu.VMEM((npc, 2, *g_block), BF16),
-        dma((len(pieces),)),
-        dma((npc,)),
-        dma((npc,)),
+    inputs = (grads, w, normed, att, resid, src, gain, small)
+    shapes = [
+        ((3 * blocks, 2, 2, 2, *block), BF16),
+        ((2, 2, 2, local // 8, width), BF16),
+        ((length, width), BF16),
+        (small.shape, F32),
     ]
-    scratch += [dma((npc, 2))] * 6 + [dma((npc,))] * 3
-    out_shape = [
-        jax.ShapeDtypeStruct((nz, *z_block), BF16),
-        jax.ShapeDtypeStruct((npc, 2, 2, 2, *g_block), BF16),
+    order = (grads, w, normed, att, resid, src, gain)
+    scratch = [
+        *[pltpu.VMEM(one.shape, one.dtype) for one in order],
+        pltpu.VMEM((2, 8, width), F32),
+        pltpu.VMEM((4, *small.shape), F32),
+        pltpu.VMEM((3, *small.shape), F32),
+        dma((8,)),
+        dma((chunks,)),
+        dma((3,)),
+        dma((3,)),
+        *Chain.scratch(chunks, (FRONT_ROWS, width)),
+        *Cube.scratch(block, FRONT_APART),
     ]
-    vmem = 2 * (3 * nz * math.prod(z_block) + 16 * npc * math.prod(g_block))
     return pl.pallas_call(
-        functools.partial(sums_kernel, n, len(z_parts), len(g_parts), chunks, pieces),
-        out_shape=out_shape,
-        in_specs=[pl.BlockSpec(memory_space=pl.ANY)] * (len(z_parts) + len(g_parts)),
-        out_specs=[pl.BlockSpec(memory_space=pl.ANY)] * len(out_shape),
+        functools.partial(front_kernel, n),
+        out_shape=[jax.ShapeDtypeStruct(*one) for one in shapes],
+        in_specs=[pl.BlockSpec(memory_space=pl.ANY)] * len(inputs),
+        out_specs=[pl.BlockSpec(memory_space=pl.ANY)] * len(shapes),
         scratch_shapes=scratch,
         compiler_params=pltpu.CompilerParams(
-            collective_id=collective_id, has_side_effects=True, vmem_limit_bytes=vmem + (2 << 20)
+            collective_id=2, has_side_effects=True, vmem_limit_bytes=60 << 20
         ),
-    )(*z_parts, *g_parts)
+    )(*inputs)
 
 
 def on_device(
@@ -1032,42 +1226,32 @@
     local_heads = local_width // HD
     units = expand_weight.shape[1]
     first_head = lax.axis_index("tensor") * local_heads
-    rows = 96
-
-    def sums(z_parts, g_parts, collective_id):
-        if not fast:
-            return (
-                [lax.psum(one.astype(BF16), "tensor").astype(F32) for one in z_parts],
-                [lax.psum(one, "dp") for one in g_parts],
-            )
-        z_low = [one.astype(BF16).reshape(length // rows, rows, width) for one in z_parts]
-        out = device_sums(n_tensor, z_low, [one.astype(BF16) for one in g_parts], collective_id)
-        z_all = out[0].reshape(len(z_parts), length, width)
-        z_out = [z_all[k].astype(F32) for k in range(len(z_parts))]
-        g_out, at = [], 0
-        for one in g_parts:
-            g_out.append(out[1][at : at + one.shape[0]].astype(F32))
-            at += one.shape[0]
-        return z_out, g_out
-
     weights = mixing_weight.transpose(1, 0, 2)
-    normed_low = layer_norm(source, first_gain, first_shift).astype(BF16)
-
-    def project(k):
-        return jnp.dot(normed_low, weights[k], preferred_element_type=F32)
-
-    query = (project(0) + mixing_bias[0]).astype(BF16).reshape(length, local_heads, HD)
-    keys = project(1).astype(BF16).reshape(length, local_heads, HD)
-    vals = (project(2) + mixing_bias[1]).astype(BF16).reshape(length, local_heads, HD)
-    masked = biased_scores(query, keys, blocks, first_head)
-    row_top = jnp.max(masked, axis=-1, keepdims=True)
-    logsum = row_top + jnp.log(jnp.sum(jnp.exp(masked - row_top), axis=-1, keepdims=True))
-    probs_low = jnp.exp(masked - logsum).astype(BF16)
-    attended = (
-        jnp.einsum("hqk,khd->qhd", probs_low, vals, preferred_element_type=F32)
-        .reshape(length, local_width)
-        .astype(BF16)
-    )
+    if fast:
+        numbers = (first_head + jnp.arange(local_heads)).astype(F32)
+        slope = jnp.broadcast_to((2.0 ** (-8.0 * (numbers + 1.0) / H))[:, None], (local_heads, 128))
+        bias = jnp.stack([mixing_bias[0], jnp.zeros_like(mixing_bias[0]), mixing_bias[1]])
+        normed_low, query, keys, vals, attended, logsum, off = head_call(
+            inputs, weights, jnp.stack([first_gain, first_shift]), bias, slope, block_ids
+        )
+    else:
+        normed_low = layer_norm(source, first_gain, first_shift).astype(BF16)
+
+        def project(k):
+            return jnp.dot(normed_low, weights[k], preferred_element_type=F32)
+
+        query = (project(0) + mixing_bias[0]).astype(BF16).reshape(length, local_heads, HD)
+        keys = project(1).astype(BF16).reshape(length, local_heads, HD)
+        vals = (project(2) + mixing_bias[1]).astype(BF16).reshape(length, local_heads, HD)
+        masked = biased_scores(query, keys, blocks, first_head)
+        row_top = jnp.max(masked, axis=-1, keepdims=True)
+        logsum = row_top + jnp.log(jnp.sum(jnp.exp(masked - row_top), axis=-1, keepdims=True))
+        probs_low = jnp.exp(masked - logsum).astype(BF16)
+        attended = (
+            jnp.einsum("hqk,khd->qhd", probs_low, vals, preferred_element_type=F32)
+            .reshape(length, local_width)
+            .astype(BF16)
+        )
     if fast:
         most = max(width, units)
         vectors = jnp.stack(
@@ -1096,16 +1280,9 @@
         second_part = jnp.einsum("tf,df->td", pre_grad, expand_weight, preferred_element_type=F32)
     shrink_bias_part = jnp.sum(upstream, axis=0)
     if fast:
-        places = jnp.arange(length)
-        off = jnp.where(
-            blocks[:, None] <= blocks[None, :], (places[:, None] - places[None, :]).astype(F32), -1e30
-        )
-        numbers = (first_head + jnp.arange(local_heads)).astype(F32)
-        slope = jnp.broadcast_to((2.0 ** (-8.0 * (numbers + 1.0) / H))[:, None], (local_heads, 128))
-        flat = [one.reshape(length, local_width) for one in (query, keys, vals)]
-        mlp_sum, weight_sums, resid_low, query_grad, keys_grad, vals_grad, sums_back = back_call(
+        mlp_sum, weight_sums, resid_low, grads, sums_back = back_call(
             n_tensor, second_part, partial_mlp, activ_low, cotangent, second_low, pre_grad, inputs, total,
-            vectors[:, :width], output_weight, *flat, logsum.reshape(local_heads, length), slope, off,
+            vectors[:, :width], output_weight, query, keys, vals, logsum, slope, off,
         )
         mlp_sum = mlp_sum.reshape(length, width).astype(F32)
         resid_low = resid_low.reshape(length, width)
@@ -1117,21 +1294,12 @@
         shrink_weight_grad = weight_sums[:pieces].astype(F32).reshape(units, width)
         expand_weight_grad = weight_sums[pieces:].astype(F32).reshape(width, units)
         outputs = (hidden_state + mlp_sum + shrink_bias).astype(BF16)
-        output_part = jnp.einsum("tc,td->cd", attended, resid_low, preferred_element_type=F32)
     else:
         shrink_part = jnp.einsum("tf,td->fd", activ_low, cotangent, preferred_element_type=F32)
         expand_part = jnp.einsum("td,tf->df", second_low, pre_grad, preferred_element_type=F32)
 
-        (second_grad, mlp_sum), (shrink_sum, expand_sum) = sums(
-            [second_part, partial_mlp],
-            [
-                shrink_part.reshape(-1, 2, 2, 2, 32, width),
-                expand_part.reshape(-1, 2, 2, 2, 32, units),
-            ],
-            1,
-        )
-        shrink_weight_grad = shrink_sum.reshape(units, width)
-        expand_weight_grad = expand_sum.reshape(width, units)
+        mlp_sum = lax.psum(partial_mlp.astype(BF16), "tensor").astype(F32)
+        second_grad = lax.psum(second_part.astype(BF16), "tensor").astype(F32)
         outputs = (hidden_state + mlp_sum + shrink_bias).astype(BF16)
         hidden_grad, second_gain_part, second_shift_part = norm_backward(
             hidden_state, second_gain, second_shift, second_grad
@@ -1160,66 +1328,71 @@
         keys_grad = (
             jnp.einsum("hqk,qhd->khd", score_grad, query, preferred_element_type=F32) * scale_factor
         ).astype(BF16)
-    grads = [one.reshape(length, local_width) for one in (query_grad, keys_grad, vals_grad)]
-    mixing_part = jnp.stack(
-        [jnp.einsum("td,tc->dc", normed_low, one, preferred_element_type=F32) for one in grads]
-    )
+        grads = [one.reshape(length, local_width) for one in (query_grad, keys_grad, vals_grad)]
     mixing_bias_part = jnp.stack(
         [jnp.sum(grads[0].astype(F32), axis=0), jnp.sum(grads[2].astype(F32), axis=0)]
     )
-    normed_part = sum(
-        jnp.einsum("tc,dc->td", one, weights[k], preferred_element_type=F32)
-        for k, one in enumerate(grads)
-    )
-    quarters = width // local_width
-    (normed_grad,), (mixing_sum, output_sum) = sums(
-        [normed_part],
-        [
-            mixing_part.reshape(-1, 2, 2, 2, 128, local_width),
-            output_part.reshape(local_width, quarters, local_width)
-            .transpose(1, 0, 2)
-            .reshape(-1, 2, 2, 2, 128, local_width),
-        ],
-        2,
-    )
-    mixing_weight_grad = mixing_sum.reshape(3, width, local_width).transpose(1, 0, 2)
-    output_weight_grad = (
-        output_sum.reshape(quarters, local_width, local_width)
-        .transpose(1, 0, 2)
-        .reshape(local_width, width)
-    )
-    source_grad, first_gain_part, first_shift_part = norm_backward(
-        source, first_gain, first_shift, normed_grad
-    )
-    input_grad = (source_grad + hidden_grad).astype(BF16)
-    small = lax.psum(
-        (
-            first_gain_part,
-            first_shift_part,
-            mixing_bias_part,
-            output_bias_part,
-            second_gain_part,
-            second_shift_part,
-            expand_bias_part,
-            shrink_bias_part,
-        ),
-        "dp",
-    )
+    if fast:
+        small = jnp.stack(
+            [
+                jnp.zeros_like(second_gain_part),
+                jnp.zeros_like(second_gain_part),
+                second_gain_part,
+                second_shift_part,
+                output_bias_part,
+                expand_bias_part,
+                shrink_bias_part,
+                jnp.pad(mixing_bias_part.reshape(-1), (0, width - 2 * local_width)),
+            ]
+        )
+        mixing_sum, output_sum, input_grad, small = front_call(
+            n_tensor, grads, weights, normed_low, attended, resid_low, inputs,
+            first_gain.reshape(1, width), small,
+        )
+        mixing_weight_grad = mixing_sum.reshape(3, width, local_width).astype(F32).transpose(1, 0, 2)
+        output_weight_grad = output_sum.reshape(local_width, width).astype(F32)
+        first_gain_grad, first_shift_grad, second_gain_grad, second_shift_grad = small[0], small[1], small[2], small[3]
+        output_bias_grad, expand_bias_grad, shrink_bias_grad = small[4], small[5], small[6]
+        mixing_bias_grad = small[7, : 2 * local_width].reshape(2, local_width)
+    else:
+        mixing_part = jnp.stack(
+            [jnp.einsum("td,tc->dc", normed_low, one, preferred_element_type=F32) for one in grads]
+        )
+        normed_part = sum(
+            jnp.einsum("tc,dc->td", one, weights[k], preferred_element_type=F32)
+            for k, one in enumerate(grads)
+        )
+        normed_grad = lax.psum(normed_part.astype(BF16), "tensor").astype(F32)
+        source_grad, first_gain_part, first_shift_part = norm_backward(
+            source, first_gain, first_shift, normed_grad
+        )
+        input_grad = (source_grad + hidden_grad).astype(BF16)
+        summed = lax.psum(
+            (
+                first_gain_part, first_shift_part, mixing_part, mixing_bias_part, output_part, output_bias_part,
+                second_gain_part, second_shift_part, expand_part, expand_bias_part, shrink_part, shrink_bias_part,
+            ),
+            "dp",
+        )
+        first_gain_grad, first_shift_grad, mixing_weight_grad, mixing_bias_grad = summed[:4]
+        mixing_weight_grad = mixing_weight_grad.transpose(1, 0, 2)
+        output_weight_grad, output_bias_grad, second_gain_grad, second_shift_grad = summed[4:8]
+        expand_weight_grad, expand_bias_grad, shrink_weight_grad, shrink_bias_grad = summed[8:]
     return (
         outputs,
         input_grad,
-        small[0],
-        small[1],
+        first_gain_grad,
+        first_shift_grad,
         mixing_weight_grad,
-        small[2],
+        mixing_bias_grad,
         output_weight_grad,
-        small[3],
-        small[4],
-        small[5],
+        output_bias_grad,
+        second_gain_grad,
+        second_shift_grad,
         expand_weight_grad,
-        small[6],
+        expand_bias_grad,
         shrink_weight_grad,
-        small[7],
+        shrink_bias_grad,
     )
 
 
@@ -1258,7 +1431,7 @@
         P(),
     )
     n_tensor = mesh.shape["tensor"]
-    fast = mesh.shape["dp"] == 8 and n_tensor % 2 == 0
+    fast = mesh.shape["dp"] == 8 and n_tensor in (2, 4)
     return jax.shard_map(
         functools.partial(on_device, fast, n_tensor),
         mesh=mesh,

time: 537 us -> 462 us (0.86)
  matrix products: 45.3 us -> 0 us
  Pallas kernels: 377 us -> 414 us
  blocking collectives: 25.2 us -> 0 us
  other arithmetic: 59.7 us -> 35.2 us
  local copies, waits for them, and re-layouts: 23.7 us -> 11.8 us
    pallas_call x1 -> x2, Pallas kernels: 97.1 us -> 147 us  [the longest x1 106 us: front_call(): pl.pallas_call(functools.partial(front_kernel, n), out_shape=[jax.ShapeDt...]
    dot_general x12 -> x0, matrix products: 45.3 us -> none  [the longest x3 10.8 us: on_device(): jnp.einsum('tc,dc->td', one, weights[k], preferred_element_type=F32)]
    psum x1 -> x0, blocking collectives: 25.2 us -> none  [on_device(): lax.psum((first_gain_part, first_shift_part, mixing_bias_part, output_bia...]
    reduce_sum x7 -> x1, other arithmetic: 17.9 us -> 0.26 us  [on_device(): jnp.sum(grads[0].astype(F32), axis=0)]
    pallas_call x1, Pallas kernels: 174 us -> 161 us  [back_call(): pl.pallas_call(functools.partial(back_kernel, n, q.shape[1] // HD), out_s...]
    convert_element_type x4 -> x0, local copies, waits for them, and re-layouts: 6.91 us -> none  [the longest x1 2.29 us: on_device(): (project(2) + mixing_bias[1]).astype(BF16).reshape(length, local_heads, HD)]
    convert_element_type x3 -> x2, other arithmetic: 12.1 us -> 9.54 us  [the longest x1 6.86 us: on_device(): outputs = (hidden_state + mlp_sum + shrink_bias).astype(BF16)]
where the time goes in v3:
time: 462 us
  Pallas kernels  414 us (90%)
  other arithmetic  35.2 us (8%)
  local copies, waits for them, and re-layouts  11.8 us (3%)
    pallas_call x1, Pallas kernels, back_call(): pl.pallas_call(functools.partial(back_kernel, n, q.shape[1] // HD), out_s...  161 us
    pallas_call x1, Pallas kernels, front_call(): pl.pallas_call(functools.partial(front_kernel, n), out_shape=[jax.ShapeDt...  106 us
    pallas_call x1, Pallas kernels, mlp_call(): pl.pallas_call(functools.partial(mlp_kernel, n, length), out_shape=out_sh...  106 us
    pallas_call x1, Pallas kernels, head_call(): pl.pallas_call(functools.partial(head_kernel, heads), out_shape=[jax.Shap...  40.4 us
    reshape x1, other arithmetic, on_device(): shrink_weight_grad = weight_sums[:pieces].astype(F32).reshape(units, width)  12.6 us
    transpose x1, other arithmetic, on_device(): mixing_sum.reshape(3, width, local_width).astype(F32).transpose(1, 0, 2)  9.52 us

profile of v3, /device:TPU:0, one launch (start us, length us, event | category | flops | bytes accessed | tf_op | source)
XLA Modules:
  0.0 461.7 jit_solution(17515259492303626580)
XLA Ops:
  0.6 0.0 copy-start.8
  0.7 0.0 copy-start.12
  0.7 0.0 copy-start.11
  0.7 0.0 copy-start.10
  0.7 0.8 fusion.5
  1.5 0.1 pad.12.clone
  1.5 0.7 pad_maximum_fusion.2.refs_3_
  2.2 1.3 pad_maximum_fusion.1.refs_2_
  3.5 0.7 broadcast_in_dim.2.refs_4_.refs_14_
  4.2 40.4 %shard_map.254 = (bf16[768,2048]{1,0:T(8,128)(2,1)}, bf16[768,512]{1,0:T(8,128)(2,1)}, bf16[768,512]{1,0:T(8,128)(2,1)}, bf16[768,512]{1,0:T(8,128)(2,1)}, bf16[...) custom-call(bf16[768,2048]{1,0:T(8,128)(2,1)} %refs_5_.5, bf16[3,2048,512]{2,1,0:T(8,128)(2,1)} %bitcast.51, ...), custom_call_target="tpu_custom_call" | custom-call | tf_op jit(solution)/shard_map/pallas_call | solution.py:275
  44.6 0.0 copy-done.8
  44.7 0.0 copy-done.12
  44.7 0.0 copy-done.11
  44.7 0.0 copy-done.10
  44.7 0.7 pad_maximum_fusion.refs_6_.refs_8_
  45.3 106.1 %shard_map.255 = (bf16[24,32,2048]{2,1,0:T(8,128)(2,1)}, bf16[768,2048]{1,0:T(8,128)(2,1)}, bf16[768,2048]{1,0:T(8,128)(2,1)}, bf16[768,2048]{1,0:T(8,128)(2,1)}...) custom-call(bf16[768,512]{1,0:T(8,128)(2,1)} %get-tuple-element.37.refs_0_.refs_3_, ...), custom_call_target="tpu_custom_call" | custom-call | tf_op jit(solution)/shard_map/pallas_call | solution.py:467
  151.5 161.1 %shard_map.256 = (bf16[16,48,2048]{2,1,0:T(8,128)(2,1)}, bf16[16,2,2,2,32,2048]{5,4,3,2,1,0:T(8,128)(2,1)}, bf16[16,48,2048]{2,1,0:T(8,128)(2,1)}, bf16[3,768,512]{2,1,0:T(8,128)(2,1)}, f32[3,8,2048]{2,1,0:T(8,128)}) custom-call(bf16[16,48,2048]{2,1,0:T(8,128)(2,1)} %bitcast.56, bf16[16,48,2048]{2,1,0:T(8,128)(2,1)} %bitcast.55, ...), custom_call_target="tpu_custom_call" | custom-call | tf_op jit(solution)/shard_map/pallas_call | solution.py:960
  312.5 6.6 %fusion.3 = (bf16[8,2,2,2,32,2048]{5,4,3,2,1,0:T(8,128)(2,1)S(1)}, bf16[8,2,2,2,32,2048]{5,4,3,2,1,0:T(8,128)(2,1)S(1)}) fusion(bf16[16,2,2,2,32,2048]{5,4,3,2,1,0:T(8,128)(2,1)} %get-tuple-element.59), kind=kLoop, calls=%fused_computation.21 | loop fusion | bytes 33554432 | tf_op jit(solution)/shard_map/slice | solution.py:1294
  319.1 0.0 copy-start.2
  319.1 0.0 copy-start.5
  319.1 0.0 copy-start.6
  319.2 0.0 copy-start.1
  319.2 12.6 %bitcast_convert_fusion = (f32[2048,2048]{1,0:T(8,128)}, f32[2048,2048]{1,0:T(8,128)}) fusion(bf16[8,2,2,2,32,2048]{5,4,3,2,1,0:T(8,128)(2,1)S(1)} %get-tuple-element.65, bf16[8,2,2,2,32,2048]{5,4,3,2,1,0:T(8,128)(2,1)S(1)} %get-tuple-element.66), kind=kLoop, calls=%fused_computation.1 | loop fusion | flops 8388608 | bytes 50331648 | tf_op jit(solution)/shard_map/reshape | solution.py:1294
  331.8 0.0 copy-done.2
  331.8 0.3 convert_reduce_fusion.2
  332.1 0.0 copy-done.5
  332.1 0.1 slice_reduce_fusion
  332.1 0.0 copy-done.6
  332.2 0.0 copy-done.1
  332.2 0.5 convert_reduce_fusion
  332.7 0.7 stack.79.refs_7_
  333.4 106.3 %shard_map.257 = (bf16[12,2,2,2,64,512]{5,4,3,2,1,0:T(8,128)(2,1)}, bf16[2,2,2,64,2048]{4,3,2,1,0:T(8,128)(2,1)}, bf16[768,2048]{1,0:T(8,128)(2,1)}, f32[8,2048]{1,0:T(8,128)}) custom-call(bf16[3,768,512]{2,1,0:T(8,128)(2,1)} %get-tuple-element.50.refs_0_, bf16[3,2048,512]{2,1,0:T(8,128)(2,1)} %bitcast.52, bf16[768,2048]{1,0:T(8,128)(2,1)} %get-tuple-element.51.refs_2_, ...), custom_call_target="tpu_custom_call" | custom-call | tf_op jit(solution)/shard_map/pallas_call | solution.py:1190
  439.7 0.0 copy-start.4
  439.7 9.5 %convert_bitcast_fusion = f32[2048,3,512]{2,0,1:T(8,128)} fusion(bf16[3,2048,512]{2,1,0:T(8,128)(2,1)} %bitcast.54), kind=kLoop, calls=%fused_computation | loop fusion | flops 3145728 | bytes 18874368 | tf_op jit(solution)/shard_map/transpose | solution.py:1352
  449.2 0.0 copy-start.7
  449.2 0.0 copy-start
  449.2 0.0 copy-start.9
  449.2 0.0 copy-done.4
  449.2 2.7 bitcast_convert_fusion.2
  451.9 0.0 copy-done.7
  451.9 0.6 fusion.4
  452.6 0.6 reshape_squeeze.3
  453.2 0.0 copy-done
  453.2 0.0 copy-done.9
  453.2 0.0 copy-start.3
  453.2 6.9 %fusion.1 = bf16[768,2048]{1,0:T(8,128)(2,1)} fusion(bf16[768,2048]{1,0:T(8,128)(2,1)S(1)} %copy-done, bf16[16,48,2048]{2,1,0:T(8,128)(2,1)} %get-tuple-element.49, bf16[24,32,2048]{2,1,0:T(8,128)(2,1)} %get-tuple-element.38, f32[2048]{0:T(1024)S(1)} %copy-done.9, f32[2048]{0:T(1024)S(1)} %copy-done.8), kind=kLoop, calls=%fused_computation.5 | loop fusion | flops 12582912 | bytes 12599296 | tf_op jit(solution)/shard_map/convert_element_type | solution.py:1296
  460.1 0.0 copy-done.3
  460.1 1.7 copy.31
  (7 shorter events, 0.1 us)
Async XLA Ops:
  0.6 44.0 %copy-start.8 = (f32[2048]{0:T(1024)S(1)}, f32[2048]{0:T(1024)}, u32[]{:S(2)}) copy-start(f32[2048]{0:T(1024)} %param.22) | copy-start | bytes 24580
  0.7 44.0 %copy-start.12 = (f32[2048]{0:T(1024)S(1)}, f32[2048]{0:T(1024)}, u32[]{:S(2)}) copy-start(f32[2048]{0:T(1024)} %param.23) | copy-start | bytes 24580
  0.7 44.0 %copy-start.11 = (f32[2048]{0:T(1024)S(1)}, f32[2048]{0:T(1024)}, u32[]{:S(2)}) copy-start(f32[2048]{0:T(1024)} %param.24) | copy-start | bytes 24580
  0.7 44.0 %copy-start.10 = (f32[2048]{0:T(1024)S(1)}, f32[2048]{0:T(1024)}, u32[]{:S(2)}) copy-start(f32[2048]{0:T(1024)} %param.26) | copy-start | bytes 24580
  319.1 12.6 %copy-start.2 = (bf16[3,768,512]{2,1,0:T(8,128)(2,1)S(1)}, bf16[3,768,512]{2,1,0:T(8,128)(2,1)}, u32[]{:S(2)}) copy-start(bf16[3,768,512]{2,1,0:T(8,128)(2,1)} %get-tuple-element.50.refs_0_) | copy-start | bytes 7077892
  319.1 12.9 %copy-start.5 = (f32[3,8,2048]{2,1,0:T(8,128)S(1)}, f32[3,8,2048]{2,1,0:T(8,128)}, u32[]{:S(2)}) copy-start(f32[3,8,2048]{2,1,0:T(8,128)} %get-tuple-element.53) | copy-start | bytes 589828
  319.1 13.0 %copy-start.6 = (f32[8,2048]{1,0:T(8,128)S(1)}, f32[8,2048]{1,0:T(8,128)}, u32[]{:S(2)}) copy-start(f32[8,2048]{1,0:T(8,128)} %get-tuple-element.54) | copy-start | bytes 196612
  319.2 13.0 %copy-start.1 = (bf16[768,2048]{1,0:T(8,128)(2,1)S(1)}, bf16[768,2048]{1,0:T(8,128)(2,1)}, u32[]{:S(2)}) copy-start(bf16[768,2048]{1,0:T(8,128)(2,1)} %refs_3_.3) | copy-start | bytes 9437188
  439.7 9.5 %copy-start.4 = (bf16[2,2,2,64,2048]{4,3,2,1,0:T(8,128)(2,1)S(1)}, bf16[2,2,2,64,2048]{4,3,2,1,0:T(8,128)(2,1)}, u32[]{:S(2)}) copy-start(bf16[2,2,2,64,2048]{4,3,2,1,0:T(8,128)(2,1)} %get-tuple-element.58) | copy-start | bytes 6291460
  449.2 2.7 copy-start.7
  449.2 4.0 copy-start
  449.2 4.0 copy-start.9
  453.2 6.9 %copy-start.3 = (bf16[768,2048]{1,0:T(8,128)(2,1)S(1)}, bf16[768,2048]{1,0:T(8,128)(2,1)}, u32[]{:S(2)}) copy-start(bf16[768,2048]{1,0:T(8,128)(2,1)} %get-tuple-element.93) | copy-start | bytes 9437188

commit v4 on v3

--- a/solution.py
+++ b/solution.py
@@ -681,43 +681,66 @@
             to[:, lanes] += (got[...] * factor).astype(BF16)
 
 
-BACK_ROWS = 48
+ROWS_BACK = 48
 BACK_SLOTS = 12
 BACK_SLACK = 2
 BACK_APART = 2
 BACK_COLUMNS = 1024
 HEAD_TILE = 256
+PIECE = 256
+GROUP = 4
 
 
 def back_kernel(n, heads, *refs):
-    (grad_h, mlp_h, activ_h, dy_h, second_h, pre_h, src_h, tot_h), refs = refs[:8], refs[8:]
+    (grad_h, mlp_h, activ_h, dy_h, second_h, pre_h, src_h, tot_h, w_h, normed_h, att_h, eb_h), refs = refs[:12], refs[12:]
     smalls_h, refs = refs[:8], refs[8:]
-    (sum_h, g_out, resid_h, grads_h, cols_h), refs = refs[:5], refs[5:]
-    (left, dy, pre, src, tot, resid), refs = refs[:6], refs[6:]
+    (out_h, shrink_out, expand_out, wo_out, mix_out, input_h, small_out), refs = refs[:7], refs[7:]
+    (left, dy, pre, src, tot, out, resid, w, att, eb), refs = refs[:10], refs[10:]
     smalls, refs = refs[:8], refs[8:]
     vec, wo, q, k, v, lse, slope, off = smalls
-    (up, qg, kg, vg, k_acc, v_acc, cols), refs = refs[:7], refs[7:]
-    (load, left_sem, part_sem, row_sem, resid_sem, sum_sem), refs = refs[:6], refs[6:]
+    (up, grads, k_acc, v_acc, cols, buf, got_small), refs = refs[:7], refs[7:]
+    (load, left_sem, part_sem, row_sem, out_sem, ss, sq), refs = refs[:7], refs[7:]
     ring, refs = Ring(n, refs[:7], BACK_SLOTS, BACK_SLACK), refs[7:]
     chain = ring.chain
-
-    per_row = dy_h.shape[1] // BACK_COLUMNS
-
-    def keep(k, piece_ref, sem):
-        here = pl.ds(pl.multiple_of(lax.rem(k, per_row) * BACK_COLUMNS, BACK_COLUMNS), BACK_COLUMNS)
-        pltpu.make_async_copy(piece_ref, g_out.at[k // per_row, :, :, :, :, here], sem).start()
-
-    cube = Cube(refs, keep, 32, BACK_APART)
-    width, units = dy.shape[1], pre.shape[1]
-    rows, per_sum = BACK_ROWS, grad_h.shape[0]
-    total_z = 2 * per_sum
-    piece = 256
-    first = activ_h.shape[1] // piece
-    total_left = first + second_h.shape[1] // piece
-    total_p = total_left * per_row
+    width, local = dy.shape[1], q.shape[1]
+    rows, per_sum = ROWS_BACK, grad_h.shape[0]
+    loaded_z, total_z = 2 * per_sum, 3 * per_sum
+    per_row = width // BACK_COLUMNS
+    first = activ_h.shape[1] // PIECE
+    total_left = first + second_h.shape[1] // PIECE
+    to_output = total_left * per_row
+    to_mixing = to_output + local // PIECE * per_row
+    pair = BACK_COLUMNS // local
+    per_matrix = width // PIECE // pair
+    total_p = to_mixing + 3 * per_matrix
+
+    def keep(p, piece_ref, sem):
+        here = pl.ds(pl.multiple_of(lax.rem(p, per_row) * BACK_COLUMNS, BACK_COLUMNS), BACK_COLUMNS)
+        for lo, hi, to in (
+            (0, first * per_row, shrink_out),
+            (first * per_row, to_output, expand_out),
+            (to_output, to_mixing, wo_out),
+        ):
+
+            @pl.when(jnp.logical_and(p >= lo, p < hi))
+            def _(lo=lo, to=to):
+                pltpu.make_async_copy(piece_ref, to.at[(p - lo) // per_row, :, :, :, :, here], sem).start()
+
+        @pl.when(p >= to_mixing)
+        def _():
+            i = p - to_mixing
+            for j in range(pair):
+                pltpu.make_async_copy(
+                    piece_ref.at[:, :, :, :, pl.ds(j * local, local)],
+                    mix_out.at[i // per_matrix, lax.rem(i, per_matrix) * pair + j],
+                    sem,
+                ).start()
+
+    cube = Cube(refs, keep, PIECE // 8, BACK_APART)
 
     loads = [pltpu.make_async_copy(a, b, load.at[j]) for j, (a, b) in enumerate(zip(smalls_h, smalls))]
-    loads += [pltpu.make_async_copy(dy_h, dy, load.at[8]), pltpu.make_async_copy(pre_h, pre, load.at[9])]
+    pairs = ((dy_h, dy), (pre_h, pre), (w_h, w), (att_h, att), (eb_h, eb), (normed_h, dy))
+    loads += [pltpu.make_async_copy(a, b, load.at[8 + j]) for j, (a, b) in enumerate(pairs)]
 
     def part_load(j, which):
         return pltpu.make_async_copy(
@@ -733,288 +756,114 @@
         def _():
             part_load(j, 1).start()
 
-    def left_load(p, which):
-        at = (p - which * first) * piece
+    def left_load(r, which):
+        at = (r - which * first) * PIECE
         return pltpu.make_async_copy(
-            (activ_h, second_h)[which].at[:, pl.ds(pl.multiple_of(at, piece), piece)],
-            left.at[lax.rem(p, 2)],
-            left_sem.at[lax.rem(p, 2)],
-        )
-
-    def left_start(p):
-        @pl.when(p < first)
-        def _():
-            left_load(p, 0).start()
-
-        @pl.when(between(p - first, total_left - first))
-        def _():
-            left_load(p, 1).start()
+            (activ_h, second_h)[which].at[:, pl.ds(pl.multiple_of(at, PIECE), PIECE)],
+            left.at[lax.rem(r, 2)],
+            left_sem.at[lax.rem(r, 2)],
+        )
+
+    def left_start(r):
+        @pl.when(r < first)
+        def _():
+            left_load(r, 0).start()
+
+        @pl.when(between(r - first, total_left - first))
+        def _():
+            left_load(r, 1).start()
 
     def row_loads(j):
+        at, chunk = lax.rem(j, 2), lax.rem(j, per_sum)
+        return (
+            pltpu.make_async_copy(src_h.at[chunk], src.at[at], row_sem.at[at, 0]),
+            pltpu.make_async_copy(tot_h.at[chunk], tot.at[at], row_sem.at[at, 1]),
+        )
+
+    def out_store(j, to):
         at = lax.rem(j, 2)
-        return (
-            pltpu.make_async_copy(src_h.at[j], src.at[at], row_sem.at[at, 0]),
-            pltpu.make_async_copy(tot_h.at[j], tot.at[at], row_sem.at[at, 1]),
-        )
-
-    def resid_store(j):
-        at = lax.rem(j, 2)
-        return pltpu.make_async_copy(resid.at[at], resid_h.at[j], resid_sem.at[at])
-
-    def sum_store(j):
-        at = ring.at(j)
-        return pltpu.make_async_copy(chain.inner_in.at[at], sum_h.at[j - per_sum], sum_sem.at[at])
+        return pltpu.make_async_copy(out.at[at], to.at[lax.rem(j, per_sum)], out_sem.at[at])
 
     part_start(0)
     left_start(0)
     loads[8].start()
     part_start(1)
-    for one in loads[:8] + loads[9:]:
+    for one in loads[:8] + [loads[9]]:
         one.start()
     barrier = pltpu.get_barrier_semaphore()
     chain.greet(barrier)
     cube.greet(barrier)
     cols[...] = jnp.zeros_like(cols)
+    buf[...] = jnp.zeros_like(buf)
     chain.wait_greetings(barrier, 3)
     loads[8].wait()
 
+    def product(p, columns, right):
+        to = cube.slot(p)
+        count = PIECE // 8
+        for side, store in ((1 - cube.c, cube.give.at[to]), (cube.c, cube.fin.at[to, cube.c])):
+            for j in range(BACK_COLUMNS // 512):
+                got = weighted(columns(j, side), right(j))
+                for a in range(2):
+                    for b in range(2):
+                        lo = (2 * a + b) * count
+                        store[a, b, :, j * 512 : (j + 1) * 512] = got[lo : lo + count]
+
+    half = PIECE // 2
+
     def produce(p):
         r, part = p // per_row, lax.rem(p, per_row)
-        at = lax.rem(r, 2)
-        to = cube.slot(p)
-
-        @pl.when(part == 0)
-        def _():
-            left_start(r + 1)
-            pltpu.make_async_copy(activ_h.at[:, pl.ds(0, piece)], left.at[at], left_sem.at[at]).wait()
-
-        mine, theirs = cube.c, 1 - cube.c
-        count = piece // 8
-
-        def product(right):
-            for side, store in ((theirs, cube.give.at[to]), (mine, cube.fin.at[to, cube.c])):
-                rows_of = left[at, :, pl.ds(pl.multiple_of(side * (piece // 2), piece // 2), piece // 2)]
-                for j in range(BACK_COLUMNS // 512):
-                    from_here = pl.ds(pl.multiple_of(part * BACK_COLUMNS + j * 512, 512), 512)
-                    got = weighted(rows_of, right[:, from_here])
-                    for a in range(2):
-                        for b in range(2):
-                            lo = (2 * a + b) * count
-                            store[a, b, :, j * 512 : (j + 1) * 512] = got[lo : lo + count]
-
-        @pl.when(r < first)
-        def _():
-            product(dy)
-
-        @pl.when(r >= first)
-        def _():
-            product(pre)
+
+        @pl.when(r < total_left)
+        def _():
+            at = lax.rem(r, 2)
+
+            @pl.when(part == 0)
+            def _():
+                left_start(r + 1)
+                pltpu.make_async_copy(activ_h.at[:, pl.ds(0, PIECE)], left.at[at], left_sem.at[at]).wait()
+
+            def columns(j, side):
+                return left[at, :, pl.ds(pl.multiple_of(side * half, half), half)]
+
+            for which, ref in enumerate((dy, pre)):
+
+                def right(j, ref=ref):
+                    return ref[:, pl.ds(pl.multiple_of(part * BACK_COLUMNS + j * 512, 512), 512)]
+
+                @pl.when((r >= first) == bool(which))
+                def _(right=right):
+                    product(p, columns, right)
+
+        @pl.when(between(p - to_output, to_mixing - to_output))
+        def _():
+            tile = r - total_left
+
+            def columns(j, side):
+                return att[:, pl.ds(pl.multiple_of(tile * PIECE + side * half, half), half)]
+
+            def right(j):
+                return resid[:, pl.ds(pl.multiple_of(part * BACK_COLUMNS + j * 512, 512), 512)]
+
+            product(p, columns, right)
+
+        @pl.when(p >= to_mixing)
+        def _():
+            i = p - to_mixing
+            tile = lax.rem(i, per_matrix) * pair
+
+            def columns(j, side):
+                return dy[:, pl.ds(pl.multiple_of((tile + j) * PIECE + side * half, half), half)]
+
+            def right(j):
+                return grads[i // per_matrix]
+
+            product(p, columns, right)
 
         cube.half(p).start()
 
-    def row_sum(x):
-        return jnp.sum(x, axis=-1, keepdims=True)
-
-    def rows_back(j):
-        for one in row_loads(j):
-            one.wait()
-        at, got = lax.rem(j, 2), ring.at(j)
-        step = 16
-
-        def body(i, carry):
-            here = pl.ds(pl.multiple_of(i * step, step), step)
-            value = src[at, here, :].astype(F32) + (tot[at, here, :].astype(F32) + vec[0:1, :])
-            centred = value - row_sum(value) / width
-            spread = lax.rsqrt(row_sum(centred * centred) / width + EPS)
-            normal = centred * spread
-            down = chain.inner_in[got, here, :].astype(F32)
-            scaled = down * vec[1:2, :]
-            flat, slope_of = row_sum(scaled) / width, row_sum(scaled * normal) / width
-            back = spread * (scaled - flat - normal * slope_of)
-            all_rows = pl.ds(pl.multiple_of(j * rows + i * step, step), step)
-            low = (back + dy[all_rows, :].astype(F32)).astype(BF16)
-            resid[at, here, :] = low
-            for c, item in enumerate((down * normal, down, low.astype(F32))):
-                cols[c] += item[0:8] + item[8:16]
-            return carry
-
-        lax.fori_loop(0, rows // step, body, 0)
-        all_rows = pl.ds(pl.multiple_of(j * rows, rows), rows)
-        up[all_rows, :] = lax.dot_general(
-            resid[at], wo[...], (((1,), (1,)), ((), ())), preferred_element_type=F32
-        ).astype(BF16)
-        resid_store(j).start()
-
-    def tick(t, carry):
-        gone = t - ring.gone
-
-        @pl.when(between(gone, total_z))
-        def _():
-            ring.retire(gone)
-
-            @pl.when(gone >= per_sum)
-            def _():
-                sum_store(gone).wait()
-
-        part_start(t + 2)
-        ready = t - chain.first
-
-        @pl.when(between(ready, total_z))
-        def _():
-            part_load(ready, 0).wait()
-            ring.reduce(ready)
-
-        back = t - chain.lag
-
-        @pl.when(between(back, total_z))
-        def _():
-            ring.spread(back)
-
-            @pl.when(back >= per_sum)
-            def _():
-                sum_store(back).start()
-
-        cube.tick(t, total_p)
-
-        @pl.when(t == 2)
-        def _():
-            for one in loads[:8] + loads[9:]:
-                one.wait()
-
-        @pl.when(t < total_p)
-        def _():
-            produce(t)
-
-        chunk = t - chain.most_lag - 1
-
-        @pl.when(between(chunk + 1, per_sum))
-        def _():
-            for one in row_loads(chunk + 1):
-                one.start()
-
-        @pl.when(between(chunk - 2, per_sum))
-        def _():
-            resid_store(chunk - 2).wait()
-
-        @pl.when(between(chunk, per_sum))
-        def _():
-            rows_back(chunk)
-
-        head = t - chain.most_lag - 1 - per_sum
-
-        @pl.when(between(head, heads))
-        def _():
-            head_backward(head, q, k, v, up, lse, slope, off, HEAD_TILE, (qg, kg, vg), (k_acc, v_acc))
-
-        return carry
-
-    ticks = max(total_z + ring.gone, total_p + cube.gone, chain.most_lag + 1 + per_sum + max(heads, 2))
-    lax.fori_loop(0, ticks, tick, 0)
-    stores = [
-        pltpu.make_async_copy(a, b, load.at[j])
-        for j, (a, b) in enumerate(((qg, grads_h.at[0]), (kg, grads_h.at[1]), (vg, grads_h.at[2]), (cols, cols_h)))
-    ]
-    for one in stores:
-        one.start()
-    for one in stores:
-        one.wait()
-
-
-def back_call(n, grad, mlp, activ, dy, second, pre, src, tot, vec, wo, q, k, v, lse, slope, off):
-    length, width = dy.shape
-    chunks = length // BACK_ROWS
-    dma = pltpu.SemaphoreType.DMA
-
-    def cut(one):
-        return one.reshape(chunks, BACK_ROWS, one.shape[-1])
-
-    smalls = (vec, wo, q, k, v, lse, slope, off)
-    inputs = (cut(grad), cut(mlp), activ, dy, second, pre, cut(src), cut(tot), *smalls)
-    tiles = (activ.shape[1] + second.shape[1]) // 256
-    shapes = [
-        ((chunks, BACK_ROWS, width), BF16),
-        ((tiles, 2, 2, 2, 32, width), BF16),
-        ((chunks, BACK_ROWS, width), BF16),
-        ((3, *q.shape), BF16),
-        ((3, 8, width), F32),
-    ]
-    slots = BACK_SLOTS
-    scratch = [
-        pltpu.VMEM((2, length, 256), BF16),
-        pltpu.VMEM(dy.shape, BF16),
-        pltpu.VMEM(pre.shape, BF16),
-        *[pltpu.VMEM((2, BACK_ROWS, width), BF16)] * 3,
-        *[pltpu.VMEM(one.shape, one.dtype) for one in smalls],
-        *[pltpu.VMEM(q.shape, BF16)] * 4,
-        *[pltpu.VMEM((length, 2 * HD), F32)] * 2,
-        pltpu.VMEM((3, 8, width), F32),
-        dma((10,)),
-        dma((2,)),
-        dma((slots,)),
-        dma((2, 2)),
-        dma((2,)),
-        dma((slots,)),
-        *Chain.scratch(slots, (BACK_ROWS, width)),
-        *Cube.scratch((32, BACK_COLUMNS), BACK_APART),
-    ]
-    return pl.pallas_call(
-        functools.partial(back_kernel, n, q.shape[1] // HD),
-        out_shape=[jax.ShapeDtypeStruct(*one) for one in shapes],
-        in_specs=[pl.BlockSpec(memory_space=pl.ANY)] * len(inputs),
-        out_specs=[pl.BlockSpec(memory_space=pl.ANY)] * len(shapes),
-        scratch_shapes=scratch,
-        compiler_params=pltpu.CompilerParams(
-            collective_id=1, has_side_effects=True, vmem_limit_bytes=60 << 20
-        ),
-    )(*inputs)
-
-
-FRONT_ROWS = 48
-
-
-def front_kernel(n, *refs):
-    (grads_h, w_h, normed_h, att_h, resid_h, src_h, gain_h, small_h), refs = refs[:8], refs[8:]
-    (mix_out, wo_out, input_h, small_out), refs = refs[:4], refs[4:]
-    (grads, w, normed, att, resid, src, gain, cols, buf, got), refs = refs[:10], refs[10:]
-    (load, row_sem, ss, sq), refs = refs[:4], refs[4:]
-    chain, refs = Chain(n, refs[:7], FRONT_SLACK), refs[7:]
-    length, width = src.shape
-    local = att.shape[1]
-    blocks = width // local
-    rows = FRONT_ROWS
-    chunks = length // rows
-    group = 4
-    total_p = 4 * blocks
-
-    def keep(k, piece_ref, sem):
-        @pl.when(k < blocks)
-        def _():
-            at = pl.ds(pl.multiple_of(k * local, local), local)
-            pltpu.make_async_copy(piece_ref, wo_out.at[:, :, :, :, at], sem).start()
-
-        @pl.when(k >= blocks)
-        def _():
-            pltpu.make_async_copy(piece_ref, mix_out.at[k - blocks], sem).start()
-
-    cube = Cube(refs, keep, 32, FRONT_APART)
-
-    pairs = (
-        (grads_h, grads), (w_h, w), (att_h, att), (resid_h, resid), (normed_h, normed), (src_h, src),
-        (gain_h, gain), (small_h, buf.at[0]),
-    )
-    loads = [pltpu.make_async_copy(a, b, load.at[j]) for j, (a, b) in enumerate(pairs)]
-    for one in loads:
-        one.start()
-    barrier = pltpu.get_barrier_semaphore()
-    chain.greet(barrier)
-    cube.greet(barrier)
-    cols[...] = jnp.zeros_like(cols)
-    chain.wait_greetings(barrier, 3)
-    for one in loads[:2]:
-        one.wait()
-
     def produce_rows(g):
-        at = pl.ds(pl.multiple_of(g * group * rows, group * rows), group * rows)
+        at = pl.ds(pl.multiple_of(g * GROUP * rows, GROUP * rows), GROUP * rows)
         for j in range(width // 512):
             here = pl.ds(j * 512, 512)
             total = sum(
@@ -1023,178 +872,255 @@
                 )
                 for m in range(3)
             ).astype(BF16)
-            for q in range(group):
-                chain.part[g * group + q, :, here] = total[q * rows : (q + 1) * rows]
-
-    half = local // 2
-    count = half // 4
-
-    def put(to, side, value):
-        for a in range(2):
-            for b in range(2):
-                lo = (2 * a + b) * count
-                to[a, b] = value[lo : lo + count]
-
-    def produce(p):
-        slot = cube.slot(p)
-        for side, to in ((1 - cube.c, cube.give.at[slot]), (cube.c, cube.fin.at[slot, cube.c])):
-
-            @pl.when(p < blocks)
-            def _(side=side, to=to):
-                left = att[:, pl.ds(pl.multiple_of(side * half, half), half)]
-                right = resid[:, pl.ds(pl.multiple_of(p * local, local), local)]
-                put(to, side, weighted(left, right))
-
-            @pl.when(p >= blocks)
-            def _(side=side, to=to):
-                m, r = p // blocks - 1, lax.rem(p, blocks)
-                left = normed[:, pl.ds(pl.multiple_of(r * local + side * half, half), half)]
-                put(to, side, weighted(left, grads[m]))
-
-        cube.half(p).start()
+            for i in range(GROUP):
+                chain.part[ring.at(loaded_z + g * GROUP + i), :, here] = total[i * rows : (i + 1) * rows]
 
     def row_sum(x):
         return jnp.sum(x, axis=-1, keepdims=True)
 
-    def row_store(j):
-        at = pl.ds(pl.multiple_of(j * rows, rows), rows)
-        return pltpu.make_async_copy(src.at[at], input_h.at[at], row_sem.at[j])
+    def norm_back(value, down, gain):
+        centred = value - row_sum(value) / width
+        spread = lax.rsqrt(row_sum(centred * centred) / width + EPS)
+        normal = centred * spread
+        scaled = down * gain
+        flat, slope_of = row_sum(scaled) / width, row_sum(scaled * normal) / width
+        return normal, spread * (scaled - flat - normal * slope_of)
+
+    def each_rows(j, what):
+        step = 16
+
+        def body(i, carry):
+            what(
+                pl.ds(pl.multiple_of(i * step, step), step),
+                pl.ds(pl.multiple_of(lax.rem(j, per_sum) * rows + i * step, step), step),
+            )
+            return carry
+
+        lax.fori_loop(0, rows // step, body, 0)
+
+    def gather(start, *items):
+        for c, item in enumerate(items):
+            cols[start + c] += item[0:8] + item[8:16]
+
+    def hidden_rows(at, here):
+        return src[at, here, :].astype(F32) + (tot[at, here, :].astype(F32) + vec[0:1, :])
 
     def rows_back(j):
-        step = 16
-
-        def body(i, carry):
-            here = pl.ds(pl.multiple_of(i * step, step), step)
-            at = pl.ds(pl.multiple_of(j * rows + i * step, step), step)
-            value = src[at, :].astype(F32)
-            centred = value - row_sum(value) / width
-            spread = lax.rsqrt(row_sum(centred * centred) / width + EPS)
-            normal = centred * spread
-            down = chain.inner_in[j, here, :].astype(F32)
-            scaled = down * gain[0:1, :]
-            flat, slope_of = row_sum(scaled) / width, row_sum(scaled * normal) / width
-            back = spread * (scaled - flat - normal * slope_of)
-            src[at, :] = (back + resid[at, :].astype(F32)).astype(BF16)
-            for c, item in enumerate((down * normal, down)):
-                cols[c] += item[0:8] + item[8:16]
-            return carry
-
-        lax.fori_loop(0, rows // step, body, 0)
-        row_store(j).start()
+        at, slot = lax.rem(j, 2), ring.at(j)
+
+        def what(here, there):
+            down = chain.inner_in[slot, here, :].astype(F32)
+            normal, back = norm_back(hidden_rows(at, here), down, vec[1:2, :])
+            given = dy[there, :].astype(F32)
+            low = (back + given).astype(BF16)
+            resid[there, :] = low
+            gather(0, down * normal, down, low.astype(F32))
+            gather(5, given)
+
+        each_rows(j, what)
+        there = pl.ds(pl.multiple_of(j * rows, rows), rows)
+        up[there, :] = lax.dot_general(
+            resid[there, :], wo[...], (((1,), (1,)), ((), ())), preferred_element_type=F32
+        ).astype(BF16)
+
+    def rows_out(j):
+        at, slot = lax.rem(j, 2), ring.at(j)
+
+        def what(here, there):
+            out[at, here, :] = (
+                hidden_rows(at, here) + chain.inner_in[slot, here, :].astype(F32) + vec[5:6, :]
+            ).astype(BF16)
+
+        each_rows(j, what)
+        out_store(j, out_h).start()
+
+    def rows_front(j):
+        at, slot = lax.rem(j, 2), ring.at(j)
+
+        def what(here, there):
+            down = chain.inner_in[slot, here, :].astype(F32)
+            normal, back = norm_back(src[at, here, :].astype(F32), down, vec[4:5, :])
+            out[at, here, :] = (back + resid[there, :].astype(F32)).astype(BF16)
+            gather(3, down * normal, down)
+
+        each_rows(j, what)
+        out_store(j, input_h).start()
 
     def swap(j):
         to = (cube.to_c, cube.to_x, cube.to_y)[j]
-        return remote(buf.at[j], got.at[j], ss.at[j], sq.at[j], "dp", to)
+        return remote(buf.at[j], got_small.at[j], ss.at[j], sq.at[j], "dp", to)
 
     def small_step(j):
         if j == 0:
-            for c in range(2):
-                buf[0, c : c + 1, :] = jnp.sum(cols[c], axis=0, keepdims=True)
+            for row, item in ((0, cols[3]), (1, cols[4]), (2, cols[0]), (3, cols[1]), (4, cols[2]), (5, eb[...]), (6, cols[5])):
+                buf[0, row : row + 1, :] = jnp.sum(item, axis=0, keepdims=True)
         else:
             swap(j - 1).wait()
-            buf[j] = buf[j - 1] + got[j - 1]
+            buf[j] = buf[j - 1] + got_small[j - 1]
         if j < 3:
             swap(j).start()
 
     late = chain.most_lag + 1
+    heads_at = late + per_sum
 
     def tick(t, carry):
-        @pl.when(jnp.logical_and(lax.rem(t, group) == 0, t < chunks))
-        def _():
-            produce_rows(t // group)
+        gone = t - ring.gone
+
+        @pl.when(between(gone, total_z))
+        def _():
+            ring.retire(gone)
+
+        part_start(t + 2)
+
+        @pl.when(jnp.logical_and(between(t - loaded_z, per_sum), lax.rem(t - loaded_z, GROUP) == 0))
+        def _():
+            produce_rows((t - loaded_z) // GROUP)
 
         ready = t - chain.first
 
-        @pl.when(between(ready, chunks))
-        def _():
-            chain.reduce(ready)
+        @pl.when(between(ready, total_z))
+        def _():
+            @pl.when(ready < loaded_z)
+            def _():
+                part_load(ready, 0).wait()
+
+            ring.reduce(ready)
 
         back = t - chain.lag
 
-        @pl.when(between(back, chunks))
-        def _():
-            chain.spread(back)
+        @pl.when(between(back, total_z))
+        def _():
+            ring.spread(back)
 
         cube.tick(t, total_p)
 
-        @pl.when(t == 0)
-        def _():
-            for one in loads[2:4]:
+        @pl.when(t == 2)
+        def _():
+            for one in loads[:8] + [loads[9]]:
                 one.wait()
-
-        @pl.when(t == 2)
-        def _():
-            for one in loads[4:]:
+            for one in loads[10:13]:
+                one.start()
+
+        @pl.when(t == heads_at)
+        def _():
+            for one in loads[10:13]:
                 one.wait()
+            loads[13].start()
+
+        @pl.when(t == to_mixing)
+        def _():
+            loads[13].wait()
 
         @pl.when(t < total_p)
         def _():
             produce(t)
 
-        @pl.when(between(t - late, chunks))
-        def _():
-            rows_back(t - late)
+        chunk = t - late
+
+        @pl.when(between(chunk + 1, total_z))
+        def _():
+            for one in row_loads(chunk + 1):
+                one.start()
+
+        @pl.when(between(chunk - 2 - per_sum, total_z - per_sum))
+        def _():
+            out_store(chunk - 2, out_h).wait()
+
+        @pl.when(between(chunk, total_z))
+        def _():
+            for one in row_loads(chunk):
+                one.wait()
+
+            for which, what in enumerate((rows_back, rows_out, rows_front)):
+
+                @pl.when(between(chunk - which * per_sum, per_sum))
+                def _(what=what):
+                    what(chunk)
+
+        head = t - heads_at
+
+        @pl.when(between(head, heads))
+        def _():
+            head_backward(
+                head, q, k, v, up, lse, slope, off, HEAD_TILE, (grads.at[0], grads.at[1], grads.at[2]), (k_acc, v_acc)
+            )
+
+        @pl.when(head == heads)
+        def _():
+            for j, m in enumerate((0, 2)):
+                buf[0, 7:8, j * local : (j + 1) * local] = jnp.sum(
+                    grads[m].astype(F32), axis=0, keepdims=True
+                )
 
         for j in range(4):
 
-            @pl.when(t == late + chunks + j)
+            @pl.when(t == late + total_z + j)
             def _(j=j):
                 small_step(j)
 
         return carry
 
-    lax.fori_loop(0, max(chunks + late + 4, total_p + cube.gone), tick, 0)
+    assert heads_at + heads <= loaded_z and heads_at + 1 < to_output
+    lax.fori_loop(0, max(total_z + late + 4, total_p + cube.gone), tick, 0)
     small_store = pltpu.make_async_copy(buf.at[3], small_out, load.at[0])
     small_store.start()
-
-    def drain(k, carry):
-        chain.drain(k)
-        row_store(k).wait()
-        return carry
-
-    lax.fori_loop(0, chunks, drain, 0)
     small_store.wait()
 
 
-FRONT_SLACK = 2
-FRONT_APART = 2
-
-
-def front_call(n, grads, w, normed, att, resid, src, gain, small):
-    length, width = src.shape
-    local = att.shape[1]
-    blocks = width // local
-    chunks = length // FRONT_ROWS
-    block = (local // 8, local)
+def back_call(n, grad, mlp, activ, dy, second, pre, src, tot, w, normed, att, eb, vec, wo, q, k, v, lse, slope, off):
+    length, width = dy.shape
+    local = q.shape[1]
+    chunks = length // ROWS_BACK
     dma = pltpu.SemaphoreType.DMA
-    inputs = (grads, w, normed, att, resid, src, gain, small)
+
+    def cut(one):
+        return one.reshape(chunks, ROWS_BACK, one.shape[-1])
+
+    smalls = (vec, wo, q, k, v, lse, slope, off)
+    inputs = (cut(grad), cut(mlp), activ, dy, second, pre, cut(src), cut(tot), w, normed, att, eb, *smalls)
+    piece = (2, 2, 2, PIECE // 8)
     shapes = [
-        ((3 * blocks, 2, 2, 2, *block), BF16),
-        ((2, 2, 2, local // 8, width), BF16),
-        ((length, width), BF16),
-        (small.shape, F32),
+        ((chunks, ROWS_BACK, width), BF16),
+        ((activ.shape[1] // PIECE, *piece, width), BF16),
+        ((second.shape[1] // PIECE, *piece, width), BF16),
+        ((local // PIECE, *piece, width), BF16),
+        ((3, width // PIECE, *piece, local), BF16),
+        ((chunks, ROWS_BACK, width), BF16),
+        ((8, width), F32),
     ]
-    order = (grads, w, normed, att, resid, src, gain)
+    slots = BACK_SLOTS
     scratch = [
-        *[pltpu.VMEM(one.shape, one.dtype) for one in order],
-        pltpu.VMEM((2, 8, width), F32),
-        pltpu.VMEM((4, *small.shape), F32),
-        pltpu.VMEM((3, *small.shape), F32),
-        dma((8,)),
-        dma((chunks,)),
+        pltpu.VMEM((2, length, PIECE), BF16),
+        pltpu.VMEM(dy.shape, BF16),
+        pltpu.VMEM(pre.shape, BF16),
+        *[pltpu.VMEM((2, ROWS_BACK, width), BF16)] * 3,
+        pltpu.VMEM(dy.shape, BF16),
+        *[pltpu.VMEM(one.shape, one.dtype) for one in (w, att, eb)],
+        *[pltpu.VMEM(one.shape, one.dtype) for one in smalls],
+        pltpu.VMEM(q.shape, BF16),
+        pltpu.VMEM((3, *q.shape), BF16),
+        *[pltpu.VMEM((length, 2 * HD), F32)] * 2,
+        pltpu.VMEM((6, 8, width), F32),
+        pltpu.VMEM((4, 8, width), F32),
+        pltpu.VMEM((3, 8, width), F32),
+        dma((14,)),
+        dma((2,)),
+        dma((slots,)),
+        dma((2, 2)),
+        dma((2,)),
         dma((3,)),
         dma((3,)),
-        *Chain.scratch(chunks, (FRONT_ROWS, width)),
-        *Cube.scratch(block, FRONT_APART),
+        *Chain.scratch(slots, (ROWS_BACK, width)),
+        *Cube.scratch((PIECE // 8, BACK_COLUMNS), BACK_APART),
     ]
     return pl.pallas_call(
-        functools.partial(front_kernel, n),
+        functools.partial(back_kernel, n, local // HD),
         out_shape=[jax.ShapeDtypeStruct(*one) for one in shapes],
         in_specs=[pl.BlockSpec(memory_space=pl.ANY)] * len(inputs),
         out_specs=[pl.BlockSpec(memory_space=pl.ANY)] * len(shapes),
         scratch_shapes=scratch,
         compiler_params=pltpu.CompilerParams(
-            collective_id=2, has_side_effects=True, vmem_limit_bytes=60 << 20
+            collective_id=1, has_side_effects=True, vmem_limit_bytes=61 << 20
         ),
     )(*inputs)
 
@@ -1257,14 +1183,12 @@
         vectors = jnp.stack(
             [
                 jnp.pad(one, (0, most - one.shape[0]))
-                for one in (output_bias, second_gain, second_shift, expand_bias)
+                for one in (output_bias, second_gain, second_shift, expand_bias, first_gain, shrink_bias)
             ]
         )
         total, second_low, activ_low, pre_grad, partial_mlp, second_part, expand_bias_part = mlp_call(
             n_tensor, attended, output_weight, inputs, cotangent, expand_weight, shrink_weight, vectors
         )
-        expand_bias_part = jnp.sum(expand_bias_part, axis=0)
-        hidden_state = source + (total.reshape(length, width).astype(F32) + output_bias)
     else:
         partial_out = jnp.dot(attended, output_weight, preferred_element_type=F32)
         resid = lax.psum(partial_out.astype(BF16), "tensor").astype(F32)
@@ -1278,23 +1202,22 @@
         pre_grad = gelu_pull(act_grad)[0].astype(BF16)
         expand_bias_part = jnp.sum(pre_grad.astype(F32), axis=0)
         second_part = jnp.einsum("tf,df->td", pre_grad, expand_weight, preferred_element_type=F32)
-    shrink_bias_part = jnp.sum(upstream, axis=0)
     if fast:
-        mlp_sum, weight_sums, resid_low, grads, sums_back = back_call(
+        outputs, shrink_sum, expand_sum, output_sum, mixing_sum, input_grad, small = back_call(
             n_tensor, second_part, partial_mlp, activ_low, cotangent, second_low, pre_grad, inputs, total,
-            vectors[:, :width], output_weight, query, keys, vals, logsum, slope, off,
-        )
-        mlp_sum = mlp_sum.reshape(length, width).astype(F32)
-        resid_low = resid_low.reshape(length, width)
-        hidden_grad = resid_low.astype(F32)
-        second_gain_part, second_shift_part, output_bias_part = (
-            jnp.sum(sums_back[k], axis=0) for k in range(3)
-        )
-        pieces = units // 256
-        shrink_weight_grad = weight_sums[:pieces].astype(F32).reshape(units, width)
-        expand_weight_grad = weight_sums[pieces:].astype(F32).reshape(width, units)
-        outputs = (hidden_state + mlp_sum + shrink_bias).astype(BF16)
+            weights, normed_low, attended, expand_bias_part, vectors[:, :width], output_weight, query, keys, vals,
+            logsum, slope, off,
+        )
+        outputs, input_grad = outputs.reshape(length, width), input_grad.reshape(length, width)
+        shrink_weight_grad = shrink_sum.astype(F32).reshape(units, width)
+        expand_weight_grad = expand_sum.astype(F32).reshape(width, units)
+        mixing_weight_grad = mixing_sum.astype(F32).reshape(3, width, local_width).transpose(1, 0, 2)
+        output_weight_grad = output_sum.astype(F32).reshape(local_width, width)
+        first_gain_grad, first_shift_grad, second_gain_grad, second_shift_grad = small[0], small[1], small[2], small[3]
+        output_bias_grad, expand_bias_grad, shrink_bias_grad = small[4], small[5], small[6]
+        mixing_bias_grad = small[7, : 2 * local_width].reshape(2, local_width)
     else:
+        shrink_bias_part = jnp.sum(upstream, axis=0)
         shrink_part = jnp.einsum("tf,td->fd", activ_low, cotangent, preferred_element_type=F32)
         expand_part = jnp.einsum("td,tf->df", second_low, pre_grad, preferred_element_type=F32)
 
@@ -1329,32 +1252,9 @@
             jnp.einsum("hqk,qhd->khd", score_grad, query, preferred_element_type=F32) * scale_factor
         ).astype(BF16)
         grads = [one.reshape(length, local_width) for one in (query_grad, keys_grad, vals_grad)]
-    mixing_bias_part = jnp.stack(
-        [jnp.sum(grads[0].astype(F32), axis=0), jnp.sum(grads[2].astype(F32), axis=0)]
-    )
-    if fast:
-        small = jnp.stack(
-            [
-                jnp.zeros_like(second_gain_part),
-                jnp.zeros_like(second_gain_part),
-                second_gain_part,
-                second_shift_part,
-                output_bias_part,
-                expand_bias_part,
-                shrink_bias_part,
-                jnp.pad(mixing_bias_part.reshape(-1), (0, width - 2 * local_width)),
-            ]
-        )
-        mixing_sum, output_sum, input_grad, small = front_call(
-            n_tensor, grads, weights, normed_low, attended, resid_low, inputs,
-            first_gain.reshape(1, width), small,
-        )
-        mixing_weight_grad = mixing_sum.reshape(3, width, local_width).astype(F32).transpose(1, 0, 2)
-        output_weight_grad = output_sum.reshape(local_width, width).astype(F32)
-        first_gain_grad, first_shift_grad, second_gain_grad, second_shift_grad = small[0], small[1], small[2], small[3]
-        output_bias_grad, expand_bias_grad, shrink_bias_grad = small[4], small[5], small[6]
-        mixing_bias_grad = small[7, : 2 * local_width].reshape(2, local_width)
-    else:
+        mixing_bias_part = jnp.stack(
+            [jnp.sum(grads[0].astype(F32), axis=0), jnp.sum(grads[2].astype(F32), axis=0)]
+        )
         mixing_part = jnp.stack(
             [jnp.einsum("td,tc->dc", normed_low, one, preferred_element_type=F32) for one in grads]
         )

time: 462 us -> 422 us (0.913)
  Pallas kernels: 414 us -> 382 us
  other arithmetic: 35.2 us -> 30.2 us
    pallas_call x2 -> x1, Pallas kernels: 267 us -> 235 us  [back_call(): pl.pallas_call(functools.partial(back_kernel, n, local // HD), out_shape=...]
    convert_element_type x2 -> x0, other arithmetic: 9.54 us -> none  [the longest x1 6.86 us: on_device(): outputs = (hidden_state + mlp_sum + shrink_bias).astype(BF16)]
    reshape x1 -> x2, other arithmetic: 12.6 us -> 21.2 us  [the longest x1 18.5 us: on_device(): shrink_weight_grad = shrink_sum.astype(F32).reshape(units, width)]
    slice x1 -> x0, local copies, waits for them, and re-layouts: 6.57 us -> none  [on_device(): shrink_weight_grad = weight_sums[:pieces].astype(F32).reshape(units, width)]
where the time goes in v4:
time: 422 us
  Pallas kernels  382 us (91%)
  other arithmetic  30.2 us (7%)
  local copies, waits for them, and re-layouts  9.15 us (2%)
    pallas_call x1, Pallas kernels, back_call(): pl.pallas_call(functools.partial(back_kernel, n, local // HD), out_shape=...  235 us
    pallas_call x1, Pallas kernels, mlp_call(): pl.pallas_call(functools.partial(mlp_kernel, n, length), out_shape=out_sh...  106 us
    pallas_call x1, Pallas kernels, head_call(): pl.pallas_call(functools.partial(head_kernel, heads), out_shape=[jax.Shap...  40.4 us
    reshape x1, other arithmetic, on_device(): shrink_weight_grad = shrink_sum.astype(F32).reshape(units, width)  18.5 us

profile of v4, /device:TPU:0, one launch (start us, length us, event | category | flops | bytes accessed | tf_op | source)
XLA Modules:
  0.0 421.7 jit_solution(4639337381150967733)
XLA Ops:
  0.6 0.8 fusion.1
  1.4 0.1 pad.1.clone
  1.5 0.7 pad_maximum_fusion.1.refs_3_
  2.2 1.3 pad_maximum_fusion.refs_2_
  3.5 0.7 broadcast_in_dim.2.refs_4_.refs_18_
  4.2 0.0 copy-start.3
  4.2 0.0 copy-start.4
  4.2 0.0 copy-start.5
  4.2 0.0 copy-start.6
  4.2 0.0 copy-start.7
  4.2 0.0 copy-start.8
  4.2 40.4 %shard_map.254 = (bf16[768,2048]{1,0:T(8,128)(2,1)}, bf16[768,512]{1,0:T(8,128)(2,1)}, bf16[768,512]{1,0:T(8,128)(2,1)}, bf16[768,512]{1,0:T(8,128)(2,1)}, bf16[...) custom-call(bf16[768,2048]{1,0:T(8,128)(2,1)} %refs_2_.1, bf16[3,2048,512]{2,1,0:T(8,128)(2,1)} %bitcast.37, ...), custom_call_target="tpu_custom_call" | custom-call | tf_op jit(solution)/shard_map/pallas_call | solution.py:275
  44.6 0.0 copy-done.3
  44.7 0.0 copy-done.4
  44.7 0.0 copy-done.5
  44.7 0.0 copy-done.6
  44.7 0.0 copy-done.7
  44.7 0.0 copy-done.8
  44.7 0.7 stack.40.refs_6_.refs_12_
  45.4 106.3 %shard_map.255 = (bf16[24,32,2048]{2,1,0:T(8,128)(2,1)}, bf16[768,2048]{1,0:T(8,128)(2,1)}, bf16[768,2048]{1,0:T(8,128)(2,1)}, bf16[768,2048]{1,0:T(8,128)(2,1)}...) custom-call(bf16[768,512]{1,0:T(8,128)(2,1)} %get-tuple-element.35.refs_0_.refs_10_, ...), custom_call_target="tpu_custom_call" | custom-call | tf_op jit(solution)/shard_map/pallas_call | solution.py:467
  151.7 234.9 %shard_map.256 = (bf16[16,48,2048]{2,1,0:T(8,128)(2,1)}, bf16[8,2,2,2,32,2048]{5,4,3,2,1,0:T(8,128)(2,1)}, bf16[8,2,2,2,32,2048]{5,4,3,2,1,0:T(8,128)(2,1)}, bf1...) custom-call(bf16[16,48,2048]{2,1,0:T(8,128)(2,1)} %bitcast.43, ...), custom_call_target="tpu_custom_call" | custom-call | tf_op jit(solution)/shard_map/pallas_call | solution.py:1116
  386.6 0.0 slice-start
  386.6 0.0 slice-start.1
  386.6 18.5 %bitcast_convert_fusion = (f32[2048,2048]{1,0:T(8,128)}, f32[2048,2048]{1,0:T(8,128)}) fusion(bf16[8,2,2,2,32,2048]{5,4,3,2,1,0:T(8,128)(2,1)} %get-tuple-element.55, bf16[8,2,2,2,32,2048]{5,4,3,2,1,0:T(8,128)(2,1)} %get-tuple-element.54), kind=kLoop, calls=%fused_computation.1 | loop fusion | flops 8388608 | bytes 50331648 | tf_op jit(solution)/shard_map/reshape | solution.py:1212
  405.1 0.0 slice-done
  405.1 0.0 slice-done.1
  405.1 0.0 copy-start.1
  405.1 7.0 %convert_bitcast_fusion = f32[2048,3,512]{2,0,1:T(8,128)} fusion(bf16[3,8,2,2,2,32,512]{6,5,4,3,2,1,0:T(8,128)(2,1)S(1)} %bitcast.40), kind=kLoop, calls=%fused_computation | loop fusion | flops 3145728 | bytes 18874368 | tf_op jit(solution)/shard_map/transpose | solution.py:1214
  412.1 0.0 copy-start.2
  412.1 0.0 copy-done.1
  412.1 2.7 bitcast_convert_fusion.2
  414.8 0.0 copy-start
  414.8 0.0 copy-done.2
  414.8 0.6 fusion
  415.4 0.6 reshape_squeeze.3
  416.1 4.0 copy.31
  420.0 0.0 copy-done
  420.0 1.7 copy.32
  (3 shorter events, 0.0 us)
Async XLA Ops:
  4.2 40.5 %copy-start.3 = (f32[2048]{0:T(1024)S(1)}, f32[2048]{0:T(1024)}, u32[]{:S(2)}) copy-start(f32[2048]{0:T(1024)} %param.17) | copy-start | bytes 24580
  4.2 40.5 %copy-start.4 = (f32[2048]{0:T(1024)S(1)}, f32[2048]{0:T(1024)}, u32[]{:S(2)}) copy-start(f32[2048]{0:T(1024)} %param.22) | copy-start | bytes 24580
  4.2 40.5 %copy-start.5 = (f32[2048]{0:T(1024)S(1)}, f32[2048]{0:T(1024)}, u32[]{:S(2)}) copy-start(f32[2048]{0:T(1024)} %param.23) | copy-start | bytes 24580
  4.2 40.5 %copy-start.6 = (f32[2048]{0:T(1024)S(1)}, f32[2048]{0:T(1024)}, u32[]{:S(2)}) copy-start(f32[2048]{0:T(1024)} %param.24) | copy-start | bytes 24580
  4.2 40.5 %copy-start.7 = (f32[2048]{0:T(1024)S(1)}, f32[2048]{0:T(1024)}, u32[]{:S(2)}) copy-start(f32[2048]{0:T(1024)} %param.26) | copy-start | bytes 24580
  4.2 40.5 %copy-start.8 = (f32[2048]{0:T(1024)S(1)}, f32[2048]{0:T(1024)}, u32[]{:S(2)}) copy-start(f32[2048]{0:T(1024)} %param.28) | copy-start | bytes 24580
  386.6 18.5 %slice-start = ((s8[6291456]{0:T(1024)(128)(4,1)}), s8[4194304]{0:T(1024)(128)(4,1)S(1)}, s32[]{:S(2)}) async-start(s8[6291456]{0:T(1024)(128)(4,1)} %bitcast.39), calls=%async_computation | async-start | bytes 8388608
  386.6 18.5 %slice-start.1 = ((s8[6291456]{0:T(1024)(128)(4,1)}), s8[2097152]{0:T(1024)(128)(4,1)S(1)}, s32[]{:S(2)}) async-start(s8[6291456]{0:T(1024)(128)(4,1)} %bitcast.39), calls=%async_computation.1 | async-start | bytes 4194304
  405.1 7.0 %copy-start.1 = (bf16[2,2,2,2,32,2048]{5,4,3,2,1,0:T(8,128)(2,1)S(1)}, bf16[2,2,2,2,32,2048]{5,4,3,2,1,0:T(8,128)(2,1)}, u32[]{:S(2)}) copy-start(bf16[2,2,2,2,32,2048]{5,4,3,2,1,0:T(8,128)(2,1)} %get-tuple-element.53) | copy-start | bytes 6291460
  412.1 2.7 copy-start.2
  414.8 5.2 %copy-start = (bf16[16,48,2048]{2,1,0:T(8,128)(2,1)S(1)}, bf16[16,48,2048]{2,1,0:T(8,128)(2,1)}, u32[]{:S(2)}) copy-start(bf16[16,48,2048]{2,1,0:T(8,128)(2,1)} %get-tuple-element.50) | copy-start | bytes 9437188

commit v5 on v4

--- a/solution.py
+++ b/solution.py
@@ -155,36 +155,36 @@
     return jnp.logical_and(k >= 0, k < count)
 
 
-def head_forward(head, q, k, v, slope, off, tile, attended, lse):
+def pair_forward(pair, q, k, v, slope, off, tile, attended, lse):
     length = q.shape[0]
-    odd = lax.rem(head, 2)
-    mask = lane_half(odd).astype(BF16)
-    lanes = pl.ds(pl.multiple_of((head // 2) * 2 * HD, 2 * HD), 2 * HD)
-    gain = slope[pl.ds(head, 1), 0:1]
+    lanes = pl.ds(pl.multiple_of(pair * 2 * HD, 2 * HD), 2 * HD)
+    masks = [lane_half(odd).astype(BF16) for odd in range(2)]
+    gains = [slope[pl.ds(2 * pair + odd, 1), 0:1] for odd in range(2)]
     for j in range(length // tile):
         rows = slice(j * tile, (j + 1) * tile)
         most = min(length, (j + 2) * tile)
-        scores = lax.dot_general(
-            k[0:most, lanes] * mask, q[rows, lanes], (((1,), (1,)), ((), ())), preferred_element_type=F32
-        )
-        scores = scores * (1.0 / math.sqrt(HD)) + gain * off[0:most, rows]
-        top = jnp.max(scores, axis=0, keepdims=True)
-        raised = jnp.exp(scores - top)
-        total = jnp.sum(raised, axis=0, keepdims=True)
-        lse[pl.ds(head, 1), rows] = top + jnp.log(total)
-        probs = (raised * (1.0 / total)).astype(BF16)
-        got = lax.dot_general(
-            v[0:most, lanes] * mask, probs, (((0,), (0,)), ((), ())), preferred_element_type=F32
-        )
-        mine = got.T.astype(BF16)
-
-        @pl.when(odd == 0)
-        def _(rows=rows, mine=mine):
-            attended[rows, lanes] = mine
-
-        @pl.when(odd == 1)
-        def _(rows=rows, mine=mine):
-            attended[rows, lanes] += mine
+        here = q[rows, lanes]
+        scores = [
+            lax.dot_general(
+                k[0:most, lanes], here * masks[odd], (((1,), (1,)), ((), ())), preferred_element_type=F32
+            )
+            for odd in range(2)
+        ]
+        got = []
+        for odd in range(2):
+            raised = scores[odd] * (1.0 / math.sqrt(HD)) + gains[odd] * off[0:most, rows]
+            top = jnp.max(raised, axis=0, keepdims=True)
+            raised = jnp.exp(raised - top)
+            total = jnp.sum(raised, axis=0, keepdims=True)
+            lse[pl.ds(2 * pair + odd, 1), rows] = top + jnp.log(total)
+            probs = (raised * (1.0 / total)).astype(BF16)
+            got.append(
+                lax.dot_general(
+                    v[0:most, lanes], probs, (((0,), (0,)), ((), ())), preferred_element_type=F32
+                )
+            )
+        both = jnp.concatenate([got[0][:HD], got[1][HD:]], axis=0)
+        attended[rows, lanes] = both.T.astype(BF16)
 
 
 def head_kernel(heads, *refs):
@@ -205,17 +205,18 @@
         one.start()
     for one in loads:
         one.wait()
-    step = 16
+    step, groups = 16, 4
 
     def normalize(i, carry):
-        at = pl.ds(pl.multiple_of(i * step, step), step)
-        value = src[at, :].astype(F32)
-        centred = value - jnp.sum(value, axis=-1, keepdims=True) / width
-        var = jnp.sum(centred * centred, axis=-1, keepdims=True) / width
-        normed[at, :] = (centred * lax.rsqrt(var + EPS) * vec[0:1, :] + vec[1:2, :]).astype(BF16)
+        ats = [pl.ds(pl.multiple_of((i * groups + g) * step, step), step) for g in range(groups)]
+        values = [src[at, :].astype(F32) for at in ats]
+        centred = [one - jnp.sum(one, axis=-1, keepdims=True) / width for one in values]
+        spread = [lax.rsqrt(jnp.sum(one * one, axis=-1, keepdims=True) / width + EPS) for one in centred]
+        for at, one, by in zip(ats, centred, spread):
+            normed[at, :] = (one * by * vec[0:1, :] + vec[1:2, :]).astype(BF16)
         return carry
 
-    lax.fori_loop(0, length // step, normalize, 0)
+    lax.fori_loop(0, length // (step * groups), normalize, 0)
 
     here = blocks[...].astype(F32)
     there = jnp.broadcast_to(here, (8, length)).T[:, 0:1]
@@ -249,11 +250,11 @@
     for one in stores[:5]:
         one.start()
 
-    def attend(head, carry):
-        head_forward(head, q, k, v, slope, off, HEAD_TILE, att, lse)
+    def attend(pair, carry):
+        pair_forward(pair, q, k, v, slope, off, HEAD_TILE, att, lse)
         return carry
 
-    lax.fori_loop(0, heads, attend, 0)
+    lax.fori_loop(0, heads // 2, attend, 0)
     for one in stores[5:]:
         one.start()
     for one in stores:
@@ -342,21 +343,26 @@
                 chain.part[g * group + q, :, cols] = got[q * ROWS : (q + 1) * ROWS]
 
     def normalize(b):
-        step = 16
+        step, groups = 16, 4
 
         def body(i, carry):
-            at = pl.ds(pl.multiple_of(b * BLOCK_ROWS + i * step, step), step)
-            k = b * per_block + i // (ROWS // step)
-            inside = pl.ds(pl.multiple_of((i % (ROWS // step)) * step, step), step)
-            value = src[at, :].astype(F32) + (chain.inner_in[k, inside, :].astype(F32) + vec[0:1, :width])
-            centred = value - jnp.mean(value, axis=-1, keepdims=True)
-            var = jnp.mean(centred * centred, axis=-1, keepdims=True)
-            second[at, :] = (
-                centred * lax.rsqrt(var + EPS) * vec[1:2, :width] + vec[2:3, :width]
-            ).astype(BF16)
+            ats, values = [], []
+            for g in range(groups):
+                r = i * groups + g
+                at = pl.ds(pl.multiple_of(b * BLOCK_ROWS + r * step, step), step)
+                k = b * per_block + r // (ROWS // step)
+                inside = pl.ds(pl.multiple_of((r % (ROWS // step)) * step, step), step)
+                ats.append(at)
+                values.append(
+                    src[at, :].astype(F32) + (chain.inner_in[k, inside, :].astype(F32) + vec[0:1, :width])
+                )
+            centred = [one - jnp.mean(one, axis=-1, keepdims=True) for one in values]
+            spread = [lax.rsqrt(jnp.mean(one * one, axis=-1, keepdims=True) + EPS) for one in centred]
+            for at, one, by in zip(ats, centred, spread):
+                second[at, :] = (one * by * vec[1:2, :width] + vec[2:3, :width]).astype(BF16)
             return carry
 
-        lax.fori_loop(0, BLOCK_ROWS // step, body, 0)
+        lax.fori_loop(0, BLOCK_ROWS // (step * groups), body, 0)
 
     def hidden_tile(b, j):
         at = pl.ds(pl.multiple_of(b * BLOCK_ROWS, BLOCK_ROWS), BLOCK_ROWS)

time: 422 us -> 402 us (0.953)
  Pallas kernels: 382 us -> 362 us
    pallas_call x1, Pallas kernels: 40.4 us -> 23.7 us  [head_call(): pl.pallas_call(functools.partial(head_kernel, heads), out_shape=[jax.Shap...]
    pallas_call x1, Pallas kernels: 106 us -> 101 us  [mlp_call(): pl.pallas_call(functools.partial(mlp_kernel, n, length), out_shape=out_sh...]
where the time goes in v5:
time: 402 us
  Pallas kernels  362 us (90%)
  other arithmetic  30.2 us (8%)
  local copies, waits for them, and re-layouts  9.15 us (2%)
    pallas_call x1, Pallas kernels, back_call(): pl.pallas_call(functools.partial(back_kernel, n, local // HD), out_shape=...  237 us
    pallas_call x1, Pallas kernels, mlp_call(): pl.pallas_call(functools.partial(mlp_kernel, n, length), out_shape=out_sh...  101 us
    pallas_call x1, Pallas kernels, head_call(): pl.pallas_call(functools.partial(head_kernel, heads), out_shape=[jax.Shap...  23.7 us
    reshape x1, other arithmetic, on_device(): shrink_weight_grad = shrink_sum.astype(F32).reshape(units, width)  18.5 us

profile of v5, /device:TPU:0, one launch (start us, length us, event | category | flops | bytes accessed | tf_op | source)
XLA Modules:
  0.0 401.6 jit_solution(10147178004463711684)
XLA Ops:
  0.6 0.8 fusion.1
  1.4 0.1 pad.1.clone
  1.5 0.7 pad_maximum_fusion.1.refs_3_
  2.2 1.3 pad_maximum_fusion.refs_2_
  3.5 0.7 broadcast_in_dim.2.refs_4_.refs_18_
  4.2 0.0 copy-start.3
  4.2 0.0 copy-start.4
  4.2 0.0 copy-start.5
  4.2 0.0 copy-start.6
  4.2 0.0 copy-start.7
  4.2 0.0 copy-start.8
  4.2 23.7 %shard_map.254 = (bf16[768,2048]{1,0:T(8,128)(2,1)}, bf16[768,512]{1,0:T(8,128)(2,1)}, bf16[768,512]{1,0:T(8,128)(2,1)}, bf16[768,512]{1,0:T(8,128)(2,1)}, bf16[...) custom-call(bf16[768,2048]{1,0:T(8,128)(2,1)} %refs_2_.1, bf16[3,2048,512]{2,1,0:T(8,128)(2,1)} %bitcast.37, ...), custom_call_target="tpu_custom_call" | custom-call | tf_op jit(solution)/shard_map/pallas_call | solution.py:276
  27.9 0.0 copy-done.3
  27.9 0.0 copy-done.4
  27.9 0.0 copy-done.5
  27.9 0.0 copy-done.6
  27.9 0.0 copy-done.7
  28.0 0.0 copy-done.8
  28.0 0.7 stack.40.refs_6_.refs_12_
  28.7 100.8 %shard_map.255 = (bf16[24,32,2048]{2,1,0:T(8,128)(2,1)}, bf16[768,2048]{1,0:T(8,128)(2,1)}, bf16[768,2048]{1,0:T(8,128)(2,1)}, bf16[768,2048]{1,0:T(8,128)(2,1)}...) custom-call(bf16[768,512]{1,0:T(8,128)(2,1)} %get-tuple-element.35.refs_0_.refs_10_, ...), custom_call_target="tpu_custom_call" | custom-call | tf_op jit(solution)/shard_map/pallas_call | solution.py:473
  129.5 237.0 %shard_map.256 = (bf16[16,48,2048]{2,1,0:T(8,128)(2,1)}, bf16[8,2,2,2,32,2048]{5,4,3,2,1,0:T(8,128)(2,1)}, bf16[8,2,2,2,32,2048]{5,4,3,2,1,0:T(8,128)(2,1)}, bf1...) custom-call(bf16[16,48,2048]{2,1,0:T(8,128)(2,1)} %bitcast.43, ...), custom_call_target="tpu_custom_call" | custom-call | tf_op jit(solution)/shard_map/pallas_call | solution.py:1122
  366.5 0.0 slice-start
  366.5 0.0 slice-start.1
  366.5 18.5 %bitcast_convert_fusion = (f32[2048,2048]{1,0:T(8,128)}, f32[2048,2048]{1,0:T(8,128)}) fusion(bf16[8,2,2,2,32,2048]{5,4,3,2,1,0:T(8,128)(2,1)} %get-tuple-element.55, bf16[8,2,2,2,32,2048]{5,4,3,2,1,0:T(8,128)(2,1)} %get-tuple-element.54), kind=kLoop, calls=%fused_computation.1 | loop fusion | flops 8388608 | bytes 50331648 | tf_op jit(solution)/shard_map/reshape | solution.py:1218
  385.0 0.0 slice-done
  385.0 0.0 slice-done.1
  385.0 0.0 copy-start.1
  385.0 7.0 %convert_bitcast_fusion = f32[2048,3,512]{2,0,1:T(8,128)} fusion(bf16[3,8,2,2,2,32,512]{6,5,4,3,2,1,0:T(8,128)(2,1)S(1)} %bitcast.40), kind=kLoop, calls=%fused_computation | loop fusion | flops 3145728 | bytes 18874368 | tf_op jit(solution)/shard_map/transpose | solution.py:1220
  392.0 0.0 copy-start.2
  392.0 0.0 copy-done.1
  392.0 2.7 bitcast_convert_fusion.2
  394.7 0.0 copy-start
  394.7 0.0 copy-done.2
  394.7 0.6 fusion
  395.4 0.6 reshape_squeeze.3
  396.0 4.0 copy.31
  400.0 0.0 copy-done
  400.0 1.7 copy.32
  (3 shorter events, 0.0 us)
Async XLA Ops:
  4.2 23.7 %copy-start.3 = (f32[2048]{0:T(1024)S(1)}, f32[2048]{0:T(1024)}, u32[]{:S(2)}) copy-start(f32[2048]{0:T(1024)} %param.17) | copy-start | bytes 24580
  4.2 23.8 %copy-start.4 = (f32[2048]{0:T(1024)S(1)}, f32[2048]{0:T(1024)}, u32[]{:S(2)}) copy-start(f32[2048]{0:T(1024)} %param.22) | copy-start | bytes 24580
  4.2 23.8 %copy-start.5 = (f32[2048]{0:T(1024)S(1)}, f32[2048]{0:T(1024)}, u32[]{:S(2)}) copy-start(f32[2048]{0:T(1024)} %param.23) | copy-start | bytes 24580
  4.2 23.8 %copy-start.6 = (f32[2048]{0:T(1024)S(1)}, f32[2048]{0:T(1024)}, u32[]{:S(2)}) copy-start(f32[2048]{0:T(1024)} %param.24) | copy-start | bytes 24580
  4.2 23.8 %copy-start.7 = (f32[2048]{0:T(1024)S(1)}, f32[2048]{0:T(1024)}, u32[]{:S(2)}) copy-start(f32[2048]{0:T(1024)} %param.26) | copy-start | bytes 24580
  4.2 23.8 %copy-start.8 = (f32[2048]{0:T(1024)S(1)}, f32[2048]{0:T(1024)}, u32[]{:S(2)}) copy-start(f32[2048]{0:T(1024)} %param.28) | copy-start | bytes 24580
  366.5 18.5 %slice-start = ((s8[6291456]{0:T(1024)(128)(4,1)}), s8[4194304]{0:T(1024)(128)(4,1)S(1)}, s32[]{:S(2)}) async-start(s8[6291456]{0:T(1024)(128)(4,1)} %bitcast.39), calls=%async_computation | async-start | bytes 8388608
  366.5 18.5 %slice-start.1 = ((s8[6291456]{0:T(1024)(128)(4,1)}), s8[2097152]{0:T(1024)(128)(4,1)S(1)}, s32[]{:S(2)}) async-start(s8[6291456]{0:T(1024)(128)(4,1)} %bitcast.39), calls=%async_computation.1 | async-start | bytes 4194304
  385.0 7.0 %copy-start.1 = (bf16[2,2,2,2,32,2048]{5,4,3,2,1,0:T(8,128)(2,1)S(1)}, bf16[2,2,2,2,32,2048]{5,4,3,2,1,0:T(8,128)(2,1)}, u32[]{:S(2)}) copy-start(bf16[2,2,2,2,32,2048]{5,4,3,2,1,0:T(8,128)(2,1)} %get-tuple-element.53) | copy-start | bytes 6291460
  392.0 2.7 copy-start.2
  394.7 5.2 %copy-start = (bf16[16,48,2048]{2,1,0:T(8,128)(2,1)S(1)}, bf16[16,48,2048]{2,1,0:T(8,128)(2,1)}, u32[]{:S(2)}) copy-start(bf16[16,48,2048]{2,1,0:T(8,128)(2,1)} %get-tuple-element.50) | copy-start | bytes 9437188

commit v6 on v5

--- a/solution.py
+++ b/solution.py
@@ -527,9 +527,9 @@
             *[dma((n,))] * 3,
         ]
 
-    def greet(self, barrier):
-        for to in (self.to_c, self.to_x, self.to_y):
-            pl.semaphore_signal(barrier, inc=1, device_id={"dp": to}, device_id_type=MESH)
+    def peer(self, m):
+        moves = (1 - 2 * self.c, 2 - 4 * self.x, 4 - 8 * self.y)
+        return lax.axis_index("dp") + sum(move for bit, move in enumerate(moves) if m >> bit & 1)
 
     def slot(self, k):
         return lax.rem(k, self.slots)
@@ -704,8 +704,8 @@
     (left, dy, pre, src, tot, out, resid, w, att, eb), refs = refs[:10], refs[10:]
     smalls, refs = refs[:8], refs[8:]
     vec, wo, q, k, v, lse, slope, off = smalls
-    (up, grads, k_acc, v_acc, cols, buf, got_small), refs = refs[:7], refs[7:]
-    (load, left_sem, part_sem, row_sem, out_sem, ss, sq), refs = refs[:7], refs[7:]
+    (up, grads, k_acc, v_acc, cols, buf, got_small, last), refs = refs[:8], refs[8:]
+    (load, left_sem, part_sem, row_sem, out_sem, ss, sq, ls, lq), refs = refs[:9], refs[9:]
     ring, refs = Ring(n, refs[:7], BACK_SLOTS, BACK_SLACK), refs[7:]
     chain = ring.chain
     width, local = dy.shape[1], q.shape[1]
@@ -798,10 +798,11 @@
         one.start()
     barrier = pltpu.get_barrier_semaphore()
     chain.greet(barrier)
-    cube.greet(barrier)
+    for m in range(1, 8):
+        pl.semaphore_signal(barrier, inc=1, device_id={"dp": cube.peer(m)}, device_id_type=MESH)
     cols[...] = jnp.zeros_like(cols)
     buf[...] = jnp.zeros_like(buf)
-    chain.wait_greetings(barrier, 3)
+    chain.wait_greetings(barrier, 7)
     loads[8].wait()
 
     def product(p, columns, right):
@@ -884,25 +885,26 @@
     def row_sum(x):
         return jnp.sum(x, axis=-1, keepdims=True)
 
-    def norm_back(value, down, gain):
-        centred = value - row_sum(value) / width
-        spread = lax.rsqrt(row_sum(centred * centred) / width + EPS)
-        normal = centred * spread
-        scaled = down * gain
-        flat, slope_of = row_sum(scaled) / width, row_sum(scaled * normal) / width
-        return normal, spread * (scaled - flat - normal * slope_of)
+    def norm_back(values, downs, gain):
+        centred = [one - row_sum(one) / width for one in values]
+        spread = [lax.rsqrt(row_sum(one * one) / width + EPS) for one in centred]
+        normal = [one * by for one, by in zip(centred, spread)]
+        scaled = [one * gain for one in downs]
+        flat = [row_sum(one) / width for one in scaled]
+        slope_of = [row_sum(one * other) / width for one, other in zip(scaled, normal)]
+        back = [
+            by * (one - low - other * high)
+            for by, one, low, other, high in zip(spread, scaled, flat, normal, slope_of)
+        ]
+        return normal, back
 
     def each_rows(j, what):
         step = 16
-
-        def body(i, carry):
-            what(
-                pl.ds(pl.multiple_of(i * step, step), step),
-                pl.ds(pl.multiple_of(lax.rem(j, per_sum) * rows + i * step, step), step),
-            )
-            return carry
-
-        lax.fori_loop(0, rows // step, body, 0)
+        start = lax.rem(j, per_sum) * rows
+        what(
+            [slice(i * step, (i + 1) * step) for i in range(rows // step)],
+            [pl.ds(pl.multiple_of(start + i * step, step), step) for i in range(rows // step)],
+        )
 
     def gather(start, *items):
         for c, item in enumerate(items):
@@ -914,14 +916,15 @@
     def rows_back(j):
         at, slot = lax.rem(j, 2), ring.at(j)
 
-        def what(here, there):
-            down = chain.inner_in[slot, here, :].astype(F32)
-            normal, back = norm_back(hidden_rows(at, here), down, vec[1:2, :])
-            given = dy[there, :].astype(F32)
-            low = (back + given).astype(BF16)
-            resid[there, :] = low
-            gather(0, down * normal, down, low.astype(F32))
-            gather(5, given)
+        def what(heres, theres):
+            downs = [chain.inner_in[slot, here, :].astype(F32) for here in heres]
+            normals, backs = norm_back([hidden_rows(at, here) for here in heres], downs, vec[1:2, :])
+            for there, down, normal, back in zip(theres, downs, normals, backs):
+                given = dy[there, :].astype(F32)
+                low = (back + given).astype(BF16)
+                resid[there, :] = low
+                gather(0, down * normal, down, low.astype(F32))
+                gather(5, given)
 
         each_rows(j, what)
         there = pl.ds(pl.multiple_of(j * rows, rows), rows)
@@ -932,10 +935,11 @@
     def rows_out(j):
         at, slot = lax.rem(j, 2), ring.at(j)
 
-        def what(here, there):
-            out[at, here, :] = (
-                hidden_rows(at, here) + chain.inner_in[slot, here, :].astype(F32) + vec[5:6, :]
-            ).astype(BF16)
+        def what(heres, theres):
+            for here in heres:
+                out[at, here, :] = (
+                    hidden_rows(at, here) + chain.inner_in[slot, here, :].astype(F32) + vec[5:6, :]
+                ).astype(BF16)
 
         each_rows(j, what)
         out_store(j, out_h).start()
@@ -943,11 +947,12 @@
     def rows_front(j):
         at, slot = lax.rem(j, 2), ring.at(j)
 
-        def what(here, there):
-            down = chain.inner_in[slot, here, :].astype(F32)
-            normal, back = norm_back(src[at, here, :].astype(F32), down, vec[4:5, :])
-            out[at, here, :] = (back + resid[there, :].astype(F32)).astype(BF16)
-            gather(3, down * normal, down)
+        def what(heres, theres):
+            downs = [chain.inner_in[slot, here, :].astype(F32) for here in heres]
+            normals, backs = norm_back([src[at, here, :].astype(F32) for here in heres], downs, vec[4:5, :])
+            for here, there, down, normal, back in zip(heres, theres, downs, normals, backs):
+                out[at, here, :] = (back + resid[there, :].astype(F32)).astype(BF16)
+                gather(3, down * normal, down)
 
         each_rows(j, what)
         out_store(j, input_h).start()
@@ -958,7 +963,7 @@
 
     def small_step(j):
         if j == 0:
-            for row, item in ((0, cols[3]), (1, cols[4]), (2, cols[0]), (3, cols[1]), (4, cols[2]), (5, eb[...]), (6, cols[5])):
+            for row, item in ((2, cols[0]), (3, cols[1]), (4, cols[2]), (5, eb[...]), (6, cols[5])):
                 buf[0, row : row + 1, :] = jnp.sum(item, axis=0, keepdims=True)
         else:
             swap(j - 1).wait()
@@ -966,6 +971,21 @@
         if j < 3:
             swap(j).start()
 
+    def last_copy(m):
+        return remote(last.at[0], last.at[m], ls.at[m], lq.at[m], "dp", cube.peer(m))
+
+    def last_start():
+        for row in range(2):
+            last[0, row : row + 1, :] = jnp.sum(cols[3 + row], axis=0, keepdims=True)
+        for m in range(1, 8):
+            last_copy(m).start()
+
+    def last_end():
+        for m in range(1, 8):
+            last_copy(m).wait()
+        two = [last[m] + last[m + 1] for m in range(0, 8, 2)]
+        buf[3, 0:2, :] = (two[0] + two[1]) + (two[2] + two[3])
+
     late = chain.most_lag + 1
     heads_at = late + per_sum
 
@@ -1060,14 +1080,20 @@
 
         for j in range(4):
 
-            @pl.when(t == late + total_z + j)
+            @pl.when(t == loaded_z + 2 + 2 * j)
             def _(j=j):
                 small_step(j)
 
+        for j, step in enumerate((last_start, last_end)):
+
+            @pl.when(t == late + total_z + j)
+            def _(step=step):
+                step()
+
         return carry
 
     assert heads_at + heads <= loaded_z and heads_at + 1 < to_output
-    lax.fori_loop(0, max(total_z + late + 4, total_p + cube.gone), tick, 0)
+    lax.fori_loop(0, max(total_z + late + 2, total_p + cube.gone), tick, 0)
     small_store = pltpu.make_async_copy(buf.at[3], small_out, load.at[0])
     small_store.start()
     small_store.wait()
@@ -1109,6 +1135,7 @@
         pltpu.VMEM((6, 8, width), F32),
         pltpu.VMEM((4, 8, width), F32),
         pltpu.VMEM((3, 8, width), F32),
+        pltpu.VMEM((8, 2, width), F32),
         dma((14,)),
         dma((2,)),
         dma((slots,)),
@@ -1116,6 +1143,8 @@
         dma((2,)),
         dma((3,)),
         dma((3,)),
+        dma((8,)),
+        dma((8,)),
         *Chain.scratch(slots, (ROWS_BACK, width)),
         *Cube.scratch((PIECE // 8, BACK_COLUMNS), BACK_APART),
     ]

time: 402 us -> 398 us (0.990)
  no operation moved by 1% of the time
where the time goes in v6:
time: 398 us
  Pallas kernels  358 us (90%)
  other arithmetic  30.2 us (8%)
  local copies, waits for them, and re-layouts  9.15 us (2%)
    pallas_call x1, Pallas kernels, back_call(): pl.pallas_call(functools.partial(back_kernel, n, local // HD), out_shape=...  233 us
    pallas_call x1, Pallas kernels, mlp_call(): pl.pallas_call(functools.partial(mlp_kernel, n, length), out_shape=out_sh...  101 us
    pallas_call x1, Pallas kernels, head_call(): pl.pallas_call(functools.partial(head_kernel, heads), out_shape=[jax.Shap...  23.7 us
    reshape x1, other arithmetic, on_device(): shrink_weight_grad = shrink_sum.astype(F32).reshape(units, width)  18.5 us

profile of v6, /device:TPU:0, one launch (start us, length us, event | category | flops | bytes accessed | tf_op | source)
XLA Modules:
  0.0 397.9 jit_solution(11488210699453183627)
XLA Ops:
  0.6 0.8 fusion.1
  1.4 0.1 pad.1.clone
  1.5 0.7 pad_maximum_fusion.1.refs_3_
  2.2 1.3 pad_maximum_fusion.refs_2_
  3.5 0.7 broadcast_in_dim.2.refs_4_.refs_18_
  4.2 0.0 copy-start.3
  4.2 0.0 copy-start.4
  4.2 0.0 copy-start.5
  4.2 0.0 copy-start.6
  4.2 0.0 copy-start.7
  4.2 0.0 copy-start.8
  4.2 23.7 %shard_map.254 = (bf16[768,2048]{1,0:T(8,128)(2,1)}, bf16[768,512]{1,0:T(8,128)(2,1)}, bf16[768,512]{1,0:T(8,128)(2,1)}, bf16[768,512]{1,0:T(8,128)(2,1)}, bf16[...) custom-call(bf16[768,2048]{1,0:T(8,128)(2,1)} %refs_2_.1, bf16[3,2048,512]{2,1,0:T(8,128)(2,1)} %bitcast.37, ...), custom_call_target="tpu_custom_call" | custom-call | tf_op jit(solution)/shard_map/pallas_call | solution.py:276
  27.9 0.0 copy-done.3
  27.9 0.0 copy-done.4
  27.9 0.0 copy-done.5
  27.9 0.0 copy-done.6
  27.9 0.0 copy-done.7
  28.0 0.0 copy-done.8
  28.0 0.7 stack.40.refs_6_.refs_12_
  28.7 100.8 %shard_map.255 = (bf16[24,32,2048]{2,1,0:T(8,128)(2,1)}, bf16[768,2048]{1,0:T(8,128)(2,1)}, bf16[768,2048]{1,0:T(8,128)(2,1)}, bf16[768,2048]{1,0:T(8,128)(2,1)}...) custom-call(bf16[768,512]{1,0:T(8,128)(2,1)} %get-tuple-element.35.refs_0_.refs_10_, ...), custom_call_target="tpu_custom_call" | custom-call | tf_op jit(solution)/shard_map/pallas_call | solution.py:473
  129.5 233.3 %shard_map.256 = (bf16[16,48,2048]{2,1,0:T(8,128)(2,1)}, bf16[8,2,2,2,32,2048]{5,4,3,2,1,0:T(8,128)(2,1)}, bf16[8,2,2,2,32,2048]{5,4,3,2,1,0:T(8,128)(2,1)}, bf1...) custom-call(bf16[16,48,2048]{2,1,0:T(8,128)(2,1)} %bitcast.43, ...), custom_call_target="tpu_custom_call" | custom-call | tf_op jit(solution)/shard_map/pallas_call | solution.py:1151
  362.8 0.0 slice-start
  362.8 0.0 slice-start.1
  362.8 18.5 %bitcast_convert_fusion = (f32[2048,2048]{1,0:T(8,128)}, f32[2048,2048]{1,0:T(8,128)}) fusion(bf16[8,2,2,2,32,2048]{5,4,3,2,1,0:T(8,128)(2,1)} %get-tuple-element.55, bf16[8,2,2,2,32,2048]{5,4,3,2,1,0:T(8,128)(2,1)} %get-tuple-element.54), kind=kLoop, calls=%fused_computation.1 | loop fusion | flops 8388608 | bytes 50331648 | tf_op jit(solution)/shard_map/reshape | solution.py:1247
  381.3 0.0 slice-done
  381.3 0.0 slice-done.1
  381.3 0.0 copy-start.1
  381.3 7.0 %convert_bitcast_fusion = f32[2048,3,512]{2,0,1:T(8,128)} fusion(bf16[3,8,2,2,2,32,512]{6,5,4,3,2,1,0:T(8,128)(2,1)S(1)} %bitcast.40), kind=kLoop, calls=%fused_computation | loop fusion | flops 3145728 | bytes 18874368 | tf_op jit(solution)/shard_map/transpose | solution.py:1249
  388.3 0.0 copy-start.2
  388.3 0.0 copy-done.1
  388.3 2.7 bitcast_convert_fusion.2
  391.0 0.0 copy-start
  391.0 0.0 copy-done.2
  391.0 0.6 fusion
  391.6 0.6 reshape_squeeze.3
  392.2 4.0 copy.31
  396.2 0.0 copy-done
  396.2 1.7 copy.32
  (3 shorter events, 0.0 us)
Async XLA Ops:
  4.2 23.7 %copy-start.3 = (f32[2048]{0:T(1024)S(1)}, f32[2048]{0:T(1024)}, u32[]{:S(2)}) copy-start(f32[2048]{0:T(1024)} %param.17) | copy-start | bytes 24580
  4.2 23.8 %copy-start.4 = (f32[2048]{0:T(1024)S(1)}, f32[2048]{0:T(1024)}, u32[]{:S(2)}) copy-start(f32[2048]{0:T(1024)} %param.22) | copy-start | bytes 24580
  4.2 23.8 %copy-start.5 = (f32[2048]{0:T(1024)S(1)}, f32[2048]{0:T(1024)}, u32[]{:S(2)}) copy-start(f32[2048]{0:T(1024)} %param.23) | copy-start | bytes 24580
  4.2 23.8 %copy-start.6 = (f32[2048]{0:T(1024)S(1)}, f32[2048]{0:T(1024)}, u32[]{:S(2)}) copy-start(f32[2048]{0:T(1024)} %param.24) | copy-start | bytes 24580
  4.2 23.8 %copy-start.7 = (f32[2048]{0:T(1024)S(1)}, f32[2048]{0:T(1024)}, u32[]{:S(2)}) copy-start(f32[2048]{0:T(1024)} %param.26) | copy-start | bytes 24580
  4.2 23.8 %copy-start.8 = (f32[2048]{0:T(1024)S(1)}, f32[2048]{0:T(1024)}, u32[]{:S(2)}) copy-start(f32[2048]{0:T(1024)} %param.28) | copy-start | bytes 24580
  362.8 18.5 %slice-start = ((s8[6291456]{0:T(1024)(128)(4,1)}), s8[4194304]{0:T(1024)(128)(4,1)S(1)}, s32[]{:S(2)}) async-start(s8[6291456]{0:T(1024)(128)(4,1)} %bitcast.39), calls=%async_computation | async-start | bytes 8388608
  362.8 18.5 %slice-start.1 = ((s8[6291456]{0:T(1024)(128)(4,1)}), s8[2097152]{0:T(1024)(128)(4,1)S(1)}, s32[]{:S(2)}) async-start(s8[6291456]{0:T(1024)(128)(4,1)} %bitcast.39), calls=%async_computation.1 | async-start | bytes 4194304
  381.3 7.0 %copy-start.1 = (bf16[2,2,2,2,32,2048]{5,4,3,2,1,0:T(8,128)(2,1)S(1)}, bf16[2,2,2,2,32,2048]{5,4,3,2,1,0:T(8,128)(2,1)}, u32[]{:S(2)}) copy-start(bf16[2,2,2,2,32,2048]{5,4,3,2,1,0:T(8,128)(2,1)} %get-tuple-element.53) | copy-start | bytes 6291460
  388.3 2.7 copy-start.2
  391.0 5.2 %copy-start = (bf16[16,48,2048]{2,1,0:T(8,128)(2,1)S(1)}, bf16[16,48,2048]{2,1,0:T(8,128)(2,1)}, u32[]{:S(2)}) copy-start(bf16[16,48,2048]{2,1,0:T(8,128)(2,1)} %get-tuple-element.50) | copy-start | bytes 9437188

commit v7 on v6

--- a/solution.py
+++ b/solution.py
@@ -292,7 +292,7 @@
 ROWS = 32
 SLACK = 2
 BLOCK_ROWS = 256
-TILE = 512
+TILE = 1024
 
 
 def mlp_kernel(n, length, *refs):

time: 398 us -> 397 us (level)
  no operation moved by 1% of the time
where the time goes in v7:
time: 397 us; the launch traced here: 396 us
  Pallas kernels  356 us (90%)
  other arithmetic  30.2 us (8%)
  local copies, waits for them, and re-layouts  9.15 us (2%)
    pallas_call x1, Pallas kernels, back_call(): pl.pallas_call(functools.partial(back_kernel, n, local // HD), out_shape=...  232 us
    pallas_call x1, Pallas kernels, mlp_call(): pl.pallas_call(functools.partial(mlp_kernel, n, length), out_shape=out_sh...  100 us
    pallas_call x1, Pallas kernels, head_call(): pl.pallas_call(functools.partial(head_kernel, heads), out_shape=[jax.Shap...  23.7 us
    reshape x1, other arithmetic, on_device(): shrink_weight_grad = shrink_sum.astype(F32).reshape(units, width)  18.5 us

profile of v7, /device:TPU:0, one launch (start us, length us, event | category | flops | bytes accessed | tf_op | source)
XLA Modules:
  0.0 396.5 jit_solution(9690608521182324638)
XLA Ops:
  0.6 0.8 fusion.1
  1.4 0.1 pad.1.clone
  1.5 0.7 pad_maximum_fusion.1.refs_3_
  2.2 1.3 pad_maximum_fusion.refs_2_
  3.5 0.7 broadcast_in_dim.2.refs_4_.refs_18_
  4.2 0.0 copy-start.3
  4.2 0.0 copy-start.4
  4.2 0.0 copy-start.5
  4.2 0.0 copy-start.6
  4.2 0.0 copy-start.7
  4.2 0.0 copy-start.8
  4.2 23.7 %shard_map.254 = (bf16[768,2048]{1,0:T(8,128)(2,1)}, bf16[768,512]{1,0:T(8,128)(2,1)}, bf16[768,512]{1,0:T(8,128)(2,1)}, bf16[768,512]{1,0:T(8,128)(2,1)}, bf16[...) custom-call(bf16[768,2048]{1,0:T(8,128)(2,1)} %refs_2_.1, bf16[3,2048,512]{2,1,0:T(8,128)(2,1)} %bitcast.37, ...), custom_call_target="tpu_custom_call" | custom-call | tf_op jit(solution)/shard_map/pallas_call | solution.py:276
  27.9 0.0 copy-done.3
  27.9 0.0 copy-done.4
  27.9 0.0 copy-done.5
  27.9 0.0 copy-done.6
  27.9 0.0 copy-done.7
  28.0 0.0 copy-done.8
  28.0 0.7 stack.40.refs_6_.refs_12_
  28.7 100.4 %shard_map.255 = (bf16[24,32,2048]{2,1,0:T(8,128)(2,1)}, bf16[768,2048]{1,0:T(8,128)(2,1)}, bf16[768,2048]{1,0:T(8,128)(2,1)}, bf16[768,2048]{1,0:T(8,128)(2,1)}...) custom-call(bf16[768,512]{1,0:T(8,128)(2,1)} %get-tuple-element.35.refs_0_.refs_10_, ...), custom_call_target="tpu_custom_call" | custom-call | tf_op jit(solution)/shard_map/pallas_call | solution.py:473
  129.0 232.3 %shard_map.256 = (bf16[16,48,2048]{2,1,0:T(8,128)(2,1)}, bf16[8,2,2,2,32,2048]{5,4,3,2,1,0:T(8,128)(2,1)}, bf16[8,2,2,2,32,2048]{5,4,3,2,1,0:T(8,128)(2,1)}, bf1...) custom-call(bf16[16,48,2048]{2,1,0:T(8,128)(2,1)} %bitcast.43, ...), custom_call_target="tpu_custom_call" | custom-call | tf_op jit(solution)/shard_map/pallas_call | solution.py:1151
  361.4 0.0 slice-start
  361.4 0.0 slice-start.1
  361.4 18.5 %bitcast_convert_fusion = (f32[2048,2048]{1,0:T(8,128)}, f32[2048,2048]{1,0:T(8,128)}) fusion(bf16[8,2,2,2,32,2048]{5,4,3,2,1,0:T(8,128)(2,1)} %get-tuple-element.55, bf16[8,2,2,2,32,2048]{5,4,3,2,1,0:T(8,128)(2,1)} %get-tuple-element.54), kind=kLoop, calls=%fused_computation.1 | loop fusion | flops 8388608 | bytes 50331648 | tf_op jit(solution)/shard_map/reshape | solution.py:1247
  379.9 0.0 slice-done
  379.9 0.0 slice-done.1
  379.9 0.0 copy-start.1
  379.9 7.0 %convert_bitcast_fusion = f32[2048,3,512]{2,0,1:T(8,128)} fusion(bf16[3,8,2,2,2,32,512]{6,5,4,3,2,1,0:T(8,128)(2,1)S(1)} %bitcast.40), kind=kLoop, calls=%fused_computation | loop fusion | flops 3145728 | bytes 18874368 | tf_op jit(solution)/shard_map/transpose | solution.py:1249
  386.9 0.0 copy-start.2
  386.9 0.0 copy-done.1
  386.9 2.7 bitcast_convert_fusion.2
  389.6 0.0 copy-start
  389.6 0.0 copy-done.2
  389.6 0.6 fusion
  390.3 0.6 reshape_squeeze.3
  390.9 4.0 %copy.31 = bf16[768,2048]{1,0:T(8,128)(2,1)} copy(bf16[768,2048]{1,0:T(8,128)(2,1)} %bitcast.45) | data formatting | bytes 6291456
  394.8 0.0 copy-done
  394.8 1.7 copy.32
  (3 shorter events, 0.0 us)
Async XLA Ops:
  4.2 23.7 %copy-start.3 = (f32[2048]{0:T(1024)S(1)}, f32[2048]{0:T(1024)}, u32[]{:S(2)}) copy-start(f32[2048]{0:T(1024)} %param.17) | copy-start | bytes 24580
  4.2 23.8 %copy-start.4 = (f32[2048]{0:T(1024)S(1)}, f32[2048]{0:T(1024)}, u32[]{:S(2)}) copy-start(f32[2048]{0:T(1024)} %param.22) | copy-start | bytes 24580
  4.2 23.8 %copy-start.5 = (f32[2048]{0:T(1024)S(1)}, f32[2048]{0:T(1024)}, u32[]{:S(2)}) copy-start(f32[2048]{0:T(1024)} %param.23) | copy-start | bytes 24580
  4.2 23.8 %copy-start.6 = (f32[2048]{0:T(1024)S(1)}, f32[2048]{0:T(1024)}, u32[]{:S(2)}) copy-start(f32[2048]{0:T(1024)} %param.24) | copy-start | bytes 24580
  4.2 23.8 %copy-start.7 = (f32[2048]{0:T(1024)S(1)}, f32[2048]{0:T(1024)}, u32[]{:S(2)}) copy-start(f32[2048]{0:T(1024)} %param.26) | copy-start | bytes 24580
  4.2 23.8 %copy-start.8 = (f32[2048]{0:T(1024)S(1)}, f32[2048]{0:T(1024)}, u32[]{:S(2)}) copy-start(f32[2048]{0:T(1024)} %param.28) | copy-start | bytes 24580
  361.4 18.5 %slice-start = ((s8[6291456]{0:T(1024)(128)(4,1)}), s8[4194304]{0:T(1024)(128)(4,1)S(1)}, s32[]{:S(2)}) async-start(s8[6291456]{0:T(1024)(128)(4,1)} %bitcast.39), calls=%async_computation | async-start | bytes 8388608
  361.4 18.5 %slice-start.1 = ((s8[6291456]{0:T(1024)(128)(4,1)}), s8[2097152]{0:T(1024)(128)(4,1)S(1)}, s32[]{:S(2)}) async-start(s8[6291456]{0:T(1024)(128)(4,1)} %bitcast.39), calls=%async_computation.1 | async-start | bytes 4194304
  379.9 7.0 %copy-start.1 = (bf16[2,2,2,2,32,2048]{5,4,3,2,1,0:T(8,128)(2,1)S(1)}, bf16[2,2,2,2,32,2048]{5,4,3,2,1,0:T(8,128)(2,1)}, u32[]{:S(2)}) copy-start(bf16[2,2,2,2,32,2048]{5,4,3,2,1,0:T(8,128)(2,1)} %get-tuple-element.53) | copy-start | bytes 6291460
  386.9 2.7 copy-start.2
  389.6 5.2 %copy-start = (bf16[16,48,2048]{2,1,0:T(8,128)(2,1)S(1)}, bf16[16,48,2048]{2,1,0:T(8,128)(2,1)}, u32[]{:S(2)}) copy-start(bf16[16,48,2048]{2,1,0:T(8,128)(2,1)} %get-tuple-element.50) | copy-start | bytes 9437188

commit v8 on v7

--- a/solution.py
+++ b/solution.py
@@ -232,14 +232,9 @@
     for m, to in enumerate((q, k, v)):
         w_loads[m].wait()
 
-        def project(i, carry, m=m, to=to):
-            at = pl.ds(pl.multiple_of(i * 256, 256), 256)
-            to[at, :] = (
-                jnp.dot(normed[at, :], w[m], preferred_element_type=F32) + bias[m : m + 1, :]
-            ).astype(BF16)
-            return carry
-
-        lax.fori_loop(0, length // 256, project, 0)
+        to[...] = (
+            jnp.dot(normed[...], w[m], preferred_element_type=F32) + bias[m : m + 1, :]
+        ).astype(BF16)
 
     stores = [
         pltpu.make_async_copy(a, b, store.at[j])

time: 397 us -> 396 us (level)
  no operation moved by 1% of the time
where the time goes in v8:
time: 396 us; the launch traced here: 395 us
  Pallas kernels  355 us (90%)
  other arithmetic  30.2 us (8%)
  local copies, waits for them, and re-layouts  9.15 us (2%)
    pallas_call x1, Pallas kernels, back_call(): pl.pallas_call(functools.partial(back_kernel, n, local // HD), out_shape=...  232 us
    pallas_call x1, Pallas kernels, mlp_call(): pl.pallas_call(functools.partial(mlp_kernel, n, length), out_shape=out_sh...  100 us
    pallas_call x1, Pallas kernels, head_call(): pl.pallas_call(functools.partial(head_kernel, heads), out_shape=[jax.Shap...  22.6 us
    reshape x1, other arithmetic, on_device(): shrink_weight_grad = shrink_sum.astype(F32).reshape(units, width)  18.5 us

profile of v8, /device:TPU:0, one launch (start us, length us, event | category | flops | bytes accessed | tf_op | source)
XLA Modules:
  0.0 395.5 jit_solution(1316939324032184480)
XLA Ops:
  0.6 0.8 fusion.1
  1.4 0.1 pad.1.clone
  1.5 0.7 pad_maximum_fusion.1.refs_3_
  2.2 1.3 pad_maximum_fusion.refs_2_
  3.5 0.7 broadcast_in_dim.2.refs_4_.refs_18_
  4.2 0.0 copy-start.3
  4.2 0.0 copy-start.4
  4.2 0.0 copy-start.5
  4.2 0.0 copy-start.6
  4.2 0.0 copy-start.7
  4.2 0.0 copy-start.8
  4.2 22.6 %shard_map.254 = (bf16[768,2048]{1,0:T(8,128)(2,1)}, bf16[768,512]{1,0:T(8,128)(2,1)}, bf16[768,512]{1,0:T(8,128)(2,1)}, bf16[768,512]{1,0:T(8,128)(2,1)}, bf16[...) custom-call(bf16[768,2048]{1,0:T(8,128)(2,1)} %refs_2_.1, bf16[3,2048,512]{2,1,0:T(8,128)(2,1)} %bitcast.37, ...), custom_call_target="tpu_custom_call" | custom-call | tf_op jit(solution)/shard_map/pallas_call | solution.py:271
  26.8 0.0 copy-done.3
  26.8 0.0 copy-done.4
  26.8 0.0 copy-done.5
  26.9 0.0 copy-done.6
  26.9 0.0 copy-done.7
  26.9 0.0 copy-done.8
  26.9 0.7 stack.40.refs_6_.refs_12_
  27.6 100.4 %shard_map.255 = (bf16[24,32,2048]{2,1,0:T(8,128)(2,1)}, bf16[768,2048]{1,0:T(8,128)(2,1)}, bf16[768,2048]{1,0:T(8,128)(2,1)}, bf16[768,2048]{1,0:T(8,128)(2,1)}...) custom-call(bf16[768,512]{1,0:T(8,128)(2,1)} %get-tuple-element.35.refs_0_.refs_10_, ...), custom_call_target="tpu_custom_call" | custom-call | tf_op jit(solution)/shard_map/pallas_call | solution.py:468
  128.0 232.4 %shard_map.256 = (bf16[16,48,2048]{2,1,0:T(8,128)(2,1)}, bf16[8,2,2,2,32,2048]{5,4,3,2,1,0:T(8,128)(2,1)}, bf16[8,2,2,2,32,2048]{5,4,3,2,1,0:T(8,128)(2,1)}, bf1...) custom-call(bf16[16,48,2048]{2,1,0:T(8,128)(2,1)} %bitcast.43, ...), custom_call_target="tpu_custom_call" | custom-call | tf_op jit(solution)/shard_map/pallas_call | solution.py:1146
  360.3 0.0 slice-start
  360.4 0.0 slice-start.1
  360.4 18.5 %bitcast_convert_fusion = (f32[2048,2048]{1,0:T(8,128)}, f32[2048,2048]{1,0:T(8,128)}) fusion(bf16[8,2,2,2,32,2048]{5,4,3,2,1,0:T(8,128)(2,1)} %get-tuple-element.55, bf16[8,2,2,2,32,2048]{5,4,3,2,1,0:T(8,128)(2,1)} %get-tuple-element.54), kind=kLoop, calls=%fused_computation.1 | loop fusion | flops 8388608 | bytes 50331648 | tf_op jit(solution)/shard_map/reshape | solution.py:1242
  378.8 0.0 slice-done
  378.8 0.0 slice-done.1
  378.9 0.0 copy-start.1
  378.9 7.0 %convert_bitcast_fusion = f32[2048,3,512]{2,0,1:T(8,128)} fusion(bf16[3,8,2,2,2,32,512]{6,5,4,3,2,1,0:T(8,128)(2,1)S(1)} %bitcast.40), kind=kLoop, calls=%fused_computation | loop fusion | flops 3145728 | bytes 18874368 | tf_op jit(solution)/shard_map/transpose | solution.py:1244
  385.9 0.0 copy-start.2
  385.9 0.0 copy-done.1
  385.9 2.7 bitcast_convert_fusion.2
  388.5 0.0 copy-start
  388.5 0.0 copy-done.2
  388.6 0.6 fusion
  389.2 0.6 reshape_squeeze.3
  389.8 4.0 %copy.31 = bf16[768,2048]{1,0:T(8,128)(2,1)} copy(bf16[768,2048]{1,0:T(8,128)(2,1)} %bitcast.45) | data formatting | bytes 6291456
  393.8 0.0 copy-done
  393.8 1.7 copy.32
  (3 shorter events, 0.0 us)
Async XLA Ops:
  4.2 22.7 %copy-start.3 = (f32[2048]{0:T(1024)S(1)}, f32[2048]{0:T(1024)}, u32[]{:S(2)}) copy-start(f32[2048]{0:T(1024)} %param.17) | copy-start | bytes 24580
  4.2 22.7 %copy-start.4 = (f32[2048]{0:T(1024)S(1)}, f32[2048]{0:T(1024)}, u32[]{:S(2)}) copy-start(f32[2048]{0:T(1024)} %param.22) | copy-start | bytes 24580
  4.2 22.7 %copy-start.5 = (f32[2048]{0:T(1024)S(1)}, f32[2048]{0:T(1024)}, u32[]{:S(2)}) copy-start(f32[2048]{0:T(1024)} %param.23) | copy-start | bytes 24580
  4.2 22.7 %copy-start.6 = (f32[2048]{0:T(1024)S(1)}, f32[2048]{0:T(1024)}, u32[]{:S(2)}) copy-start(f32[2048]{0:T(1024)} %param.24) | copy-start | bytes 24580
  4.2 22.7 %copy-start.7 = (f32[2048]{0:T(1024)S(1)}, f32[2048]{0:T(1024)}, u32[]{:S(2)}) copy-start(f32[2048]{0:T(1024)} %param.26) | copy-start | bytes 24580
  4.2 22.7 %copy-start.8 = (f32[2048]{0:T(1024)S(1)}, f32[2048]{0:T(1024)}, u32[]{:S(2)}) copy-start(f32[2048]{0:T(1024)} %param.28) | copy-start | bytes 24580
  360.3 18.5 %slice-start = ((s8[6291456]{0:T(1024)(128)(4,1)}), s8[4194304]{0:T(1024)(128)(4,1)S(1)}, s32[]{:S(2)}) async-start(s8[6291456]{0:T(1024)(128)(4,1)} %bitcast.39), calls=%async_computation | async-start | bytes 8388608
  360.4 18.5 %slice-start.1 = ((s8[6291456]{0:T(1024)(128)(4,1)}), s8[2097152]{0:T(1024)(128)(4,1)S(1)}, s32[]{:S(2)}) async-start(s8[6291456]{0:T(1024)(128)(4,1)} %bitcast.39), calls=%async_computation.1 | async-start | bytes 4194304
  378.9 7.0 %copy-start.1 = (bf16[2,2,2,2,32,2048]{5,4,3,2,1,0:T(8,128)(2,1)S(1)}, bf16[2,2,2,2,32,2048]{5,4,3,2,1,0:T(8,128)(2,1)}, u32[]{:S(2)}) copy-start(bf16[2,2,2,2,32,2048]{5,4,3,2,1,0:T(8,128)(2,1)} %get-tuple-element.53) | copy-start | bytes 6291460
  385.9 2.7 copy-start.2
  388.5 5.2 %copy-start = (bf16[16,48,2048]{2,1,0:T(8,128)(2,1)S(1)}, bf16[16,48,2048]{2,1,0:T(8,128)(2,1)}, u32[]{:S(2)}) copy-start(bf16[16,48,2048]{2,1,0:T(8,128)(2,1)} %get-tuple-element.50) | copy-start | bytes 9437188
